TPU v7x, 32 devices: a whole 2x2x4 slice. The times are simulated.
32 devices in a mesh: tm: 8 (over y, x, core), group: 4 (over z).
Axes of the slice: x: 2, y: 2, z: 4, core: 2. Of those that a mesh axis runs over, the one named last changes fastest.
Arguments:
- tokens: bfloat16 [8, 1024, 1024], P('tm', 'group'), may hold values from -6 to 6
- conv_weight: float32 [3, 1024], replicated, may hold values from -3 to 3
- qkv_weight: bfloat16 [1024, 3072], replicated, may hold values from -0.1875 to 0.1875
- attn_out_weight: bfloat16 [1024, 1024], replicated, may hold values from -0.1875 to 0.1875
- router_weight: bfloat16 [1024, 16], replicated, may hold values from -0.375 to 0.375
- expert_ids: int32 [8, 1024, 2], P('tm', 'group'), may hold values from 0 to 15, as said below
- expert_in: bfloat16 [32, 1024, 2048], P(('tm', 'group')), may hold values from -0.1875 to 0.1875
- expert_out: bfloat16 [32, 2048, 1024], P(('tm', 'group')), may hold values from -0.09375 to 0.09375
Outputs:
- layer_out: bfloat16 [8, 1024, 1024], P('tm', 'group')
Inputs may be any that keep to these rules, and one draw needn't show every extreme that they name: `expert_ids`: each row names two different experts. In the rows of one device (one frame, 256 consecutive spatial positions) * 4 experts are named exactly 64 times each and the others share the remaining routes as evenly as possible; one expert is among the fully named ones on every device.
All inputs are finite; a program needn't handle non-finite values.
Results may differ from a plain program's by a relative error of at most 0.0095.
Values may be sent and summed in bfloat16 or wider, within the bound.
No kernel may reach another device: no remote copies, remote signals or barrier semaphores. Data moves between devices by JAX's collectives and lax.ppermute only.
A program may use at most 128 MiB of HBM per device.

v0:
```python
import math

import jax
import jax.numpy as jnp
from jax import lax
from jax.sharding import PartitionSpec as P

D = 1024
HEADS = 16
HD = 64


def with_halo(cells, sides, width):
    for axis, dim in sides:
        count = lax.axis_size(axis)
        ends = count - 1
        head = lax.slice_in_dim(cells, 0, width, axis=dim)
        tail = lax.slice_in_dim(cells, cells.shape[dim] - width, cells.shape[dim], axis=dim)
        cells = jnp.concatenate(
            [
                lax.ppermute(tail, axis, [(i, (i + 1) % count) for i in range(ends)]),
                cells,
                lax.ppermute(head, axis, [((i + 1) % count, i) for i in range(ends)]),
            ],
            axis=dim,
        )
    return cells


def layer_normed(values):
    values = values.astype(jnp.float32)
    centre = jnp.mean(values, -1, keepdims=True)
    spread = jnp.mean((values - centre) ** 2, -1, keepdims=True)
    return ((values - centre) / jnp.sqrt(spread + 1e-05)).astype(jnp.bfloat16)


def unit_scaled(values):
    return (values / jnp.sqrt(jnp.mean(values * values, -1, keepdims=True) + 1e-06)).astype(
        jnp.bfloat16
    )


def convolved(padded, current, conv_weight):
    summed = (
        conv_weight[0] * padded[:-2].astype(jnp.float32)
        + conv_weight[1] * padded[1:-1].astype(jnp.float32)
        + conv_weight[2] * padded[2:].astype(jnp.float32)
    )
    return (current.astype(jnp.float32) + summed).astype(jnp.bfloat16)


def time_mixing(normed, qkv_weight, attn_out_weight):
    frames, across, channels = normed.shape
    projected = jnp.dot(
        normed.reshape(frames * across, channels), qkv_weight, preferred_element_type=jnp.float32
    )
    projected = projected.reshape(frames, across, 3, HEADS, HD)
    queries = unit_scaled(projected[:, :, 0])
    keys_all = unit_scaled(projected[:, :, 1])
    values_all = projected[:, :, 2].astype(jnp.bfloat16)
    scores = jnp.einsum(
        "fshd,gshd->shfg", queries, keys_all, preferred_element_type=jnp.float32
    ) / math.sqrt(HD)
    weights = jnp.exp(scores)
    weights = (weights / jnp.sum(weights, -1, keepdims=True)).astype(jnp.bfloat16)
    context = jnp.einsum(
        "shfg,gshd->fshd", weights, values_all, preferred_element_type=jnp.float32
    ).astype(jnp.bfloat16)
    mixed_out = jnp.dot(
        context.reshape(frames * across, channels),
        attn_out_weight,
        preferred_element_type=jnp.float32,
    )
    return mixed_out.astype(jnp.bfloat16).reshape(frames, across, channels)


def half_partial(slot_rows, inner_weight, outer_weight):
    flat_rows = slot_rows.reshape(-1, slot_rows.shape[-1])
    hidden = jax.nn.gelu(
        jnp.dot(flat_rows, inner_weight, preferred_element_type=jnp.float32)
    ).astype(jnp.bfloat16)
    return jnp.dot(hidden, outer_weight, preferred_element_type=jnp.float32).reshape(
        slot_rows.shape
    )


def body(
    tokens,
    conv_weight,
    qkv_weight,
    attn_out_weight,
    router_weight,
    expert_ids,
    expert_in,
    expert_out,
):
    shards = lax.axis_size("tm")
    spatial = tokens.shape[1]
    across = spatial // shards
    extended = with_halo(tokens, (("tm", 0),), 1)
    stream_one = convolved(extended, tokens, conv_weight)
    normed = layer_normed(stream_one).reshape(1, shards, across, D)
    received = lax.all_to_all(normed, "tm", split_axis=1, concat_axis=0, tiled=True)
    number = received.shape[2]
    mixed_out = time_mixing(received.reshape(shards, number, D), qkv_weight, attn_out_weight)
    attended = lax.all_to_all(
        mixed_out.reshape(shards, 1, number, D), "tm", split_axis=0, concat_axis=1, tiled=True
    )
    stream_two = (
        stream_one.astype(jnp.float32) + attended.reshape(1, spatial, D).astype(jnp.float32)
    ).astype(jnp.bfloat16)
    moe_rows = layer_normed(stream_two).reshape(spatial, D)
    experts = router_weight.shape[1]
    capacity = 4 * spatial // experts
    logits = jnp.dot(moe_rows, router_weight, preferred_element_type=jnp.float32)
    routed = expert_ids.reshape(spatial, 2)
    matches = routed[:, :, None] == jnp.arange(experts, dtype=jnp.int32)[None, None, :]
    chosen = jnp.sum(jnp.where(matches, logits[:, None, :], 0.0), -1)
    gate_values = jax.nn.sigmoid(chosen)
    shares = gate_values / jnp.sum(gate_values, -1, keepdims=True)
    flat_match = matches.reshape(spatial * 2, experts).astype(jnp.int32)
    slot_index = jnp.sum((jnp.cumsum(flat_match, 0) - flat_match) * flat_match, -1)
    flat_ids = routed.reshape(spatial * 2)
    outbox = (
        jnp.zeros((experts, capacity, D), jnp.bfloat16)
        .at[flat_ids, slot_index]
        .set(jnp.repeat(moe_rows, 2, axis=0))
    )
    inner_weight = expert_in[0]
    outer_weight = expert_out[0]
    doubled = jnp.broadcast_to(outbox[:, None], (experts, 2, capacity, D)).reshape(
        2 * experts, capacity, D
    )
    partial_sum = half_partial(
        lax.all_to_all(doubled, ("tm", "group"), split_axis=0, concat_axis=0, tiled=True),
        inner_weight,
        outer_weight,
    )
    returned = lax.all_to_all(partial_sum, ("tm", "group"), split_axis=0, concat_axis=0, tiled=True)
    results = jnp.sum(returned.reshape(experts, 2, capacity, D), 1).astype(jnp.bfloat16)
    picked = results[flat_ids, slot_index].reshape(spatial, 2, D).astype(jnp.float32)
    moe_out = jnp.sum(shares[:, :, None] * picked, 1)
    layer_out = stream_two.reshape(spatial, D).astype(jnp.float32) + moe_out
    return layer_out.astype(jnp.bfloat16).reshape(1, spatial, D)


def solution(mesh):
    placed = (
        P("tm", "group", None),
        P(),
        P(),
        P(),
        P(),
        P("tm", "group", None),
        P(("tm", "group"), None, None),
        P(("tm", "group"), None, None),
    )
    return jax.shard_map(
        body, mesh=mesh, in_specs=placed, out_specs=P("tm", "group", None), check_vma=False
    )
```

profile of v0, /device:TPU:9, one launch (start us, length us, event | category | flops | bytes accessed | tf_op | source)
XLA Modules:
  0.0 453.5 jit_solution(820518736820092722)
XLA Ops:
  0.0 2.7 collective-permute-start.1
  2.7 3.0 collective-permute-start
  5.7 0.8 fusion.44
  6.6 6.2 %collective-permute-done.1 = bf16[1,256,1024]{2,1,0:T(8,128)(2,1)S(1)} collective-permute-done((bf16[1,256,1024]{2,1,0:T(8,128)(2,1)}, bf16[1,256,1024]{2,1,0:T(8,128)(2,1)S(1)}, u32[]{:S(2)}, u32[]{:S(2)}) %collective-permute-start.1) | collective-permute-done | bytes 524320 | tf_op jit(solution)/shard_map/ppermute | solution.py:23
  12.8 1.5 convert_reduce_fusion.1
  14.6 1.0 fusion.20
  15.6 8.0 %all-to-all-start = ((bf16[1,8,32,1024]{3,2,0,1:T(8,128)(2,1)}), bf16[1,8,32,1024]{3,2,0,1:T(8,128)(2,1)S(1)}, u32[]{:S(2)}, u32[]{:S(2)}) async-start(bf16[1,8,32,1024]{3,2,0,1:T(8,128)(2,1)} %bitcast.3), calls=%async_computation | async-start | bytes 1048576 | tf_op jit(solution)/shard_map/all_to_all | solution.py:103
  23.9 8.7 %copy.41 = bf16[1024,3072]{0,1:T(8,128)(2,1)} copy(bf16[1024,3072]{1,0:T(8,128)(2,1)} %param.10) | data formatting | bytes 12582912 | tf_op args[2]
  32.6 5.6 %fusion.33 = f32[8,32,3,16,64]{4,1,3,2,0:T(8,128)S(1)} fusion(bf16[3,16,64,1024,1]{3,2,1,0,4:T(8,128)(2,1)} %bitcast.89, bf16[1,8,32,1024]{3,2,0,1:T(8,128)(2,1)S(1)} %all-to-all-done), kind=kOutput, calls=%fused_computation.57 | convolution fusion | flops 1610612736 | bytes 9961472 | tf_op jit(solution)/shard_map/dot_general | solution.py:54
  38.2 1.2 multiply_reduce_fusion.2
  39.6 1.4 divide_convert_fusion.2
  41.0 2.8 fusion.11
  43.9 1.5 fusion.12
  45.4 1.2 copy.46
  46.6 1.9 reshape.211
  48.5 1.5 convolution_convert_fusion.1
  50.0 4.2 all-to-all-start.1
  54.5 1.2 reduce-window.6
  56.1 5.0 %all-to-all-done.1 = bf16[8,1,32,1024]{3,2,1,0:T(8,128)(2,1)S(1)} async-done(((bf16[8,1,32,1024]{3,2,1,0:T(8,128)(2,1)}), bf16[8,1,32,1024]{3,2,1,0:T(8,128)(2,1)S(1)}, u32[]{:S(2)}, u32[]{:S(2)}) %all-to-all-start.1) | async-done | bytes 524320 | tf_op jit(solution)/shard_map/all_to_all | solution.py:106
  61.8 0.5 broadcast_in_dim.21
  62.3 1.2 reshape.228
  63.8 50.3 %scatter_fusion = bf16[16,64,1024]{2,1,0:T(8,128)(2,1)S(1)} fusion(bf16[16,64,1024]{2,1,0:T(8,128)(2,1)S(1)} %broadcast_in_dim.20, s32[512]{0:T(512)S(1)} %bitcast.86, bf16[512,1024]{1,0:T(8,128)(2,1)} %reshape.228), kind=kCustom, calls=%fused_computation.1 | custom fusion | bytes 3149824 | tf_op jit(solution)/shard_map/scatter | solution.py:127
  114.7 98.6 %all_to_all.28 = bf16[32,64,1024]{2,1,0:T(8,128)(2,1)S(1)} all-to-all(bf16[32,64,1024]{2,1,0:T(8,128)(2,1)S(1)} %bitcast.88), channel_id=1, replica_groups=mesh['tm'=8,'group'=4] {'tm','group'}, dimensions={0} | all-to-all | bytes 8388608 | tf_op jit(solution)/shard_map/all_to_all | solution.py:135
  213.4 12.5 %fusion.7 = bf16[2048,2048]{1,0:T(8,128)(2,1)S(1)} fusion(bf16[2048,1024]{1,0:T(8,128)(2,1)S(1)} %bitcast.90, bf16[1,1024,2048]{2,1,0:T(8,128)(2,1)S(1)} %copy-done.4), kind=kOutput, calls=%fused_computation.10 | convolution fusion | flops 8627683328 | bytes 16777216 | tf_op jit(solution)/shard_map/dot_general | solution.py:80
  225.8 10.9 %fusion.8 = f32[32,64,1024]{2,1,0:T(8,128)} fusion(bf16[32,64,2048]{2,1,0:T(8,128)(2,1)S(1)} %bitcast.98, bf16[1,2048,1024]{2,1,0:T(8,128)(2,1)S(1)} %copy-done.5), kind=kOutput, calls=%fused_computation.12 | convolution fusion | flops 8589934592 | bytes 20971520 | tf_op jit(solution)/shard_map/dot_general | solution.py:82
  236.8 4.8 %all-to-all-start.3 = ((f32[32,64,1024]{2,1,0:T(8,128)}), f32[32,64,1024]{2,1,0:T(8,128)}, u32[]{:S(2)}, u32[]{:S(2)}) async-start(f32[32,64,1024]{2,1,0:T(8,128)} %fusion.8), calls=%async_computation.3 | async-start | bytes 16777216 | tf_op jit(solution)/shard_map/all_to_all | solution.py:139
  242.1 185.7 %all-to-all-done.3 = f32[32,64,1024]{2,1,0:T(8,128)} async-done(((f32[32,64,1024]{2,1,0:T(8,128)}), f32[32,64,1024]{2,1,0:T(8,128)}, u32[]{:S(2)}, u32[]{:S(2)}) %all-to-all-start.3) | async-done | bytes 8388640 | tf_op jit(solution)/shard_map/all_to_all | solution.py:139
  427.8 6.3 %bitcast_reduce_fusion = bf16[16,64,1024]{2,1,0:T(8,128)(2,1)} fusion(f32[32,64,1024]{2,1,0:T(8,128)} %all-to-all-done.3), kind=kLoop, calls=%fused_computation.11 | loop fusion | flops 1048576 | bytes 10485760 | tf_op jit(solution)/shard_map/reduce_sum | solution.py:140
  434.1 10.7 %gather_fusion = bf16[512,1024]{1,0:T(8,128)(2,1)} fusion(bf16[16,64,1024]{2,1,0:T(8,128)(2,1)} %bitcast_reduce_fusion, s32[512]{0:T(512)S(1)} %bitcast.87), kind=kCustom, calls=%fused_computation | custom fusion | bytes 2101248 | tf_op jit(solution)/shard_map/gather | solution.py:141
  444.9 3.4 reshape.219
  448.3 4.3 multiply_reduce_fusion
  452.6 0.9 fusion.25
  (41 shorter events, 3.5 us)
Async XLA Ops:
  0.0 48.5 %copy-start = (bf16[1024,1024]{1,0:T(8,128)(2,1)S(1)}, bf16[1024,1024]{1,0:T(8,128)(2,1)}, u32[]{:S(2)}) copy-start(bf16[1024,1024]{1,0:T(8,128)(2,1)} %param.11) | copy-start | bytes 6291460
  0.0 23.6 %copy-start.3 = (s32[1,256,2]{1,2,0:T(2,128)S(1)}, s32[1,256,2]{1,2,0:T(2,128)}, u32[]{:S(2)}) copy-start(s32[1,256,2]{1,2,0:T(2,128)} %param.13) | copy-start | bytes 6148
  0.0 12.8 %collective-permute-start.1 = (bf16[1,256,1024]{2,1,0:T(8,128)(2,1)}, bf16[1,256,1024]{2,1,0:T(8,128)(2,1)S(1)}, u32[]{:S(2)}, u32[]{:S(2)}) collective-permute-start(bf16[1,256,1024]{2,1,0:T(8,128)(2,1)} %param.8), channel_id=1, source_target_pairs={{4,0},{8,4},{12,8},{16,12},{20,16},{24,20},{28,24},{5,1},{9,5},{13... | collective-permute-start | bytes 1572872 | tf_op jit(solution)/shard_map/ppermute | solution.py:23
  2.7 10.1 %collective-permute-start = (bf16[1,256,1024]{2,1,0:T(8,128)(2,1)}, bf16[1,256,1024]{2,1,0:T(8,128)(2,1)S(1)}, u32[]{:S(2)}, u32[]{:S(2)}) collective-permute-start(bf16[1,256,1024]{2,1,0:T(8,128)(2,1)} %param.8), channel_id=1, source_target_pairs={{0,4},{4,8},{8,12},{12,16},{16,20},{20,24},{24,28},{1,5},{5,9},{9,... | collective-permute-start | bytes 1572872 | tf_op jit(solution)/shard_map/ppermute | solution.py:21
  15.6 17.0 %all-to-all-start = ((bf16[1,8,32,1024]{3,2,0,1:T(8,128)(2,1)}), bf16[1,8,32,1024]{3,2,0,1:T(8,128)(2,1)S(1)}, u32[]{:S(2)}, u32[]{:S(2)}) async-start(bf16[1,8,32,1024]{3,2,0,1:T(8,128)(2,1)} %bitcast.3), calls=%async_computation | async-start | bytes 1048576 | tf_op jit(solution)/shard_map/all_to_all | solution.py:103
  50.0 11.0 %all-to-all-start.1 = ((bf16[8,1,32,1024]{3,2,1,0:T(8,128)(2,1)}), bf16[8,1,32,1024]{3,2,1,0:T(8,128)(2,1)S(1)}, u32[]{:S(2)}, u32[]{:S(2)}) async-start(bf16[8,1,32,1024]{3,2,1,0:T(8,128)(2,1)} %bitcast.92), calls=%async_computation.1 | async-start | bytes 1048576 | tf_op jit(solution)/shard_map/all_to_all | solution.py:106
  114.7 98.7 %copy-start.4 = (bf16[1,1024,2048]{2,1,0:T(8,128)(2,1)S(1)}, bf16[1,1024,2048]{2,1,0:T(8,128)(2,1)}, u32[]{:S(2)}) copy-start(bf16[1,1024,2048]{2,1,0:T(8,128)(2,1)} %param.14) | copy-start | bytes 12582916
  213.4 12.5 %copy-start.5 = (bf16[1,2048,1024]{2,1,0:T(8,128)(2,1)S(1)}, bf16[1,2048,1024]{2,1,0:T(8,128)(2,1)}, u32[]{:S(2)}) copy-start(bf16[1,2048,1024]{2,1,0:T(8,128)(2,1)} %param.15) | copy-start | bytes 12582916
  236.8 4.9 %copy-start.2 = (bf16[1024,16]{0,1:T(8,128)(2,1)S(1)}, bf16[1024,16]{0,1:T(8,128)(2,1)}, u32[]{:S(2)}) copy-start(bf16[1024,16]{0,1:T(8,128)(2,1)} %param.12) | copy-start | bytes 98308
  236.8 191.0 %all-to-all-start.3 = ((f32[32,64,1024]{2,1,0:T(8,128)}), f32[32,64,1024]{2,1,0:T(8,128)}, u32[]{:S(2)}, u32[]{:S(2)}) async-start(f32[32,64,1024]{2,1,0:T(8,128)} %fusion.8), calls=%async_computation.3 | async-start | bytes 16777216 | tf_op jit(solution)/shard_map/all_to_all | solution.py:139
  434.1 19.4 %copy-start.1 = (bf16[1024,1024]{1,0:T(8,128)(2,1)S(1)}, bf16[1024,1024]{1,0:T(8,128)(2,1)}, u32[]{:S(2)}) copy-start(bf16[1024,1024]{1,0:T(8,128)(2,1)} %param.11) | copy-start | bytes 6291460
where the time goes:
time: 457 us; the launch traced here: 454 us
  waiting for transfers between devices  197 us (43%)
  blocking collectives  98.6 us (22%)
  local copies, waits for them, and re-layouts  80.8 us (18%)
  matrix products  35.1 us (8%)
  starting transfers between devices  22.8 us (5%)
  other arithmetic  19.2 us (4%)
    all_to_all x1, waiting for transfers between devices, body(): lax.all_to_all(partial_sum, ('tm', 'group'), split_axis=0, concat_axis=0,...  186 us
    all_to_all x1, blocking collectives, body(): lax.all_to_all(doubled, ('tm', 'group'), split_axis=0, concat_axis=0, til...  98.6 us
    scatter x1, local copies, waits for them, and re-layouts, body(): outbox = jnp.zeros((experts, capacity, D), jnp.bfloat16).at[flat_ids, slo...  50.3 us
    dot_general x1, matrix products, half_partial(): jnp.dot(flat_rows, inner_weight, preferred_element_type=jnp.float32)  12.5 us
    dot_general x1, matrix products, half_partial(): jnp.dot(hidden, outer_weight, preferred_element_type=jnp.float32)  10.9 us
    gather x1, local copies, waits for them, and re-layouts, body(): results[flat_ids, slot_index].reshape(spatial, 2, D).astype(jnp.float32)  10.7 us
  transfers between devices with their start and end apart: 5, of which 3 were waited for; matrix products, arithmetic and copies ran while one was open for 3% of the time, Pallas kernels for 0%

commit v1 on v0

v1 whole, which is shorter than its diff:
```python
import math

import jax
import jax.numpy as jnp
from jax import lax
from jax.sharding import PartitionSpec as P

HD = 64


def layer_normed(values):
    values = values.astype(jnp.float32)
    centre = jnp.mean(values, -1, keepdims=True)
    spread = jnp.mean((values - centre) ** 2, -1, keepdims=True)
    return ((values - centre) / jnp.sqrt(spread + 1e-05)).astype(jnp.bfloat16)


def unit_scaled(values):
    return (values / jnp.sqrt(jnp.mean(values * values, -1, keepdims=True) + 1e-06)).astype(
        jnp.bfloat16
    )


def convolved(frames, conv_weight):
    wide = frames.astype(jnp.float32)
    padded = jnp.pad(wide, ((1, 1), (0, 0), (0, 0)))
    summed = conv_weight[0] * padded[:-2] + conv_weight[1] * wide + conv_weight[2] * padded[2:]
    return (wide + summed).astype(jnp.bfloat16)


def time_mixing(normed, qkv_weight, attn_out_weight):
    frames, across, channels = normed.shape
    heads = channels // HD
    projected = jnp.dot(
        normed.reshape(frames * across, channels), qkv_weight, preferred_element_type=jnp.float32
    )
    projected = projected.reshape(frames, across, 3, heads, HD)
    queries = unit_scaled(projected[:, :, 0])
    keys_all = unit_scaled(projected[:, :, 1])
    values_all = projected[:, :, 2].astype(jnp.bfloat16)
    scores = jnp.einsum(
        "fshd,gshd->shfg", queries, keys_all, preferred_element_type=jnp.float32
    ) / math.sqrt(HD)
    weights = jnp.exp(scores)
    weights = (weights / jnp.sum(weights, -1, keepdims=True)).astype(jnp.bfloat16)
    context = jnp.einsum(
        "shfg,gshd->fshd", weights, values_all, preferred_element_type=jnp.float32
    ).astype(jnp.bfloat16)
    mixed_out = jnp.dot(
        context.reshape(frames * across, channels),
        attn_out_weight,
        preferred_element_type=jnp.float32,
    )
    return mixed_out.astype(jnp.bfloat16).reshape(frames, across, channels)


def body(
    tokens,
    conv_weight,
    qkv_weight,
    attn_out_weight,
    router_weight,
    expert_ids,
    expert_in,
    expert_out,
):
    shards = lax.axis_size("tm")
    groups = lax.axis_size("group")
    classes = groups // 2
    mine = lax.axis_index("group") // 2
    spatial, channels = tokens.shape[1:]
    across = spatial // shards
    experts = router_weight.shape[1]
    capacity = 4 * spatial // experts

    def swapped(rows, step):
        if step == 0:
            return rows
        return lax.ppermute(rows, "group", [(i, i ^ step) for i in range(groups)])

    routed = expert_ids.reshape(spatial, 2)
    ids = [swapped(routed, step) for step in range(groups)]

    received = lax.all_to_all(
        tokens.reshape(1, shards, across, channels), "tm", split_axis=1, concat_axis=0, tiled=True
    ).reshape(shards, across, channels)
    stream_one = convolved(received, conv_weight)
    attended = time_mixing(layer_normed(stream_one), qkv_weight, attn_out_weight)
    stream_two = (stream_one.astype(jnp.float32) + attended.astype(jnp.float32)).astype(
        jnp.bfloat16
    )
    stream = lax.all_to_all(
        stream_two.reshape(shards, 1, across, channels),
        "tm",
        split_axis=0,
        concat_axis=1,
        tiled=True,
    ).reshape(spatial, channels)

    home = jnp.arange(shards, dtype=jnp.int32) * classes + mine
    blocks = [swapped(stream, step) for step in range(groups)]
    partials = []
    for step in range(groups):
        rows = layer_normed(blocks[step])
        logits = jnp.dot(rows, router_weight, preferred_element_type=jnp.float32)
        matches = ids[step][:, :, None] == jnp.arange(experts, dtype=jnp.int32)
        chosen = jnp.sum(jnp.where(matches, logits[:, None, :], 0.0), -1)
        gates = jax.nn.sigmoid(chosen)
        shares = gates / jnp.sum(gates, -1, keepdims=True)
        here = ids[step][:, :, None] == home
        weight = jnp.sum(jnp.where(here, shares[:, :, None], 0.0), 1)
        member = jnp.any(here, 1)
        order = jnp.arange(spatial, dtype=jnp.int32)
        earlier = (order[:, None] > order[None, :]).astype(jnp.bfloat16)
        rank = jnp.dot(
            earlier, member.astype(jnp.bfloat16), preferred_element_type=jnp.float32
        ).astype(jnp.int32)
        slots = jnp.arange(capacity, dtype=jnp.int32)
        picks = member[:, :, None] & (rank[:, :, None] == slots)
        send = picks.astype(jnp.bfloat16).reshape(spatial, shards * capacity)
        back = jnp.where(picks, weight[:, :, None], 0.0).astype(jnp.bfloat16)
        back = back.reshape(spatial, shards * capacity)
        outbox = lax.dot_general(
            send, rows, (((0,), (0,)), ((), ())), preferred_element_type=jnp.float32
        ).astype(jnp.bfloat16)
        inbox = lax.all_to_all(
            outbox.reshape(shards, capacity, channels), "tm", split_axis=0, concat_axis=0, tiled=True
        ).reshape(shards * capacity, channels)
        hidden = jax.nn.gelu(
            jnp.dot(inbox, expert_in[0], preferred_element_type=jnp.float32)
        ).astype(jnp.bfloat16)
        partial = jnp.dot(hidden, expert_out[0], preferred_element_type=jnp.float32)
        returned = lax.all_to_all(
            partial.astype(jnp.bfloat16).reshape(shards, capacity, channels),
            "tm",
            split_axis=0,
            concat_axis=0,
            tiled=True,
        ).reshape(shards * capacity, channels)
        mixed = jnp.dot(back, returned, preferred_element_type=jnp.float32)
        if step:
            mixed = swapped(mixed.astype(jnp.bfloat16), step).astype(jnp.float32)
        partials.append(mixed)
    total = stream.astype(jnp.float32)
    for mixed in partials:
        total = total + mixed
    return total.astype(jnp.bfloat16).reshape(1, spatial, channels)


def solution(mesh):
    placed = (
        P("tm", "group", None),
        P(),
        P(),
        P(),
        P(),
        P("tm", "group", None),
        P(("tm", "group"), None, None),
        P(("tm", "group"), None, None),
    )
    return jax.shard_map(
        body, mesh=mesh, in_specs=placed, out_specs=P("tm", "group", None), check_vma=False
    )
```

time: 457 us -> 281 us (0.61)
  waiting for transfers between devices: 197 us -> 91.9 us
  blocking collectives: 98.6 us -> 0 us
  local copies, waits for them, and re-layouts: 80.8 us -> 15.5 us
  starting transfers between devices: 22.8 us -> 79 us
  matrix products: 35.1 us -> 71.2 us
    all_to_all x3 -> x10, waiting for transfers between devices: 191 us -> 32.9 us  [the longest x4 18.3 us: body(): lax.all_to_all(outbox.reshape(shards, capacity, channels), 'tm', split_ax...]
    all_to_all x1 -> x0, blocking collectives: 98.6 us -> none  [body(): lax.all_to_all(doubled, ('tm', 'group'), split_axis=0, concat_axis=0, til...]
    all_to_all x3 -> x10, starting transfers between devices: 17.1 us -> 71.6 us  [the longest x4 31.2 us: body(): lax.all_to_all(partial.astype(jnp.bfloat16).reshape(shards, capacity, cha...]
    ppermute x2 -> x9, waiting for transfers between devices: 6.21 us -> 59 us  [swapped(): return lax.ppermute(rows, 'group', [(i, i ^ step) for i in range(groups)])]
    scatter x1 -> x0, local copies, waits for them, and re-layouts: 50.3 us -> none  [body(): outbox = jnp.zeros((experts, capacity, D), jnp.bfloat16).at[flat_ids, slo...]
    dot_general x3 -> x20, matrix products: 23.6 us -> 60.5 us  [the longest x4 37.4 us: body(): partial = jnp.dot(hidden, expert_out[0], preferred_element_type=jnp.float32)]
    gather x1 -> x0, local copies, waits for them, and re-layouts: 10.7 us -> none  [body(): results[flat_ids, slot_index].reshape(spatial, 2, D).astype(jnp.float32)]
    reduce_sum x4 -> x5, other arithmetic: 10.8 us -> 2.1 us  [the longest x4 1.33 us: body(): shares = gates / jnp.sum(gates, -1, keepdims=True)]
  transfers between devices with their start and end apart: 5 -> 19, of which waited for: 3 -> 11; matrix products, arithmetic and copies ran while one was open for 3% -> 31% of each run, Pallas kernels for 0% -> 0%
where the time goes in v1:
time: 281 us; the launch traced here: 279 us
  waiting for transfers between devices  91.9 us (33%)
  starting transfers between devices  79 us (28%)
  matrix products  71.2 us (25%)
  other arithmetic  20.7 us (7%)
  local copies, waits for them, and re-layouts  15.5 us (6%)
    ppermute x9, waiting for transfers between devices, swapped(): return lax.ppermute(rows, 'group', [(i, i ^ step) for i in range(groups)])  59 us
    dot_general x4, matrix products, body(): partial = jnp.dot(hidden, expert_out[0], preferred_element_type=jnp.float32)  37.4 us
    all_to_all x4, starting transfers between devices, body(): lax.all_to_all(partial.astype(jnp.bfloat16).reshape(shards, capacity, cha...  31.2 us
    all_to_all x4, starting transfers between devices, body(): lax.all_to_all(outbox.reshape(shards, capacity, channels), 'tm', split_ax...  31 us
    all_to_all x4, waiting for transfers between devices, body(): lax.all_to_all(outbox.reshape(shards, capacity, channels), 'tm', split_ax...  18.3 us
    all_to_all x4, waiting for transfers between devices, body(): lax.all_to_all(partial.astype(jnp.bfloat16).reshape(shards, capacity, cha...  10.6 us
    dot_general x4, matrix products, body(): mixed = jnp.dot(back, returned, preferred_element_type=jnp.float32)  10.5 us
    unnamed x51, local copies, waits for them, and re-layouts  9.39 us
  transfers between devices with their start and end apart: 19, of which 11 were waited for; matrix products, arithmetic and copies ran while one was open for 31% of the time, Pallas kernels for 0%

profile of v1, /device:TPU:9, one launch (start us, length us, event | category | flops | bytes accessed | tf_op | source)
XLA Modules:
  0.0 278.8 jit_solution(12095422469277350351)
XLA Ops:
  2.7 5.2 %all-to-all-start = ((bf16[1,8,32,1024]{3,2,0,1:T(8,128)(2,1)}), bf16[1,8,32,1024]{3,2,0,1:T(8,128)(2,1)S(1)}, u32[]{:S(2)}, u32[]{:S(2)}) async-start(bf16[1,8,32,1024]{3,2,0,1:T(8,128)(2,1)} %bitcast.183), calls=%async_computation | async-start | bytes 1048576 | tf_op jit(solution)/shard_map/all_to_all | solution.py:84
  8.8 8.7 %copy.63 = bf16[1024,3072]{0,1:T(8,128)(2,1)} copy(bf16[1024,3072]{1,0:T(8,128)(2,1)} %param.10) | data formatting | bytes 12582912 | tf_op args[2]
  20.7 5.7 %fusion.119 = f32[8,32,3,16,64]{4,1,3,2,0:T(8,128)S(1)} fusion(bf16[3,16,64,1024,1]{3,2,1,0,4:T(8,128)(2,1)} %bitcast.172, bf16[8,32,1024]{2,1,0:T(8,128)(2,1)S(1)} %get-tuple-element.16, f32[8,32]{1,0:T(8,128)S(1)} %add_sqrt_fusion.3, f32[8,32]{1,0:T(8,128)S(1)} %broadcast_multiply_fusion.1), kind=kOutput, calls=%fused_computation.138 | convolution fusion | flops 1611661312 | bytes 9963520 | tf_op jit(solution)/shard_map/dot_general | solution.py:34
  29.3 2.8 %fusion.56 = (f32[32,16,8]{2,1,0:T(8,128)S(1)}, f32[32,16,8,8]{2,3,1,0:T(8,128)S(1)}) fusion(bf16[8,32,16,64]{3,1,2,0:T(8,128)(2,1)S(1)} %get-tuple-element.18, bf16[8,32,16,64]{3,1,2,0:T(8,128)(2,1)S(1)} %get-tuple-element.17), kind=kOutput, calls=%fused_computation.61 | convolution fusion | flops 4255744 | bytes 1196032 | tf_op jit(solution)/shard_map/fshd,gshd->shfg/dot_general | solution.py:41
  38.4 4.2 %all-to-all-start.1 = ((bf16[8,1,32,1024]{3,2,1,0:T(8,128)(2,1)}), bf16[8,1,32,1024]{3,2,1,0:T(8,128)(2,1)S(1)}, u32[]{:S(2)}, u32[]{:S(2)}) async-start(bf16[8,1,32,1024]{3,2,1,0:T(8,128)(2,1)} %fusion.117), calls=%async_computation.1 | async-start | bytes 1048576 | tf_op jit(solution)/shard_map/all_to_all | solution.py:92
  45.4 4.0 %all-to-all-done.1 = bf16[8,1,32,1024]{3,2,1,0:T(8,128)(2,1)S(1)} async-done(((bf16[8,1,32,1024]{3,2,1,0:T(8,128)(2,1)}), bf16[8,1,32,1024]{3,2,1,0:T(8,128)(2,1)S(1)}, u32[]{:S(2)}, u32[]{:S(2)}) %all-to-all-start.1) | async-done | bytes 524320 | tf_op jit(solution)/shard_map/all_to_all | solution.py:92
  57.3 7.6 %all-to-all-start.2 = ((bf16[8,64,1024]{2,1,0:T(8,128)(2,1)}), bf16[8,64,1024]{2,1,0:T(8,128)(2,1)}, u32[]{:S(2)}, u32[]{:S(2)}) async-start(bf16[8,64,1024]{2,1,0:T(8,128)(2,1)} %bitcast.173), calls=%async_computation.2 | async-start | bytes 2097152 | tf_op jit(solution)/shard_map/all_to_all | solution.py:126
  66.7 2.7 collective-permute-done.1
  77.6 18.3 %collective-permute-done.7 = bf16[256,1024]{1,0:T(8,128)(2,1)S(1)} collective-permute-done((bf16[256,1024]{1,0:T(8,128)(2,1)S(1)}, bf16[256,1024]{1,0:T(8,128)(2,1)S(1)}, u32[]{:S(2)}, u32[]{:S(2)}) %collective-permute-start.7) | collective-permute-done | bytes 524320 | tf_op jit(solution)/shard_map/ppermute | solution.py:79
  100.0 8.1 %all-to-all-start.4 = ((bf16[8,64,1024]{2,1,0:T(8,128)(2,1)}), bf16[8,64,1024]{2,1,0:T(8,128)(2,1)}, u32[]{:S(2)}, u32[]{:S(2)}) async-start(bf16[8,64,1024]{2,1,0:T(8,128)(2,1)} %bitcast.175), calls=%async_computation.4 | async-start | bytes 2097152 | tf_op jit(solution)/shard_map/all_to_all | solution.py:126
  110.7 2.5 convolution_convert_fusion.1
  113.2 6.8 %all-to-all-done.4 = bf16[8,64,1024]{2,1,0:T(8,128)(2,1)} async-done(((bf16[8,64,1024]{2,1,0:T(8,128)(2,1)}), bf16[8,64,1024]{2,1,0:T(8,128)(2,1)}, u32[]{:S(2)}, u32[]{:S(2)}) %all-to-all-start.4) | async-done | bytes 1048608 | tf_op jit(solution)/shard_map/all_to_all | solution.py:126
  120.0 7.6 %all-to-all-start.6 = ((bf16[8,64,1024]{2,1,0:T(8,128)(2,1)}), bf16[8,64,1024]{2,1,0:T(8,128)(2,1)}, u32[]{:S(2)}, u32[]{:S(2)}) async-start(bf16[8,64,1024]{2,1,0:T(8,128)(2,1)} %bitcast.174), calls=%async_computation.6 | async-start | bytes 2097152 | tf_op jit(solution)/shard_map/all_to_all | solution.py:126
  130.5 9.0 %all-to-all-done.6 = bf16[8,64,1024]{2,1,0:T(8,128)(2,1)} async-done(((bf16[8,64,1024]{2,1,0:T(8,128)(2,1)}), bf16[8,64,1024]{2,1,0:T(8,128)(2,1)}, u32[]{:S(2)}, u32[]{:S(2)}) %all-to-all-start.6) | async-done | bytes 1048608 | tf_op jit(solution)/shard_map/all_to_all | solution.py:126
  139.5 7.7 %all-to-all-start.8 = ((bf16[8,64,1024]{2,1,0:T(8,128)(2,1)}), bf16[8,64,1024]{2,1,0:T(8,128)(2,1)}, u32[]{:S(2)}, u32[]{:S(2)}) async-start(bf16[8,64,1024]{2,1,0:T(8,128)(2,1)} %bitcast.176), calls=%async_computation.8 | async-start | bytes 2097152 | tf_op jit(solution)/shard_map/all_to_all | solution.py:126
  147.3 9.3 %fusion.60 = bf16[512,1024]{1,0:T(8,128)(2,1)} fusion(bf16[1,2048,1024]{2,1,0:T(8,128)(2,1)} %param.15, bf16[512,1024]{1,0:T(8,128)(2,1)} %bitcast.31, bf16[1,1024,2048]{2,1,0:T(8,128)(2,1)} %param.14), kind=kOutput, calls=%fused_computation.71 | convolution fusion | flops 4304928768 | bytes 10485760 | tf_op jit(solution)/shard_map/dot_general | solution.py:132
  156.6 2.6 all-to-all-done.8
  159.2 7.7 %all-to-all-start.5 = ((bf16[8,64,1024]{2,1,0:T(8,128)(2,1)}), bf16[8,64,1024]{2,1,0:T(8,128)(2,1)}, u32[]{:S(2)}, u32[]{:S(2)}) async-start(bf16[8,64,1024]{2,1,0:T(8,128)(2,1)} %bitcast.180), calls=%async_computation.5 | async-start | bytes 2097152 | tf_op jit(solution)/shard_map/all_to_all | solution.py:133
  166.9 9.4 %fusion.63 = bf16[512,1024]{1,0:T(8,128)(2,1)} fusion(bf16[1,2048,1024]{2,1,0:T(8,128)(2,1)} %param.15, bf16[512,1024]{1,0:T(8,128)(2,1)} %bitcast.37, bf16[1,1024,2048]{2,1,0:T(8,128)(2,1)} %param.14), kind=kOutput, calls=%fused_computation.72 | convolution fusion | flops 4304928768 | bytes 10485760 | tf_op jit(solution)/shard_map/dot_general | solution.py:132
  178.6 8.0 %all-to-all-start.7 = ((bf16[8,64,1024]{2,1,0:T(8,128)(2,1)}), bf16[8,64,1024]{2,1,0:T(8,128)(2,1)}, u32[]{:S(2)}, u32[]{:S(2)}) async-start(bf16[8,64,1024]{2,1,0:T(8,128)(2,1)} %bitcast.181), calls=%async_computation.7 | async-start | bytes 2097152 | tf_op jit(solution)/shard_map/all_to_all | solution.py:133
  186.5 9.4 %fusion.66 = bf16[512,1024]{1,0:T(8,128)(2,1)} fusion(bf16[1,2048,1024]{2,1,0:T(8,128)(2,1)} %param.15, bf16[512,1024]{1,0:T(8,128)(2,1)} %bitcast.43, bf16[1,1024,2048]{2,1,0:T(8,128)(2,1)} %param.14), kind=kOutput, calls=%fused_computation.73 | convolution fusion | flops 4304928768 | bytes 10485760 | tf_op jit(solution)/shard_map/dot_general | solution.py:132
  195.9 2.6 all-to-all-done.7
  198.4 7.7 %all-to-all-start.9 = ((bf16[8,64,1024]{2,1,0:T(8,128)(2,1)}), bf16[8,64,1024]{2,1,0:T(8,128)(2,1)}, u32[]{:S(2)}, u32[]{:S(2)}) async-start(bf16[8,64,1024]{2,1,0:T(8,128)(2,1)} %bitcast.179), calls=%async_computation.9 | async-start | bytes 2097152 | tf_op jit(solution)/shard_map/all_to_all | solution.py:133
  206.2 9.4 %fusion.57 = bf16[512,1024]{1,0:T(8,128)(2,1)} fusion(bf16[1,2048,1024]{2,1,0:T(8,128)(2,1)} %param.15, bf16[512,1024]{1,0:T(8,128)(2,1)} %bitcast.23, bf16[1,1024,2048]{2,1,0:T(8,128)(2,1)} %param.14), kind=kOutput, calls=%fused_computation.70 | convolution fusion | flops 4304928768 | bytes 10485760 | tf_op jit(solution)/shard_map/dot_general | solution.py:132
  215.6 2.5 fusion.70
  218.1 7.8 %all-to-all-start.3 = ((bf16[8,64,1024]{2,1,0:T(8,128)(2,1)}), bf16[8,64,1024]{2,1,0:T(8,128)(2,1)}, u32[]{:S(2)}, u32[]{:S(2)}) async-start(bf16[8,64,1024]{2,1,0:T(8,128)(2,1)} %bitcast.178), calls=%async_computation.3 | async-start | bytes 2097152 | tf_op jit(solution)/shard_map/all_to_all | solution.py:133
  225.9 2.5 fusion.71
  228.5 2.5 fusion.72
  232.2 5.7 %all-to-all-done.3 = bf16[8,64,1024]{2,1,0:T(8,128)(2,1)} async-done(((bf16[8,64,1024]{2,1,0:T(8,128)(2,1)}), bf16[8,64,1024]{2,1,0:T(8,128)(2,1)}, u32[]{:S(2)}, u32[]{:S(2)}) %all-to-all-start.3) | async-done | bytes 1048608 | tf_op jit(solution)/shard_map/all_to_all | solution.py:133
  237.8 24.9 %collective-permute-done.5 = bf16[256,1024]{1,0:T(8,128)(2,1)} collective-permute-done((bf16[256,1024]{1,0:T(8,128)(2,1)}, bf16[256,1024]{1,0:T(8,128)(2,1)}, u32[]{:S(2)}, u32[]{:S(2)}) %collective-permute-start.5) | collective-permute-done | bytes 524320 | tf_op jit(solution)/shard_map/ppermute | solution.py:79
  262.7 13.1 %collective-permute-done.8 = bf16[256,1024]{1,0:T(8,128)(2,1)} collective-permute-done((bf16[256,1024]{1,0:T(8,128)(2,1)}, bf16[256,1024]{1,0:T(8,128)(2,1)}, u32[]{:S(2)}, u32[]{:S(2)}) %collective-permute-start.8) | collective-permute-done | bytes 524320 | tf_op jit(solution)/shard_map/ppermute | solution.py:79
  275.8 3.0 %fusion.116 = bf16[1,256,1024]{2,1,0:T(8,128)(2,1)} fusion(bf16[256,1024]{1,0:T(8,128)(2,1)} %collective-permute-done.8, bf16[256,1024]{1,0:T(8,128)(2,1)} %collective-permute-done.5, bf16[256,1024]{1,0:T(8,128)(2,1)S(1)} %collective-permute-done.2, bf16[8,64,1024]{2,1,0:T(8,128)(2,1)} %all-to-all-done.3, bf16[256,1024]{1,0:T(8,128)(2,1)S(1)} %bitcast.171, ...), kind=kOutput, calls=%fused_computation.135 | convolution fusion | flops 271187968 | bytes 3684352 | tf_op jit(solution)/shard_map/dot_general | solution.py:140
  (135 shorter events, 49.5 us)
Async XLA Ops:
  0.0 36.7 %copy-start = (bf16[1024,1024]{1,0:T(8,128)(2,1)S(1)}, bf16[1024,1024]{1,0:T(8,128)(2,1)}, u32[]{:S(2)}) copy-start(bf16[1024,1024]{1,0:T(8,128)(2,1)} %param.11) | copy-start | bytes 6291460
  0.0 18.1 %collective-permute-start = (s32[256,2]{0,1:T(2,128)}, s32[256,2]{0,1:T(2,128)S(1)}, u32[]{:S(2)}, u32[]{:S(2)}) collective-permute-start(s32[256,2]{0,1:T(2,128)} %bitcast.185), channel_id=1, source_target_pairs={{0,1},{1,0},{2,3},{3,2},{4,5},{5,4},{6,7},{7,6},{8,9},{9,8},{10,11... | collective-permute-start | bytes 6152 | tf_op jit(solution)/shard_map/ppermute | solution.py:79
  0.0 18.1 %collective-permute-start.3 = (s32[256,2]{0,1:T(2,128)}, s32[256,2]{0,1:T(2,128)S(1)}, u32[]{:S(2)}, u32[]{:S(2)}) collective-permute-start(s32[256,2]{0,1:T(2,128)} %bitcast.186), channel_id=1, source_target_pairs={{0,2},{1,3},{2,0},{3,1},{4,6},{5,7},{6,4},{7,5},{8,10},{9,11},{10,... | collective-permute-start | bytes 6152 | tf_op jit(solution)/shard_map/ppermute | solution.py:79
  2.5 15.7 %collective-permute-start.6 = (s32[256,2]{0,1:T(2,128)}, s32[256,2]{0,1:T(2,128)S(1)}, u32[]{:S(2)}, u32[]{:S(2)}) collective-permute-start(s32[256,2]{0,1:T(2,128)} %bitcast.187), channel_id=1, source_target_pairs={{0,3},{1,2},{2,1},{3,0},{4,7},{5,6},{6,5},{7,4},{8,11},{9,10},{10,... | collective-permute-start | bytes 6152 | tf_op jit(solution)/shard_map/ppermute | solution.py:79
  2.7 17.2 %all-to-all-start = ((bf16[1,8,32,1024]{3,2,0,1:T(8,128)(2,1)}), bf16[1,8,32,1024]{3,2,0,1:T(8,128)(2,1)S(1)}, u32[]{:S(2)}, u32[]{:S(2)}) async-start(bf16[1,8,32,1024]{3,2,0,1:T(8,128)(2,1)} %bitcast.183), calls=%async_computation | async-start | bytes 1048576 | tf_op jit(solution)/shard_map/all_to_all | solution.py:84
  18.3 24.4 %copy-start.22 = (pred[256,8]{0,1:T(8,128)(4,1)}, pred[256,8]{0,1:T(8,128)(4,1)S(1)}, u32[]{:S(2)}) copy-start(pred[256,8]{0,1:T(8,128)(4,1)S(1)} %get-tuple-element.12) | copy-start | bytes 6148
  18.3 24.5 %copy-start.18 = (pred[256,8]{0,1:T(8,128)(4,1)}, pred[256,8]{0,1:T(8,128)(4,1)S(1)}, u32[]{:S(2)}) copy-start(pred[256,8]{0,1:T(8,128)(4,1)S(1)} %get-tuple-element.14) | copy-start | bytes 6148
  18.3 25.8 %copy-start.10 = (pred[256,8]{0,1:T(8,128)(4,1)}, pred[256,8]{0,1:T(8,128)(4,1)S(1)}, u32[]{:S(2)}) copy-start(pred[256,8]{0,1:T(8,128)(4,1)S(1)} %get-tuple-element.11) | copy-start | bytes 6148
  38.4 11.0 %all-to-all-start.1 = ((bf16[8,1,32,1024]{3,2,1,0:T(8,128)(2,1)}), bf16[8,1,32,1024]{3,2,1,0:T(8,128)(2,1)S(1)}, u32[]{:S(2)}, u32[]{:S(2)}) async-start(bf16[8,1,32,1024]{3,2,1,0:T(8,128)(2,1)} %fusion.117), calls=%async_computation.1 | async-start | bytes 1048576 | tf_op jit(solution)/shard_map/all_to_all | solution.py:92
  49.4 20.0 %collective-permute-start.1 = (bf16[256,1024]{1,0:T(8,128)(2,1)S(1)}, bf16[256,1024]{1,0:T(8,128)(2,1)}, u32[]{:S(2)}, u32[]{:S(2)}) collective-permute-start(bf16[256,1024]{1,0:T(8,128)(2,1)S(1)} %bitcast.167), channel_id=1, source_target_pairs={{0,1},{1,0},{2,3},{3,2},{4,5},{5,4},{6,7},{7,6},{8,9},{9,8},{10,11... | collective-permute-start | bytes 1572872 | tf_op jit(solution)/shard_map/ppermute | solution.py:79
  50.5 23.0 %collective-permute-start.4 = (bf16[256,1024]{1,0:T(8,128)(2,1)S(1)}, bf16[256,1024]{1,0:T(8,128)(2,1)}, u32[]{:S(2)}, u32[]{:S(2)}) collective-permute-start(bf16[256,1024]{1,0:T(8,128)(2,1)S(1)} %bitcast.168), channel_id=1, source_target_pairs={{0,2},{1,3},{2,0},{3,1},{4,6},{5,7},{6,4},{7,5},{8,10},{9,11},{10,... | collective-permute-start | bytes 1572872 | tf_op jit(solution)/shard_map/ppermute | solution.py:79
  52.6 43.2 %collective-permute-start.7 = (bf16[256,1024]{1,0:T(8,128)(2,1)S(1)}, bf16[256,1024]{1,0:T(8,128)(2,1)S(1)}, u32[]{:S(2)}, u32[]{:S(2)}) collective-permute-start(bf16[256,1024]{1,0:T(8,128)(2,1)S(1)} %bitcast.169), channel_id=1, source_target_pairs={{0,3},{1,2},{2,1},{3,0},{4,7},{5,6},{6,5},{7,4},{8,11},{9,10},{10,... | collective-permute-start | bytes 1572872 | tf_op jit(solution)/shard_map/ppermute | solution.py:79
  57.3 42.7 %all-to-all-start.2 = ((bf16[8,64,1024]{2,1,0:T(8,128)(2,1)}), bf16[8,64,1024]{2,1,0:T(8,128)(2,1)}, u32[]{:S(2)}, u32[]{:S(2)}) async-start(bf16[8,64,1024]{2,1,0:T(8,128)(2,1)} %bitcast.173), calls=%async_computation.2 | async-start | bytes 2097152 | tf_op jit(solution)/shard_map/all_to_all | solution.py:126
  64.9 31.1 %copy-start.6 = (s32[256,2]{0,1:T(2,128)S(1)}, s32[256,2]{0,1:T(2,128)}, u32[]{:S(2)}) copy-start(s32[256,2]{0,1:T(2,128)} %copy-done.5) | copy-start | bytes 6148
  76.0 33.9 %copy-start.8 = (s32[256,2]{0,1:T(2,128)S(1)}, s32[256,2]{0,1:T(2,128)}, u32[]{:S(2)}) copy-start(s32[256,2]{0,1:T(2,128)} %copy-done.7) | copy-start | bytes 6148
  77.3 21.2 %copy-start.2 = (bf16[256,1024]{1,0:T(8,128)(2,1)}, bf16[256,1024]{1,0:T(8,128)(2,1)S(1)}, u32[]{:S(2)}) copy-start(bf16[256,1024]{1,0:T(8,128)(2,1)S(1)} %fusion.88) | copy-start | bytes 1572868
  98.5 30.6 %copy-start.1 = (bf16[256,1024]{1,0:T(8,128)(2,1)S(1)}, bf16[256,1024]{1,0:T(8,128)(2,1)}, u32[]{:S(2)}) copy-start(bf16[256,1024]{1,0:T(8,128)(2,1)} %fusion.86) | copy-start | bytes 1572868
  100.0 20.0 %all-to-all-start.4 = ((bf16[8,64,1024]{2,1,0:T(8,128)(2,1)}), bf16[8,64,1024]{2,1,0:T(8,128)(2,1)}, u32[]{:S(2)}, u32[]{:S(2)}) async-start(bf16[8,64,1024]{2,1,0:T(8,128)(2,1)} %bitcast.175), calls=%async_computation.4 | async-start | bytes 2097152 | tf_op jit(solution)/shard_map/all_to_all | solution.py:126
  120.0 19.6 %all-to-all-start.6 = ((bf16[8,64,1024]{2,1,0:T(8,128)(2,1)}), bf16[8,64,1024]{2,1,0:T(8,128)(2,1)}, u32[]{:S(2)}, u32[]{:S(2)}) async-start(bf16[8,64,1024]{2,1,0:T(8,128)(2,1)} %bitcast.174), calls=%async_computation.6 | async-start | bytes 2097152 | tf_op jit(solution)/shard_map/all_to_all | solution.py:126
  139.5 19.6 %all-to-all-start.8 = ((bf16[8,64,1024]{2,1,0:T(8,128)(2,1)}), bf16[8,64,1024]{2,1,0:T(8,128)(2,1)}, u32[]{:S(2)}, u32[]{:S(2)}) async-start(bf16[8,64,1024]{2,1,0:T(8,128)(2,1)} %bitcast.176), calls=%async_computation.8 | async-start | bytes 2097152 | tf_op jit(solution)/shard_map/all_to_all | solution.py:126
  159.2 19.4 %all-to-all-start.5 = ((bf16[8,64,1024]{2,1,0:T(8,128)(2,1)}), bf16[8,64,1024]{2,1,0:T(8,128)(2,1)}, u32[]{:S(2)}, u32[]{:S(2)}) async-start(bf16[8,64,1024]{2,1,0:T(8,128)(2,1)} %bitcast.180), calls=%async_computation.5 | async-start | bytes 2097152 | tf_op jit(solution)/shard_map/all_to_all | solution.py:133
  178.6 19.9 %all-to-all-start.7 = ((bf16[8,64,1024]{2,1,0:T(8,128)(2,1)}), bf16[8,64,1024]{2,1,0:T(8,128)(2,1)}, u32[]{:S(2)}, u32[]{:S(2)}) async-start(bf16[8,64,1024]{2,1,0:T(8,128)(2,1)} %bitcast.181), calls=%async_computation.7 | async-start | bytes 2097152 | tf_op jit(solution)/shard_map/all_to_all | solution.py:133
  198.4 19.7 %all-to-all-start.9 = ((bf16[8,64,1024]{2,1,0:T(8,128)(2,1)}), bf16[8,64,1024]{2,1,0:T(8,128)(2,1)}, u32[]{:S(2)}, u32[]{:S(2)}) async-start(bf16[8,64,1024]{2,1,0:T(8,128)(2,1)} %bitcast.179), calls=%async_computation.9 | async-start | bytes 2097152 | tf_op jit(solution)/shard_map/all_to_all | solution.py:133
  215.6 10.4 %copy-start.21 = (pred[256,8]{0,1:T(8,128)(4,1)S(1)}, pred[256,8]{0,1:T(8,128)(4,1)}, u32[]{:S(2)}) copy-start(pred[256,8]{0,1:T(8,128)(4,1)} %copy-done.20) | copy-start | bytes 6148
  215.6 12.9 %copy-start.14 = (s32[256,8]{0,1:T(8,128)S(1)}, s32[256,8]{0,1:T(8,128)}, u32[]{:S(2)}) copy-start(s32[256,8]{0,1:T(8,128)} %convolution_convert_fusion.6) | copy-start | bytes 24580
  215.6 12.9 %copy-start.19 = (pred[256,8]{0,1:T(8,128)(4,1)S(1)}, pred[256,8]{0,1:T(8,128)(4,1)}, u32[]{:S(2)}) copy-start(pred[256,8]{0,1:T(8,128)(4,1)} %copy-done.18) | copy-start | bytes 6148
  218.1 19.7 %collective-permute-start.2 = (bf16[256,1024]{1,0:T(8,128)(2,1)}, bf16[256,1024]{1,0:T(8,128)(2,1)S(1)}, u32[]{:S(2)}, u32[]{:S(2)}) collective-permute-start(bf16[256,1024]{1,0:T(8,128)(2,1)} %fusion.70), channel_id=1, source_target_pairs={{0,1},{1,0},{2,3},{3,2},{4,5},{5,4},{6,7},{7,6},{8,9},{9,8},{10,11... | collective-permute-start | bytes 1572872 | tf_op jit(solution)/shard_map/ppermute | solution.py:79
  218.1 57.7 %copy-start.11 = (pred[256,8]{0,1:T(8,128)(4,1)S(1)}, pred[256,8]{0,1:T(8,128)(4,1)}, u32[]{:S(2)}) copy-start(pred[256,8]{0,1:T(8,128)(4,1)} %copy-done.10) | copy-start | bytes 6148
  218.1 57.7 %copy-start.13 = (s32[256,8]{0,1:T(8,128)S(1)}, s32[256,8]{0,1:T(8,128)}, u32[]{:S(2)}) copy-start(s32[256,8]{0,1:T(8,128)} %copy-done.12) | copy-start | bytes 24580
  218.1 19.7 %all-to-all-start.3 = ((bf16[8,64,1024]{2,1,0:T(8,128)(2,1)}), bf16[8,64,1024]{2,1,0:T(8,128)(2,1)}, u32[]{:S(2)}, u32[]{:S(2)}) async-start(bf16[8,64,1024]{2,1,0:T(8,128)(2,1)} %bitcast.178), calls=%async_computation.3 | async-start | bytes 2097152 | tf_op jit(solution)/shard_map/all_to_all | solution.py:133
  228.5 34.3 %collective-permute-start.5 = (bf16[256,1024]{1,0:T(8,128)(2,1)}, bf16[256,1024]{1,0:T(8,128)(2,1)}, u32[]{:S(2)}, u32[]{:S(2)}) collective-permute-start(bf16[256,1024]{1,0:T(8,128)(2,1)} %fusion.71), channel_id=1, source_target_pairs={{0,2},{1,3},{2,0},{3,1},{4,6},{5,7},{6,4},{7,5},{8,10},{9,11},{10,... | collective-permute-start | bytes 1572872 | tf_op jit(solution)/shard_map/ppermute | solution.py:79
  231.0 44.8 %collective-permute-start.8 = (bf16[256,1024]{1,0:T(8,128)(2,1)}, bf16[256,1024]{1,0:T(8,128)(2,1)}, u32[]{:S(2)}, u32[]{:S(2)}) collective-permute-start(bf16[256,1024]{1,0:T(8,128)(2,1)} %fusion.72), channel_id=1, source_target_pairs={{0,3},{1,2},{2,1},{3,0},{4,7},{5,6},{6,5},{7,4},{8,11},{9,10},{10,... | collective-permute-start | bytes 1572872 | tf_op jit(solution)/shard_map/ppermute | solution.py:79
  (12 other events, 78.9 us)

commit v2 on v1

v2 whole, which is shorter than its diff:
```python
import functools
import math

import jax
import jax.numpy as jnp
from jax import lax
from jax.experimental import pallas as pl
from jax.experimental.pallas import tpu as pltpu
from jax.sharding import PartitionSpec as P


HD = 64
VMEM = pl.BlockSpec(memory_space=pltpu.VMEM)
SMEM = pl.BlockSpec(memory_space=pltpu.SMEM)
LIMIT = pltpu.CompilerParams(vmem_limit_bytes=28 * 2**20)


def layer_normed(values):
    values = values.astype(jnp.float32)
    centre = jnp.mean(values, -1, keepdims=True)
    spread = jnp.mean((values - centre) ** 2, -1, keepdims=True)
    return ((values - centre) / jnp.sqrt(spread + 1e-05)).astype(jnp.bfloat16)


def dot(a, b, contract=((1,), (0,))):
    return lax.dot_general(a, b, (contract, ((), ())), preferred_element_type=jnp.float32)


PLACES = 16


def mixing_kernel(tokens, taps, qkv, outer, stream, kept, normed, queries, keys, values, mixed):
    frames, across, channels = tokens.shape
    blocks = across // PLACES
    rows = frames * PLACES
    bf16 = jnp.bfloat16

    def spans(frame):
        for block in range(blocks):
            at = block * rows + frame * PLACES
            yield block * PLACES, at

    for frame in range(frames):
        wide = tokens[frame].astype(jnp.float32)
        summed = taps[1:2, :] * wide
        if frame > 0:
            summed = taps[0:1, :] * tokens[frame - 1].astype(jnp.float32) + summed
        if frame < frames - 1:
            summed = summed + taps[2:3, :] * tokens[frame + 1].astype(jnp.float32)
        stream_one = (wide + summed).astype(bf16)
        unit = layer_normed(stream_one)
        for place, at in spans(frame):
            kept[at : at + PLACES, :] = stream_one[place : place + PLACES, :]
            normed[at : at + PLACES, :] = unit[place : place + PLACES, :]

    width = 256
    head_a = lax.broadcasted_iota(jnp.int32, (width, width), 0) // HD
    head_b = lax.broadcasted_iota(jnp.int32, (width, width), 1) // HD
    same_head = jnp.where(head_a == head_b, 1.0 / HD, 0.0).astype(bf16)

    for target, base in ((queries, 0), (keys, channels)):
        for at in range(0, channels, width):
            part = dot(normed[...], qkv[:, base + at : base + at + width])
            square = part * part
            high = square.astype(bf16)
            low = (square - high.astype(jnp.float32)).astype(bf16)
            mean = dot(high, same_head) + dot(low, same_head)
            target[:, at : at + width] = (part / jnp.sqrt(mean + 1e-06)).astype(bf16)
    for at in range(0, channels, width):
        base = 2 * channels + at
        values[:, at : at + width] = dot(normed[...], qkv[:, base : base + width]).astype(bf16)

    pair = 2 * HD
    first = lax.broadcasted_iota(jnp.int32, (rows, pair), 1) < HD
    place_a = lax.broadcasted_iota(jnp.int32, (rows, 2 * rows), 0) % PLACES
    place_b = lax.broadcasted_iota(jnp.int32, (rows, 2 * rows), 1) % PLACES
    same_place = place_a == place_b
    ones_a = jnp.where(first, 1.0, 0.0).astype(bf16)
    ones_b = jnp.where(first, 0.0, 1.0).astype(bf16)
    ones = jnp.concatenate([ones_a, ones_b], 0)
    for block in range(blocks):
        here = slice(block * rows, (block + 1) * rows)
        for at in range(0, channels, pair):
            query = queries[here, at : at + pair]
            key = keys[here, at : at + pair]
            value = values[here, at : at + pair]
            both = jnp.concatenate([key * ones_a, key * ones_b], 0)
            scores = dot(query, both, ((1,), (1,))) * (1.0 / math.sqrt(HD))
            weights = jnp.where(same_place, jnp.exp(scores), 0.0).astype(bf16)
            both = jnp.concatenate([value * ones_a, value * ones_b], 0)
            summed = dot(weights, jnp.concatenate([both, ones], 1))
            mixed[here, at : at + pair] = (summed[:, :pair] / summed[:, pair:]).astype(bf16)

    attended = dot(mixed[...], outer[...]).astype(bf16).astype(jnp.float32)
    total = (kept[...].astype(jnp.float32) + attended).astype(bf16)
    for frame in range(frames):
        for place, at in spans(frame):
            stream[frame, place : place + PLACES, :] = total[at : at + PLACES, :]


def time_mixing(received, conv_weight, qkv_weight, attn_out_weight):
    frames, across, channels = received.shape
    scratch = pltpu.VMEM((frames * across, channels), jnp.bfloat16)
    return pl.pallas_call(
        mixing_kernel,
        out_shape=jax.ShapeDtypeStruct(received.shape, jnp.bfloat16),
        in_specs=[VMEM] * 4,
        out_specs=VMEM,
        scratch_shapes=[scratch] * 6,
        compiler_params=LIMIT,
        name="mixing",
    )(received, conv_weight, qkv_weight, attn_out_weight)


def dispatch_kernel(
    chips, classes, capacity, place, own, other, own_ids, other_ids, router, *outs
):
    boxes, combs = outs[:chips], outs[chips:]
    tokens = own.shape[0]
    experts = router.shape[0]
    slots = chips * capacity
    chip, core, mine = place[0], place[1], place[2]
    slot = lax.broadcasted_iota(jnp.int32, (slots, tokens), 0)
    target = jnp.bitwise_xor(slot // capacity, chip)
    target = (2 * target + core) * classes + mine
    order = slot % capacity
    before = lax.broadcasted_iota(jnp.int32, (tokens, tokens), 0)
    after = lax.broadcasted_iota(jnp.int32, (tokens, tokens), 1)
    earlier = (before < after).astype(jnp.float32).astype(jnp.bfloat16)
    kinds = lax.broadcasted_iota(jnp.int32, (experts, tokens), 0)
    for side, (rows, ids) in enumerate(((own, own_ids), (other, other_ids))):
        first, second = ids[0:1, :], ids[1:2, :]
        logits = dot(router[...], rows[...], ((1,), (1,)))
        gate_a = jax.nn.sigmoid(
            jnp.sum(jnp.where(kinds == first, logits, 0.0), 0, keepdims=True)
        )
        gate_b = jax.nn.sigmoid(
            jnp.sum(jnp.where(kinds == second, logits, 0.0), 0, keepdims=True)
        )
        whole = gate_a + gate_b
        hit_a, hit_b = target == first, target == second
        member = jnp.where(hit_a | hit_b, 1.0, 0.0)
        rank = dot(member.astype(jnp.bfloat16), earlier)
        taken = jnp.where(rank == order.astype(jnp.float32), member, 0.0)
        share = jnp.where(hit_a, gate_a / whole, gate_b / whole)
        combs[side][...] = (taken * share).astype(jnp.bfloat16)
        moved = dot(taken.astype(jnp.bfloat16), rows[...]).astype(jnp.bfloat16)
        for k in range(chips):
            boxes[k][side * capacity : (side + 1) * capacity, :] = moved[
                k * capacity : (k + 1) * capacity, :
            ]


def dispatched(place, own, other, own_ids, other_ids, router, chips, classes, capacity):
    tokens, channels = own.shape
    bf16 = jnp.bfloat16
    shapes = [jax.ShapeDtypeStruct((2 * capacity, channels), bf16)] * chips
    shapes += [jax.ShapeDtypeStruct((chips * capacity, tokens), bf16)] * 2
    outs = pl.pallas_call(
        functools.partial(dispatch_kernel, chips, classes, capacity),
        out_shape=shapes,
        in_specs=[SMEM] + [VMEM] * 5,
        out_specs=[VMEM] * (chips + 2),
        compiler_params=LIMIT,
        name="dispatch",
    )(place, own, other, own_ids, other_ids, router)
    return outs[:chips], outs[chips:]


def expert_kernel(chips, *refs):
    inputs, (inner, outer) = refs[:chips], refs[chips : chips + 2]
    outputs, (gathered, total) = refs[chips + 2 : 2 * chips + 2], refs[2 * chips + 2 :]
    step, last = pl.program_id(0), pl.num_programs(0) - 1
    size = inputs[0].shape[0]

    @pl.when(step == 0)
    def _():
        for k in range(chips):
            gathered[k * size : (k + 1) * size, :] = inputs[k][...]

    hidden = jax.nn.gelu(dot(gathered[...], inner[0])).astype(jnp.bfloat16)
    part = dot(hidden, outer[0])

    @pl.when(step == 0)
    def _():
        total[...] = part

    @pl.when((step > 0) & (step < last))
    def _():
        total[...] += part

    @pl.when(step == last)
    def _():
        done = (total[...] + part).astype(jnp.bfloat16)
        for k in range(chips):
            outputs[k][...] = done[k * size : (k + 1) * size, :]


def expert_rows(pieces, expert_in, expert_out):
    chips = len(pieces)
    size, channels = pieces[0].shape
    units = expert_in.shape[2]
    tile = units // 4
    whole = pl.BlockSpec((size, channels), lambda i: (0, 0))
    rows = chips * size
    return pl.pallas_call(
        functools.partial(expert_kernel, chips),
        out_shape=[jax.ShapeDtypeStruct((size, channels), jnp.bfloat16)] * chips,
        grid=(units // tile,),
        in_specs=[whole] * chips
        + [
            pl.BlockSpec((1, channels, tile), lambda i: (0, 0, i)),
            pl.BlockSpec((1, tile, channels), lambda i: (0, i, 0)),
        ],
        out_specs=[whole] * chips,
        scratch_shapes=[
            pltpu.VMEM((rows, channels), jnp.bfloat16),
            pltpu.VMEM((rows, channels), jnp.float32),
        ],
        compiler_params=LIMIT,
        cost_estimate=pl.CostEstimate(
            flops=4 * rows * channels * units,
            transcendentals=rows * units,
            bytes_accessed=4 * channels * units,
        ),
        name="experts",
    )(*pieces, *(pltpu.with_memory_space_constraint(w, pltpu.HBM) for w in (expert_in, expert_out)))


def combine_kernel(chips, *refs):
    pieces, combs = refs[:chips], refs[chips : chips + 2]
    own, other = refs[chips + 2 :]
    capacity = pieces[0].shape[0] // 2
    for side, out in enumerate((own, other)):
        rows = jnp.concatenate(
            [pieces[k][side * capacity : (side + 1) * capacity, :] for k in range(chips)], 0
        )
        out[...] = dot(combs[side][...], rows, ((0,), (0,))).astype(out.dtype)


def combined(pieces, combs):
    chips = len(pieces)
    tokens = combs[0].shape[1]
    channels = pieces[0].shape[1]
    return pl.pallas_call(
        functools.partial(combine_kernel, chips),
        out_shape=[
            jax.ShapeDtypeStruct((tokens, channels), jnp.float32),
            jax.ShapeDtypeStruct((tokens, channels), jnp.bfloat16),
        ],
        in_specs=[VMEM] * (chips + 2),
        out_specs=[VMEM] * 2,
        compiler_params=LIMIT,
        name="combine",
    )(*pieces, *combs)


def body(
    tokens,
    conv_weight,
    qkv_weight,
    attn_out_weight,
    router_weight,
    expert_ids,
    expert_in,
    expert_out,
):
    shards = lax.axis_size("tm")
    groups = lax.axis_size("group")
    chips = shards // 2
    classes = groups // 2
    spatial, channels = tokens.shape[1:]
    across = spatial // shards
    experts = router_weight.shape[1]
    capacity = 4 * spatial // experts
    at = lax.axis_index("tm")
    place = jnp.stack([at // 2, at % 2, lax.axis_index("group") // 2]).astype(jnp.int32)

    def swapped(rows, axis, step):
        if step == 0:
            return rows
        size = lax.axis_size(axis)
        return lax.ppermute(rows, axis, [(i, i ^ step) for i in range(size)])

    routed = expert_ids.reshape(spatial, 2).T
    pair = jnp.concatenate([routed, swapped(routed, "tm", 1)], 0)
    ids = [swapped(pair, "group", step) for step in range(groups)]

    received = lax.all_to_all(
        tokens.reshape(1, shards, across, channels),
        "tm",
        split_axis=1,
        concat_axis=0,
        tiled=True,
    ).reshape(shards, across, channels)
    stream_two = time_mixing(received, conv_weight, qkv_weight, attn_out_weight)
    stream = lax.all_to_all(
        stream_two.reshape(shards, 1, across, channels),
        "tm",
        split_axis=0,
        concat_axis=1,
        tiled=True,
    ).reshape(spatial, channels)

    router = router_weight.T
    normed = layer_normed(stream)
    blocks = [normed]
    for step in range(1, groups):
        if step % 2:
            blocks.append(swapped(blocks[step - 1], "group", 1))
        else:
            blocks.append(swapped(normed, "group", step))
    total = stream.astype(jnp.float32)
    for step in range(groups):
        own = blocks[step]
        other = swapped(own, "tm", 1)
        boxes, combs = dispatched(
            place,
            own,
            other,
            ids[step][:2],
            ids[step][2:],
            router,
            chips,
            classes,
            capacity,
        )
        pieces = [swapped(boxes[k], "tm", 2 * k) for k in range(chips)]
        results = expert_rows(pieces, expert_in, expert_out)
        returned = [swapped(results[k], "tm", 2 * k) for k in range(chips)]
        here, there = combined(returned, combs)
        mixed = here + swapped(there, "tm", 1).astype(jnp.float32)
        if step:
            mixed = swapped(mixed.astype(jnp.bfloat16), "group", step)
            mixed = mixed.astype(jnp.float32)
        total = total + mixed
    return total.astype(jnp.bfloat16).reshape(1, spatial, channels)


def solution(mesh):
    placed = (
        P("tm", "group", None),
        P(),
        P(),
        P(),
        P(),
        P("tm", "group", None),
        P(("tm", "group"), None, None),
        P(("tm", "group"), None, None),
    )
    return jax.shard_map(
        body, mesh=mesh, in_specs=placed, out_specs=P("tm", "group", None), check_vma=False
    )
```

time: 281 us -> 231 us (0.82)
  matrix products: 71.2 us -> 0 us
  Pallas kernels: 0 us -> 45.8 us
  blocking collectives: 0 us -> 25 us
  starting transfers between devices: 79 us -> 54.6 us
  other arithmetic: 20.7 us -> 2.49 us
  local copies, waits for them, and re-layouts: 15.5 us -> 5.27 us
  waiting for transfers between devices: 91.9 us -> 95.9 us
    all_to_all x10 -> x0, starting transfers between devices: 71.6 us -> none  [the longest x4 31.2 us: body(): lax.all_to_all(partial.astype(jnp.bfloat16).reshape(shards, capacity, cha...]
    dot_general x24 -> x0, matrix products: 71.2 us -> none  [the longest x4 37.4 us: body(): partial = jnp.dot(hidden, expert_out[0], preferred_element_type=jnp.float32)]
    ppermute x9 -> x42, starting transfers between devices: 7.33 us -> 54.6 us  [swapped(): return lax.ppermute(rows, axis, [(i, i ^ step) for i in range(size)])]
    pallas_call x0 -> x13, Pallas kernels: none -> 45.8 us  [the longest x4 31.8 us: expert_rows(): pl.pallas_call(functools.partial(expert_kernel, chips), out_shape=[jax.Sh...]
    ppermute x9 -> x42, waiting for transfers between devices: 59 us -> 95.9 us  [swapped(): return lax.ppermute(rows, axis, [(i, i ^ step) for i in range(size)])]
    all_to_all x10 -> x0, waiting for transfers between devices: 32.9 us -> none  [the longest x4 18.3 us: body(): lax.all_to_all(outbox.reshape(shards, capacity, channels), 'tm', split_ax...]
    all_to_all x0 -> x2, blocking collectives: none -> 25 us  [the longest x1 12.9 us: body(): lax.all_to_all(tokens.reshape(1, shards, across, channels), 'tm', split_a...]
    unnamed x51 -> x10, local copies, waits for them, and re-layouts: 9.39 us -> 5.1 us
  transfers between devices with their start and end apart: 19 -> 42, of which waited for: 11 -> 13; matrix products, arithmetic and copies ran while one was open for 31% -> 0% of each run, Pallas kernels for 0% -> 17%
where the time goes in v2:
time: 231 us; the launch traced here: 229 us
  waiting for transfers between devices  95.9 us (42%)
  starting transfers between devices  54.6 us (24%)
  Pallas kernels  45.8 us (20%)
  blocking collectives  25 us (11%)
  local copies, waits for them, and re-layouts  5.27 us (2%)
  other arithmetic  2.49 us (1%)
    ppermute x42, waiting for transfers between devices, swapped(): return lax.ppermute(rows, axis, [(i, i ^ step) for i in range(size)])  95.9 us
    ppermute x42, starting transfers between devices, swapped(): return lax.ppermute(rows, axis, [(i, i ^ step) for i in range(size)])  54.6 us
    pallas_call x4, Pallas kernels, expert_rows(): pl.pallas_call(functools.partial(expert_kernel, chips), out_shape=[jax.Sh...  31.8 us
    all_to_all x1, blocking collectives, body(): lax.all_to_all(tokens.reshape(1, shards, across, channels), 'tm', split_a...  12.9 us
    all_to_all x1, blocking collectives, body(): lax.all_to_all(stream_two.reshape(shards, 1, across, channels), 'tm', spl...  12.1 us
    pallas_call x1, Pallas kernels, time_mixing(): pl.pallas_call(mixing_kernel, out_shape=jax.ShapeDtypeStruct(received.sha...  6.51 us
    pallas_call x4, Pallas kernels, dispatched(): pl.pallas_call(functools.partial(dispatch_kernel, chips, classes, capacit...  5.67 us
    unnamed x10, local copies, waits for them, and re-layouts  5.1 us
  transfers between devices with their start and end apart: 42, of which 13 were waited for; matrix products, arithmetic and copies ran while one was open for 0% of the time, Pallas kernels for 17%

profile of v2, /device:TPU:9, one launch (start us, length us, event | category | flops | bytes accessed | tf_op | source)
XLA Modules:
  0.0 229.3 jit_solution(5357774736973937920)
XLA Ops:
  0.0 12.9 %all_to_all.8 = bf16[1,8,32,1024]{3,2,0,1:T(8,128)(2,1)S(1)} all-to-all(bf16[1,8,32,1024]{3,2,0,1:T(8,128)(2,1)} %bitcast.37), channel_id=1, replica_groups=mesh['tm'=8,'group'=4] {'tm'}, dimensions={1} | all-to-all | bytes 1048576 | tf_op jit(solution)/shard_map/all_to_all | solution.py:289
  12.9 2.8 %copy-done = bf16[1024,3072]{1,0:T(8,128)(2,1)S(1)} copy-done((bf16[1024,3072]{1,0:T(8,128)(2,1)S(1)}, bf16[1024,3072]{1,0:T(8,128)(2,1)}, u32[]{:S(2)}) %copy-start) | copy-done | bytes 6291480
  15.7 1.6 copy-done.1
  18.0 6.5 %mixing.1 = bf16[8,32,1024]{2,1,0:T(8,128)(2,1)S(1)} custom-call(bf16[8,32,1024]{2,1,0:T(8,128)(2,1)S(1)} %bitcast.29, f32[3,1024]{1,0:T(4,128)S(1)} %copy-done.3, bf16[1024,3072]{1,0:T(8,128)(2,1)S(1)} %copy-done, bf16[1024,1024]{1,0:T(8,128)(2,1)S(1)} %copy-done.1), custom_call_target="tpu_custom_call" | custom-call | tf_op jit(solution)/shard_map/mixing/pallas_call | solution.py:104
  24.5 12.1 %all_to_all.9 = bf16[8,1,32,1024]{3,2,1,0:T(8,128)(2,1)S(1)} all-to-all(bf16[8,1,32,1024]{3,2,1,0:T(8,128)(2,1)S(1)} %bitcast.28), channel_id=1, replica_groups=mesh['tm'=8,'group'=4] {'tm'}, dimensions={0} | all-to-all | bytes 1048576 | tf_op jit(solution)/shard_map/all_to_all | solution.py:297
  37.5 2.4 %collective-permute-start.20 = (bf16[256,1024]{1,0:T(8,128)(2,1)S(1)}, bf16[256,1024]{1,0:T(8,128)(2,1)S(1)}, u32[]{:S(2)}, u32[]{:S(2)}) collective-permute-start(bf16[256,1024]{1,0:T(8,128)(2,1)S(1)} %fusion.3.own), channel_id=1, source_target_pairs={{0,2},{1,3},{2,0},{3,1},{4,6},{5,7},{6,4},{7,5},{8,10},{9,11},{10,... | collective-permute-start | bytes 1572872 | tf_op jit(solution)/shard_map/ppermute | solution.py:283
  40.0 22.6 %collective-permute-done.20.own = bf16[256,1024]{1,0:T(8,128)(2,1)S(1)} collective-permute-done((bf16[256,1024]{1,0:T(8,128)(2,1)S(1)}, bf16[256,1024]{1,0:T(8,128)(2,1)S(1)}, u32[]{:S(2)}, u32[]{:S(2)}) %collective-permute-start.20) | collective-permute-done | bytes 524320 | tf_op jit(solution)/shard_map/ppermute | solution.py:283
  63.6 1.8 collective-permute-done.1.other_ids
  65.4 3.1 %collective-permute-start.22 = (s32[4,256]{1,0:T(4,128)S(1)}, s32[4,256]{1,0:T(4,128)S(1)}, u32[]{:S(2)}, u32[]{:S(2)}) collective-permute-start(s32[4,256]{1,0:T(4,128)S(1)} %pad_add_fusion), channel_id=1, source_target_pairs={{0,2},{1,3},{2,0},{3,1},{4,6},{5,7},{6,4},{7,5},{8,10},{9,11},{10,... | collective-permute-start | bytes 12296 | tf_op jit(solution)/shard_map/ppermute | solution.py:283
  69.5 3.6 %collective-permute-start.11 = (s32[4,256]{1,0:T(4,128)S(1)}, s32[4,256]{1,0:T(4,128)S(1)}, u32[]{:S(2)}, u32[]{:S(2)}) collective-permute-start(s32[4,256]{1,0:T(4,128)S(1)} %pad_add_fusion), channel_id=1, source_target_pairs={{0,1},{1,0},{2,3},{3,2},{4,5},{5,4},{6,7},{7,6},{8,9},{9,8},{10,11... | collective-permute-start | bytes 12296 | tf_op jit(solution)/shard_map/ppermute | solution.py:283
  73.1 2.1 collective-permute-start.10
  77.6 3.9 %collective-permute-done.11 = s32[4,256]{1,0:T(4,128)S(1)} collective-permute-done((s32[4,256]{1,0:T(4,128)S(1)}, s32[4,256]{1,0:T(4,128)S(1)}, u32[]{:S(2)}, u32[]{:S(2)}) %collective-permute-start.11) | collective-permute-done | bytes 4128 | tf_op jit(solution)/shard_map/ppermute | solution.py:283
  81.8 1.8 collective-permute-start.25
  83.6 2.1 collective-permute-start.32
  89.5 4.7 %collective-permute-done.24.refs_2_ = bf16[128,1024]{1,0:T(8,128)(2,1)S(1)} collective-permute-done((bf16[128,1024]{1,0:T(8,128)(2,1)S(1)}, bf16[128,1024]{1,0:T(8,128)(2,1)S(1)}, u32[]{:S(2)}, u32[]{:S(2)}) %collective-permute-start.24) | collective-permute-done | bytes 262176 | tf_op jit(solution)/shard_map/ppermute | solution.py:283
  95.2 8.0 %experts.6 = (bf16[128,1024]{1,0:T(8,128)(2,1)S(1)}, bf16[128,1024]{1,0:T(8,128)(2,1)S(1)}, bf16[128,1024]{1,0:T(8,128)(2,1)S(1)}, bf16[128,1024]{1,0:T(8,128)(2,1)S(1)}) custom-call(bf16[128,1024]{1,0:T(8,128)(2,1)S(1)} %get-tuple-element.77.refs_0_, bf16[128,1024]{1,0:T(8,128)(2,1)S(1)} %collective-permute-done.23.refs_1_, ...), custom_call_target="tpu_custom_call" | custom-call | flops 4294967296 | bytes 8388608 | tf_op jit(solution)/shard_map/experts/pallas_call | solution.py:206
  103.2 1.7 collective-permute-start.13
  108.4 8.0 %experts.4 = (bf16[128,1024]{1,0:T(8,128)(2,1)S(1)}, bf16[128,1024]{1,0:T(8,128)(2,1)S(1)}, bf16[128,1024]{1,0:T(8,128)(2,1)S(1)}, bf16[128,1024]{1,0:T(8,128)(2,1)S(1)}) custom-call(bf16[128,1024]{1,0:T(8,128)(2,1)S(1)} %get-tuple-element.53.refs_0_, bf16[128,1024]{1,0:T(8,128)(2,1)S(1)} %collective-permute-done.2.refs_1_, ...), custom_call_target="tpu_custom_call" | custom-call | flops 4294967296 | bytes 8388608 | tf_op jit(solution)/shard_map/experts/pallas_call | solution.py:206
  120.7 3.1 %collective-permute-done.27.refs_2_ = bf16[128,1024]{1,0:T(8,128)(2,1)S(1)} collective-permute-done((bf16[128,1024]{1,0:T(8,128)(2,1)S(1)}, bf16[128,1024]{1,0:T(8,128)(2,1)S(1)}, u32[]{:S(2)}, u32[]{:S(2)}) %collective-permute-start.27) | collective-permute-done | bytes 262176 | tf_op jit(solution)/shard_map/ppermute | solution.py:283
  123.9 2.3 %collective-permute-start.35 = (bf16[128,1024]{1,0:T(8,128)(2,1)S(1)}, bf16[128,1024]{1,0:T(8,128)(2,1)S(1)}, u32[]{:S(2)}, u32[]{:S(2)}) collective-permute-start(bf16[128,1024]{1,0:T(8,128)(2,1)S(1)} %get-tuple-element.91), channel_id=1, source_target_pairs={{0,16},{4,20},{8,24},{12,28},{16,0},{20,4},{24,8},{28,12},{1,17},{... | collective-permute-start | bytes 786440 | tf_op jit(solution)/shard_map/ppermute | solution.py:283
  127.3 8.0 %experts.5 = (bf16[128,1024]{1,0:T(8,128)(2,1)S(1)}, bf16[128,1024]{1,0:T(8,128)(2,1)S(1)}, bf16[128,1024]{1,0:T(8,128)(2,1)S(1)}, bf16[128,1024]{1,0:T(8,128)(2,1)S(1)}) custom-call(bf16[128,1024]{1,0:T(8,128)(2,1)S(1)} %get-tuple-element.65.refs_0_, bf16[128,1024]{1,0:T(8,128)(2,1)S(1)} %collective-permute-done.12.refs_1_, ...), custom_call_target="tpu_custom_call" | custom-call | flops 4294967296 | bytes 8388608 | tf_op jit(solution)/shard_map/experts/pallas_call | solution.py:206
  138.4 7.9 %collective-permute-done.35.refs_2_ = bf16[128,1024]{1,0:T(8,128)(2,1)S(1)} collective-permute-done((bf16[128,1024]{1,0:T(8,128)(2,1)S(1)}, bf16[128,1024]{1,0:T(8,128)(2,1)S(1)}, u32[]{:S(2)}, u32[]{:S(2)}) %collective-permute-start.35) | collective-permute-done | bytes 262176 | tf_op jit(solution)/shard_map/ppermute | solution.py:283
  146.3 4.0 %collective-permute-start.17 = (bf16[128,1024]{1,0:T(8,128)(2,1)S(1)}, bf16[128,1024]{1,0:T(8,128)(2,1)S(1)}, u32[]{:S(2)}, u32[]{:S(2)}) collective-permute-start(bf16[128,1024]{1,0:T(8,128)(2,1)S(1)} %get-tuple-element.72), channel_id=1, source_target_pairs={{0,24},{4,28},{8,16},{12,20},{16,8},{20,12},{24,0},{28,4},{1,25},{... | collective-permute-start | bytes 786440 | tf_op jit(solution)/shard_map/ppermute | solution.py:283
  150.2 7.4 %collective-permute-start.29 = (bf16[256,1024]{1,0:T(8,128)(2,1)S(1)}, bf16[256,1024]{1,0:T(8,128)(2,1)S(1)}, u32[]{:S(2)}, u32[]{:S(2)}) collective-permute-start(bf16[256,1024]{1,0:T(8,128)(2,1)S(1)} %get-tuple-element.88), channel_id=1, source_target_pairs={{0,4},{4,0},{8,12},{12,8},{16,20},{20,16},{24,28},{28,24},{1,5},{5... | collective-permute-start | bytes 1572872 | tf_op jit(solution)/shard_map/ppermute | solution.py:283
  157.6 8.0 %experts.7 = (bf16[128,1024]{1,0:T(8,128)(2,1)S(1)}, bf16[128,1024]{1,0:T(8,128)(2,1)S(1)}, bf16[128,1024]{1,0:T(8,128)(2,1)S(1)}, bf16[128,1024]{1,0:T(8,128)(2,1)S(1)}) custom-call(bf16[128,1024]{1,0:T(8,128)(2,1)S(1)} %get-tuple-element.89.refs_0_, bf16[128,1024]{1,0:T(8,128)(2,1)S(1)} %collective-permute-done.34.refs_1_, ...), custom_call_target="tpu_custom_call" | custom-call | flops 4294967296 | bytes 8388608 | tf_op jit(solution)/shard_map/experts/pallas_call | solution.py:206
  166.4 1.7 collective-permute-start.38
  170.9 2.4 %collective-permute-done.37.refs_1_ = bf16[128,1024]{1,0:T(8,128)(2,1)S(1)} collective-permute-done((bf16[128,1024]{1,0:T(8,128)(2,1)S(1)}, bf16[128,1024]{1,0:T(8,128)(2,1)S(1)}, u32[]{:S(2)}, u32[]{:S(2)}) %collective-permute-start.37) | collective-permute-done | bytes 262176 | tf_op jit(solution)/shard_map/ppermute | solution.py:283
  173.3 1.8 collective-permute-start.8
  175.1 5.7 %collective-permute-done.39.refs_3_ = bf16[128,1024]{1,0:T(8,128)(2,1)S(1)} collective-permute-done((bf16[128,1024]{1,0:T(8,128)(2,1)S(1)}, bf16[128,1024]{1,0:T(8,128)(2,1)S(1)}, u32[]{:S(2)}, u32[]{:S(2)}) %collective-permute-start.39) | collective-permute-done | bytes 262176 | tf_op jit(solution)/shard_map/ppermute | solution.py:283
  184.1 1.6 collective-permute-start.41
  185.8 19.7 %collective-permute-done.30 = bf16[256,1024]{1,0:T(8,128)(2,1)S(1)} collective-permute-done((bf16[256,1024]{1,0:T(8,128)(2,1)S(1)}, bf16[256,1024]{1,0:T(8,128)(2,1)S(1)}, u32[]{:S(2)}, u32[]{:S(2)}) %collective-permute-start.30) | collective-permute-done | bytes 524320 | tf_op jit(solution)/shard_map/ppermute | solution.py:283
  206.5 21.5 %collective-permute-done.41 = bf16[256,1024]{1,0:T(8,128)(2,1)S(1)} collective-permute-done((bf16[256,1024]{1,0:T(8,128)(2,1)S(1)}, bf16[256,1024]{1,0:T(8,128)(2,1)S(1)}, u32[]{:S(2)}, u32[]{:S(2)}) %collective-permute-start.41) | collective-permute-done | bytes 524320 | tf_op jit(solution)/shard_map/ppermute | solution.py:283
  (93 shorter events, 32.6 us)
Async XLA Ops:
  37.5 25.1 %collective-permute-start.20 = (bf16[256,1024]{1,0:T(8,128)(2,1)S(1)}, bf16[256,1024]{1,0:T(8,128)(2,1)S(1)}, u32[]{:S(2)}, u32[]{:S(2)}) collective-permute-start(bf16[256,1024]{1,0:T(8,128)(2,1)S(1)} %fusion.3.own), channel_id=1, source_target_pairs={{0,2},{1,3},{2,0},{3,1},{4,6},{5,7},{6,4},{7,5},{8,10},{9,11},{10,... | collective-permute-start | bytes 1572872 | tf_op jit(solution)/shard_map/ppermute | solution.py:283
  39.8 29.7 %collective-permute-start.9 = (bf16[256,1024]{1,0:T(8,128)(2,1)S(1)}, bf16[256,1024]{1,0:T(8,128)(2,1)S(1)}, u32[]{:S(2)}, u32[]{:S(2)}) collective-permute-start(bf16[256,1024]{1,0:T(8,128)(2,1)S(1)} %fusion.3.own), channel_id=1, source_target_pairs={{0,1},{1,0},{2,3},{3,2},{4,5},{5,4},{6,7},{7,6},{8,9},{9,8},{10,11... | collective-permute-start | bytes 1572872 | tf_op jit(solution)/shard_map/ppermute | solution.py:283
  63.1 18.7 %collective-permute-start = (bf16[256,1024]{1,0:T(8,128)(2,1)S(1)}, bf16[256,1024]{1,0:T(8,128)(2,1)S(1)}, u32[]{:S(2)}, u32[]{:S(2)}) collective-permute-start(bf16[256,1024]{1,0:T(8,128)(2,1)S(1)} %fusion.3.own), channel_id=1, source_target_pairs={{0,4},{4,0},{8,12},{12,8},{16,20},{20,16},{24,28},{28,24},{1,5},{5... | collective-permute-start | bytes 1572872 | tf_op jit(solution)/shard_map/ppermute | solution.py:283
  68.5 15.1 %collective-permute-start.31 = (bf16[256,1024]{1,0:T(8,128)(2,1)S(1)}, bf16[256,1024]{1,0:T(8,128)(2,1)S(1)}, u32[]{:S(2)}, u32[]{:S(2)}) collective-permute-start(bf16[256,1024]{1,0:T(8,128)(2,1)S(1)} %collective-permute-done.20.own), channel_id=1, source_target_pairs={{0,1},{1,0},{2,3},{3,2},{4,5},{5,4},{6,7},{7,6},{8,9},{9,8},{10,11... | collective-permute-start | bytes 1572872 | tf_op jit(solution)/shard_map/ppermute | solution.py:283
  73.1 13.9 %collective-permute-start.10 = (bf16[256,1024]{1,0:T(8,128)(2,1)S(1)}, bf16[256,1024]{1,0:T(8,128)(2,1)S(1)}, u32[]{:S(2)}, u32[]{:S(2)}) collective-permute-start(bf16[256,1024]{1,0:T(8,128)(2,1)S(1)} %collective-permute-done.9.own), channel_id=1, source_target_pairs={{0,4},{4,0},{8,12},{12,8},{16,20},{20,16},{24,28},{28,24},{1,5},{5... | collective-permute-start | bytes 1572872 | tf_op jit(solution)/shard_map/ppermute | solution.py:283
  76.7 12.5 %collective-permute-start.23 = (bf16[128,1024]{1,0:T(8,128)(2,1)S(1)}, bf16[128,1024]{1,0:T(8,128)(2,1)S(1)}, u32[]{:S(2)}, u32[]{:S(2)}) collective-permute-start(bf16[128,1024]{1,0:T(8,128)(2,1)S(1)} %get-tuple-element.78), channel_id=1, source_target_pairs={{0,8},{4,12},{8,0},{12,4},{16,24},{20,28},{24,16},{28,20},{1,9},{5... | collective-permute-start | bytes 786440 | tf_op jit(solution)/shard_map/ppermute | solution.py:283
  81.5 12.7 %collective-permute-start.24 = (bf16[128,1024]{1,0:T(8,128)(2,1)S(1)}, bf16[128,1024]{1,0:T(8,128)(2,1)S(1)}, u32[]{:S(2)}, u32[]{:S(2)}) collective-permute-start(bf16[128,1024]{1,0:T(8,128)(2,1)S(1)} %get-tuple-element.79), channel_id=1, source_target_pairs={{0,16},{4,20},{8,24},{12,28},{16,0},{20,4},{24,8},{28,12},{1,17},{... | collective-permute-start | bytes 786440 | tf_op jit(solution)/shard_map/ppermute | solution.py:283
  81.8 12.4 %collective-permute-start.25 = (bf16[128,1024]{1,0:T(8,128)(2,1)S(1)}, bf16[128,1024]{1,0:T(8,128)(2,1)S(1)}, u32[]{:S(2)}, u32[]{:S(2)}) collective-permute-start(bf16[128,1024]{1,0:T(8,128)(2,1)S(1)} %get-tuple-element.80), channel_id=1, source_target_pairs={{0,24},{4,28},{8,16},{12,20},{16,8},{20,12},{24,0},{28,4},{1,25},{... | collective-permute-start | bytes 786440 | tf_op jit(solution)/shard_map/ppermute | solution.py:283
  83.6 23.9 %collective-permute-start.32 = (bf16[256,1024]{1,0:T(8,128)(2,1)S(1)}, bf16[256,1024]{1,0:T(8,128)(2,1)S(1)}, u32[]{:S(2)}, u32[]{:S(2)}) collective-permute-start(bf16[256,1024]{1,0:T(8,128)(2,1)S(1)} %collective-permute-done.31.own), channel_id=1, source_target_pairs={{0,4},{4,0},{8,12},{12,8},{16,20},{20,16},{24,28},{28,24},{1,5},{5... | collective-permute-start | bytes 1572872 | tf_op jit(solution)/shard_map/ppermute | solution.py:283
  87.1 16.1 %collective-permute-start.2 = (bf16[128,1024]{1,0:T(8,128)(2,1)S(1)}, bf16[128,1024]{1,0:T(8,128)(2,1)S(1)}, u32[]{:S(2)}, u32[]{:S(2)}) collective-permute-start(bf16[128,1024]{1,0:T(8,128)(2,1)S(1)} %get-tuple-element.54), channel_id=1, source_target_pairs={{0,8},{4,12},{8,0},{12,4},{16,24},{20,28},{24,16},{28,20},{1,9},{5... | collective-permute-start | bytes 786440 | tf_op jit(solution)/shard_map/ppermute | solution.py:283
  89.2 15.7 %collective-permute-start.3 = (bf16[128,1024]{1,0:T(8,128)(2,1)S(1)}, bf16[128,1024]{1,0:T(8,128)(2,1)S(1)}, u32[]{:S(2)}, u32[]{:S(2)}) collective-permute-start(bf16[128,1024]{1,0:T(8,128)(2,1)S(1)} %get-tuple-element.55), channel_id=1, source_target_pairs={{0,16},{4,20},{8,24},{12,28},{16,0},{20,4},{24,8},{28,12},{1,17},{... | collective-permute-start | bytes 786440 | tf_op jit(solution)/shard_map/ppermute | solution.py:283
  103.2 14.6 %collective-permute-start.13 = (bf16[128,1024]{1,0:T(8,128)(2,1)S(1)}, bf16[128,1024]{1,0:T(8,128)(2,1)S(1)}, u32[]{:S(2)}, u32[]{:S(2)}) collective-permute-start(bf16[128,1024]{1,0:T(8,128)(2,1)S(1)} %get-tuple-element.67), channel_id=1, source_target_pairs={{0,16},{4,20},{8,24},{12,28},{16,0},{20,4},{24,8},{28,12},{1,17},{... | collective-permute-start | bytes 786440 | tf_op jit(solution)/shard_map/ppermute | solution.py:283
  104.9 13.4 %collective-permute-start.14 = (bf16[128,1024]{1,0:T(8,128)(2,1)S(1)}, bf16[128,1024]{1,0:T(8,128)(2,1)S(1)}, u32[]{:S(2)}, u32[]{:S(2)}) collective-permute-start(bf16[128,1024]{1,0:T(8,128)(2,1)S(1)} %get-tuple-element.68), channel_id=1, source_target_pairs={{0,24},{4,28},{8,16},{12,20},{16,8},{20,12},{24,0},{28,4},{1,25},{... | collective-permute-start | bytes 786440 | tf_op jit(solution)/shard_map/ppermute | solution.py:283
  105.7 13.9 %collective-permute-start.26 = (bf16[128,1024]{1,0:T(8,128)(2,1)S(1)}, bf16[128,1024]{1,0:T(8,128)(2,1)S(1)}, u32[]{:S(2)}, u32[]{:S(2)}) collective-permute-start(bf16[128,1024]{1,0:T(8,128)(2,1)S(1)} %get-tuple-element.82), channel_id=1, source_target_pairs={{0,8},{4,12},{8,0},{12,4},{16,24},{20,28},{24,16},{28,20},{1,9},{5... | collective-permute-start | bytes 786440 | tf_op jit(solution)/shard_map/ppermute | solution.py:283
  106.1 17.7 %collective-permute-start.27 = (bf16[128,1024]{1,0:T(8,128)(2,1)S(1)}, bf16[128,1024]{1,0:T(8,128)(2,1)S(1)}, u32[]{:S(2)}, u32[]{:S(2)}) collective-permute-start(bf16[128,1024]{1,0:T(8,128)(2,1)S(1)} %get-tuple-element.83), channel_id=1, source_target_pairs={{0,16},{4,20},{8,24},{12,28},{16,0},{20,4},{24,8},{28,12},{1,17},{... | collective-permute-start | bytes 786440 | tf_op jit(solution)/shard_map/ppermute | solution.py:283
  107.5 18.7 %collective-permute-start.28 = (bf16[128,1024]{1,0:T(8,128)(2,1)S(1)}, bf16[128,1024]{1,0:T(8,128)(2,1)S(1)}, u32[]{:S(2)}, u32[]{:S(2)}) collective-permute-start(bf16[128,1024]{1,0:T(8,128)(2,1)S(1)} %get-tuple-element.84), channel_id=1, source_target_pairs={{0,24},{4,28},{8,16},{12,20},{16,8},{20,12},{24,0},{28,4},{1,25},{... | collective-permute-start | bytes 786440 | tf_op jit(solution)/shard_map/ppermute | solution.py:283
  117.8 17.9 %collective-permute-start.5 = (bf16[128,1024]{1,0:T(8,128)(2,1)S(1)}, bf16[128,1024]{1,0:T(8,128)(2,1)S(1)}, u32[]{:S(2)}, u32[]{:S(2)}) collective-permute-start(bf16[128,1024]{1,0:T(8,128)(2,1)S(1)} %get-tuple-element.58), channel_id=1, source_target_pairs={{0,8},{4,12},{8,0},{12,4},{16,24},{20,28},{24,16},{28,20},{1,9},{5... | collective-permute-start | bytes 786440 | tf_op jit(solution)/shard_map/ppermute | solution.py:283
  118.3 18.8 %collective-permute-start.6 = (bf16[128,1024]{1,0:T(8,128)(2,1)S(1)}, bf16[128,1024]{1,0:T(8,128)(2,1)S(1)}, u32[]{:S(2)}, u32[]{:S(2)}) collective-permute-start(bf16[128,1024]{1,0:T(8,128)(2,1)S(1)} %get-tuple-element.59), channel_id=1, source_target_pairs={{0,16},{4,20},{8,24},{12,28},{16,0},{20,4},{24,8},{28,12},{1,17},{... | collective-permute-start | bytes 786440 | tf_op jit(solution)/shard_map/ppermute | solution.py:283
  119.7 18.8 %collective-permute-start.34 = (bf16[128,1024]{1,0:T(8,128)(2,1)S(1)}, bf16[128,1024]{1,0:T(8,128)(2,1)S(1)}, u32[]{:S(2)}, u32[]{:S(2)}) collective-permute-start(bf16[128,1024]{1,0:T(8,128)(2,1)S(1)} %get-tuple-element.90), channel_id=1, source_target_pairs={{0,8},{4,12},{8,0},{12,4},{16,24},{20,28},{24,16},{28,20},{1,9},{5... | collective-permute-start | bytes 786440 | tf_op jit(solution)/shard_map/ppermute | solution.py:283
  123.9 22.4 %collective-permute-start.35 = (bf16[128,1024]{1,0:T(8,128)(2,1)S(1)}, bf16[128,1024]{1,0:T(8,128)(2,1)S(1)}, u32[]{:S(2)}, u32[]{:S(2)}) collective-permute-start(bf16[128,1024]{1,0:T(8,128)(2,1)S(1)} %get-tuple-element.91), channel_id=1, source_target_pairs={{0,16},{4,20},{8,24},{12,28},{16,0},{20,4},{24,8},{28,12},{1,17},{... | collective-permute-start | bytes 786440 | tf_op jit(solution)/shard_map/ppermute | solution.py:283
  126.2 24.0 %collective-permute-start.36 = (bf16[128,1024]{1,0:T(8,128)(2,1)S(1)}, bf16[128,1024]{1,0:T(8,128)(2,1)S(1)}, u32[]{:S(2)}, u32[]{:S(2)}) collective-permute-start(bf16[128,1024]{1,0:T(8,128)(2,1)S(1)} %get-tuple-element.92), channel_id=1, source_target_pairs={{0,24},{4,28},{8,16},{12,20},{16,8},{20,12},{24,0},{28,4},{1,25},{... | collective-permute-start | bytes 786440 | tf_op jit(solution)/shard_map/ppermute | solution.py:283
  135.7 33.9 %collective-permute-start.7 = (bf16[128,1024]{1,0:T(8,128)(2,1)S(1)}, bf16[128,1024]{1,0:T(8,128)(2,1)S(1)}, u32[]{:S(2)}, u32[]{:S(2)}) collective-permute-start(bf16[128,1024]{1,0:T(8,128)(2,1)S(1)} %get-tuple-element.60), channel_id=1, source_target_pairs={{0,24},{4,28},{8,16},{12,20},{16,8},{20,12},{24,0},{28,4},{1,25},{... | collective-permute-start | bytes 786440 | tf_op jit(solution)/shard_map/ppermute | solution.py:283
  137.1 28.5 %collective-permute-start.15 = (bf16[128,1024]{1,0:T(8,128)(2,1)S(1)}, bf16[128,1024]{1,0:T(8,128)(2,1)S(1)}, u32[]{:S(2)}, u32[]{:S(2)}) collective-permute-start(bf16[128,1024]{1,0:T(8,128)(2,1)S(1)} %get-tuple-element.70), channel_id=1, source_target_pairs={{0,8},{4,12},{8,0},{12,4},{16,24},{20,28},{24,16},{28,20},{1,9},{5... | collective-permute-start | bytes 786440 | tf_op jit(solution)/shard_map/ppermute | solution.py:283
  138.4 28.0 %collective-permute-start.16 = (bf16[128,1024]{1,0:T(8,128)(2,1)S(1)}, bf16[128,1024]{1,0:T(8,128)(2,1)S(1)}, u32[]{:S(2)}, u32[]{:S(2)}) collective-permute-start(bf16[128,1024]{1,0:T(8,128)(2,1)S(1)} %get-tuple-element.71), channel_id=1, source_target_pairs={{0,16},{4,20},{8,24},{12,28},{16,0},{20,4},{24,8},{28,12},{1,17},{... | collective-permute-start | bytes 786440 | tf_op jit(solution)/shard_map/ppermute | solution.py:283
  146.3 21.8 %collective-permute-start.17 = (bf16[128,1024]{1,0:T(8,128)(2,1)S(1)}, bf16[128,1024]{1,0:T(8,128)(2,1)S(1)}, u32[]{:S(2)}, u32[]{:S(2)}) collective-permute-start(bf16[128,1024]{1,0:T(8,128)(2,1)S(1)} %get-tuple-element.72), channel_id=1, source_target_pairs={{0,24},{4,28},{8,16},{12,20},{16,8},{20,12},{24,0},{28,4},{1,25},{... | collective-permute-start | bytes 786440 | tf_op jit(solution)/shard_map/ppermute | solution.py:283
  150.2 32.2 %collective-permute-start.29 = (bf16[256,1024]{1,0:T(8,128)(2,1)S(1)}, bf16[256,1024]{1,0:T(8,128)(2,1)S(1)}, u32[]{:S(2)}, u32[]{:S(2)}) collective-permute-start(bf16[256,1024]{1,0:T(8,128)(2,1)S(1)} %get-tuple-element.88), channel_id=1, source_target_pairs={{0,4},{4,0},{8,12},{12,8},{16,20},{20,16},{24,28},{28,24},{1,5},{5... | collective-permute-start | bytes 1572872 | tf_op jit(solution)/shard_map/ppermute | solution.py:283
  168.1 12.7 %collective-permute-start.39 = (bf16[128,1024]{1,0:T(8,128)(2,1)S(1)}, bf16[128,1024]{1,0:T(8,128)(2,1)S(1)}, u32[]{:S(2)}, u32[]{:S(2)}) collective-permute-start(bf16[128,1024]{1,0:T(8,128)(2,1)S(1)} %get-tuple-element.96), channel_id=1, source_target_pairs={{0,24},{4,28},{8,16},{12,20},{16,8},{20,12},{24,0},{28,4},{1,25},{... | collective-permute-start | bytes 786440 | tf_op jit(solution)/shard_map/ppermute | solution.py:283
  169.6 13.1 %collective-permute-start.18 = (bf16[256,1024]{1,0:T(8,128)(2,1)S(1)}, bf16[256,1024]{1,0:T(8,128)(2,1)S(1)}, u32[]{:S(2)}, u32[]{:S(2)}) collective-permute-start(bf16[256,1024]{1,0:T(8,128)(2,1)S(1)} %get-tuple-element.76), channel_id=1, source_target_pairs={{0,4},{4,0},{8,12},{12,8},{16,20},{20,16},{24,28},{28,24},{1,5},{5... | collective-permute-start | bytes 1572872 | tf_op jit(solution)/shard_map/ppermute | solution.py:283
  173.3 12.5 %collective-permute-start.8 = (bf16[256,1024]{1,0:T(8,128)(2,1)S(1)}, bf16[256,1024]{1,0:T(8,128)(2,1)S(1)}, u32[]{:S(2)}, u32[]{:S(2)}) collective-permute-start(bf16[256,1024]{1,0:T(8,128)(2,1)S(1)} %get-tuple-element.64), channel_id=1, source_target_pairs={{0,4},{4,0},{8,12},{12,8},{16,20},{20,16},{24,28},{28,24},{1,5},{5... | collective-permute-start | bytes 1572872 | tf_op jit(solution)/shard_map/ppermute | solution.py:283
  182.6 22.9 %collective-permute-start.30 = (bf16[256,1024]{1,0:T(8,128)(2,1)S(1)}, bf16[256,1024]{1,0:T(8,128)(2,1)S(1)}, u32[]{:S(2)}, u32[]{:S(2)}) collective-permute-start(bf16[256,1024]{1,0:T(8,128)(2,1)S(1)} %add_convert_fusion.1), channel_id=1, source_target_pairs={{0,2},{1,3},{2,0},{3,1},{4,6},{5,7},{6,4},{7,5},{8,10},{9,11},{10,... | collective-permute-start | bytes 1572872 | tf_op jit(solution)/shard_map/ppermute | solution.py:283
  182.8 23.6 %collective-permute-start.19 = (bf16[256,1024]{1,0:T(8,128)(2,1)S(1)}, bf16[256,1024]{1,0:T(8,128)(2,1)S(1)}, u32[]{:S(2)}, u32[]{:S(2)}) collective-permute-start(bf16[256,1024]{1,0:T(8,128)(2,1)S(1)} %add_convert_fusion.2), channel_id=1, source_target_pairs={{0,1},{1,0},{2,3},{3,2},{4,5},{5,4},{6,7},{7,6},{8,9},{9,8},{10,11... | collective-permute-start | bytes 1572872 | tf_op jit(solution)/shard_map/ppermute | solution.py:283
  184.1 43.9 %collective-permute-start.41 = (bf16[256,1024]{1,0:T(8,128)(2,1)S(1)}, bf16[256,1024]{1,0:T(8,128)(2,1)S(1)}, u32[]{:S(2)}, u32[]{:S(2)}) collective-permute-start(bf16[256,1024]{1,0:T(8,128)(2,1)S(1)} %add_convert_fusion), channel_id=1, source_target_pairs={{0,3},{1,2},{2,1},{3,0},{4,7},{5,6},{6,5},{7,4},{8,11},{9,10},{10,... | collective-permute-start | bytes 1572872 | tf_op jit(solution)/shard_map/ppermute | solution.py:283
  (15 other events, 186.1 us)

commit v3 on v2

--- a/solution.py
+++ b/solution.py
@@ -11,8 +11,7 @@
 
 HD = 64
 VMEM = pl.BlockSpec(memory_space=pltpu.VMEM)
-SMEM = pl.BlockSpec(memory_space=pltpu.SMEM)
-LIMIT = pltpu.CompilerParams(vmem_limit_bytes=28 * 2**20)
+LIMIT = pltpu.CompilerParams(vmem_limit_bytes=12 * 2**20)
 
 
 def layer_normed(values):
@@ -29,7 +28,27 @@
 PLACES = 16
 
 
-def mixing_kernel(tokens, taps, qkv, outer, stream, kept, normed, queries, keys, values, mixed):
+def mixing_kernel(
+    tokens, taps_far, qkv_far, outer_far, inner_far, last_far, stream, inner, last, *scratch
+):
+    kept, normed, queries, keys, values, mixed, taps, qkv, outer, arrived = scratch
+    size = tokens.shape[-1]
+    copies = [
+        pltpu.make_async_copy(
+            qkv_far.at[:, part * size : (part + 1) * size],
+            qkv.at[:, part * size : (part + 1) * size],
+            arrived.at[part],
+        )
+        for part in range(3)
+    ]
+    copies.append(pltpu.make_async_copy(outer_far, outer, arrived.at[3]))
+    copies.append(pltpu.make_async_copy(inner_far.at[0], inner, arrived.at[4]))
+    copies.append(pltpu.make_async_copy(last_far.at[0], last, arrived.at[5]))
+    copies.append(pltpu.make_async_copy(taps_far, taps, arrived.at[6]))
+    copies[6].start()
+    for copy in copies[:4]:
+        copy.start()
+    copies[6].wait()
     frames, across, channels = tokens.shape
     blocks = across // PLACES
     rows = frames * PLACES
@@ -59,6 +78,7 @@
     same_head = jnp.where(head_a == head_b, 1.0 / HD, 0.0).astype(bf16)
 
     for target, base in ((queries, 0), (keys, channels)):
+        copies[base // channels].wait()
         for at in range(0, channels, width):
             part = dot(normed[...], qkv[:, base + at : base + at + width])
             square = part * part
@@ -66,6 +86,9 @@
             low = (square - high.astype(jnp.float32)).astype(bf16)
             mean = dot(high, same_head) + dot(low, same_head)
             target[:, at : at + width] = (part / jnp.sqrt(mean + 1e-06)).astype(bf16)
+    copies[2].wait()
+    copies[4].start()
+    copies[5].start()
     for at in range(0, channels, width):
         base = 2 * channels + at
         values[:, at : at + width] = dot(normed[...], qkv[:, base : base + width]).astype(bf16)
@@ -91,35 +114,57 @@
             summed = dot(weights, jnp.concatenate([both, ones], 1))
             mixed[here, at : at + pair] = (summed[:, :pair] / summed[:, pair:]).astype(bf16)
 
+    copies[3].wait()
     attended = dot(mixed[...], outer[...]).astype(bf16).astype(jnp.float32)
     total = (kept[...].astype(jnp.float32) + attended).astype(bf16)
     for frame in range(frames):
         for place, at in spans(frame):
             stream[frame, place : place + PLACES, :] = total[at : at + PLACES, :]
-
-
-def time_mixing(received, conv_weight, qkv_weight, attn_out_weight):
+    copies[4].wait()
+    copies[5].wait()
+
+
+def time_mixing(received, conv_weight, qkv_weight, attn_out_weight, expert_in, expert_out):
     frames, across, channels = received.shape
-    scratch = pltpu.VMEM((frames * across, channels), jnp.bfloat16)
+    bf16 = jnp.bfloat16
+    rows = pltpu.VMEM((frames * across, channels), bf16)
+    far = pl.BlockSpec(memory_space=pltpu.HBM)
     return pl.pallas_call(
         mixing_kernel,
-        out_shape=jax.ShapeDtypeStruct(received.shape, jnp.bfloat16),
-        in_specs=[VMEM] * 4,
-        out_specs=VMEM,
-        scratch_shapes=[scratch] * 6,
-        compiler_params=LIMIT,
+        out_shape=[
+            jax.ShapeDtypeStruct(received.shape, bf16),
+            jax.ShapeDtypeStruct(expert_in.shape[1:], bf16),
+            jax.ShapeDtypeStruct(expert_out.shape[1:], bf16),
+        ],
+        in_specs=[VMEM] + [far] * 5,
+        out_specs=[VMEM] * 3,
+        scratch_shapes=[rows] * 6
+        + [
+            pltpu.VMEM(conv_weight.shape, jnp.float32),
+            pltpu.VMEM(qkv_weight.shape, bf16),
+            pltpu.VMEM(attn_out_weight.shape, bf16),
+            pltpu.SemaphoreType.DMA((7,)),
+        ],
+        compiler_params=pltpu.CompilerParams(vmem_limit_bytes=40 * 2**20),
         name="mixing",
-    )(received, conv_weight, qkv_weight, attn_out_weight)
+    )(
+        received,
+        *(
+            pltpu.with_memory_space_constraint(part, pltpu.HBM)
+            for part in (conv_weight, qkv_weight, attn_out_weight, expert_in, expert_out)
+        ),
+    )
 
 
 def dispatch_kernel(
-    chips, classes, capacity, place, own, other, own_ids, other_ids, router, *outs
+    chips, classes, capacity, own, other, own_ids, other_ids, router, *outs
 ):
     boxes, combs = outs[:chips], outs[chips:]
     tokens = own.shape[0]
     experts = router.shape[0]
     slots = chips * capacity
-    chip, core, mine = place[0], place[1], place[2]
+    at = lax.axis_index("tm")
+    chip, core, mine = at // 2, at % 2, lax.axis_index("group") // 2
     slot = lax.broadcasted_iota(jnp.int32, (slots, tokens), 0)
     target = jnp.bitwise_xor(slot // capacity, chip)
     target = (2 * target + core) * classes + mine
@@ -151,7 +196,7 @@
             ]
 
 
-def dispatched(place, own, other, own_ids, other_ids, router, chips, classes, capacity):
+def dispatched(own, other, own_ids, other_ids, router, chips, classes, capacity):
     tokens, channels = own.shape
     bf16 = jnp.bfloat16
     shapes = [jax.ShapeDtypeStruct((2 * capacity, channels), bf16)] * chips
@@ -159,72 +204,80 @@
     outs = pl.pallas_call(
         functools.partial(dispatch_kernel, chips, classes, capacity),
         out_shape=shapes,
-        in_specs=[SMEM] + [VMEM] * 5,
+        in_specs=[VMEM] * 5,
         out_specs=[VMEM] * (chips + 2),
         compiler_params=LIMIT,
         name="dispatch",
-    )(place, own, other, own_ids, other_ids, router)
+    )(own, other, own_ids, other_ids, router)
     return outs[:chips], outs[chips:]
 
 
 def expert_kernel(chips, *refs):
     inputs, (inner, outer) = refs[:chips], refs[chips : chips + 2]
-    outputs, (gathered, total) = refs[chips + 2 : 2 * chips + 2], refs[2 * chips + 2 :]
-    step, last = pl.program_id(0), pl.num_programs(0) - 1
+    outputs, (gathered, total) = refs[chips + 2 : -2], refs[-2:]
     size = inputs[0].shape[0]
-
-    @pl.when(step == 0)
-    def _():
-        for k in range(chips):
-            gathered[k * size : (k + 1) * size, :] = inputs[k][...]
-
-    hidden = jax.nn.gelu(dot(gathered[...], inner[0])).astype(jnp.bfloat16)
-    part = dot(hidden, outer[0])
-
-    @pl.when(step == 0)
-    def _():
-        total[...] = part
-
-    @pl.when((step > 0) & (step < last))
-    def _():
-        total[...] += part
-
-    @pl.when(step == last)
-    def _():
-        done = (total[...] + part).astype(jnp.bfloat16)
-        for k in range(chips):
-            outputs[k][...] = done[k * size : (k + 1) * size, :]
-
-
-def expert_rows(pieces, expert_in, expert_out):
+    units = inner.shape[1]
+    tile = units // 4
+    for k in range(chips):
+        gathered[k * size : (k + 1) * size, :] = inputs[k][...]
+    for at in range(0, units, tile):
+        hidden = jax.nn.gelu(dot(gathered[...], inner[:, at : at + tile])).astype(jnp.bfloat16)
+        part = dot(hidden, outer[at : at + tile, :])
+        if at == 0:
+            total[...] = part
+        elif at + tile < units:
+            total[...] += part
+        else:
+            done = (total[...] + part).astype(jnp.bfloat16)
+            step = outputs[0].shape[0]
+            for k, out in enumerate(outputs):
+                out[...] = done[k * step : (k + 1) * step, :]
+
+
+def expert_rows(pieces, inner, outer, joined):
     chips = len(pieces)
     size, channels = pieces[0].shape
-    units = expert_in.shape[2]
-    tile = units // 4
-    whole = pl.BlockSpec((size, channels), lambda i: (0, 0))
+    units = inner.shape[1]
     rows = chips * size
+    count = 1 if joined else chips
     return pl.pallas_call(
         functools.partial(expert_kernel, chips),
-        out_shape=[jax.ShapeDtypeStruct((size, channels), jnp.bfloat16)] * chips,
-        grid=(units // tile,),
-        in_specs=[whole] * chips
-        + [
-            pl.BlockSpec((1, channels, tile), lambda i: (0, 0, i)),
-            pl.BlockSpec((1, tile, channels), lambda i: (0, i, 0)),
-        ],
-        out_specs=[whole] * chips,
+        out_shape=[jax.ShapeDtypeStruct((rows // count, channels), jnp.bfloat16)] * count,
+        in_specs=[VMEM] * (chips + 2),
+        out_specs=[VMEM] * count,
         scratch_shapes=[
             pltpu.VMEM((rows, channels), jnp.bfloat16),
             pltpu.VMEM((rows, channels), jnp.float32),
         ],
-        compiler_params=LIMIT,
+        compiler_params=pltpu.CompilerParams(vmem_limit_bytes=20 * 2**20),
         cost_estimate=pl.CostEstimate(
             flops=4 * rows * channels * units,
             transcendentals=rows * units,
             bytes_accessed=4 * channels * units,
         ),
         name="experts",
-    )(*pieces, *(pltpu.with_memory_space_constraint(w, pltpu.HBM) for w in (expert_in, expert_out)))
+    )(*pieces, inner, outer)
+
+
+def pair_kernel(one, two, *outs):
+    size = outs[0].shape[0]
+    for k, out in enumerate(outs):
+        at = slice(k * size, (k + 1) * size)
+        out[...] = (one[at, :].astype(jnp.float32) + two[at, :].astype(jnp.float32)).astype(
+            out.dtype
+        )
+
+
+def pair_summed(one, two, chips):
+    rows, channels = one.shape
+    return pl.pallas_call(
+        pair_kernel,
+        out_shape=[jax.ShapeDtypeStruct((rows // chips, channels), one.dtype)] * chips,
+        in_specs=[VMEM] * 2,
+        out_specs=[VMEM] * chips,
+        compiler_params=LIMIT,
+        name="pair",
+    )(one, two)
 
 
 def combine_kernel(chips, *refs):
@@ -253,6 +306,46 @@
         compiler_params=LIMIT,
         name="combine",
     )(*pieces, *combs)
+
+
+def norm_kernel(rows, out):
+    out[...] = layer_normed(rows[...])
+
+
+def row_normed(rows):
+    return pl.pallas_call(
+        norm_kernel,
+        out_shape=jax.ShapeDtypeStruct(rows.shape, rows.dtype),
+        in_specs=[VMEM],
+        out_specs=VMEM,
+        compiler_params=LIMIT,
+        name="norm",
+    )(rows)
+
+
+def sum_kernel(halves, *refs):
+    whole, (first, second), out = refs[:-1], halves, refs[-1]
+    half = out.shape[0] // 2
+    parts, whole = whole[-(first + second) :], whole[: -(first + second)]
+    for at, group in ((0, parts[:first]), (half, parts[first:])):
+        total = whole[0][at : at + half, :].astype(jnp.float32)
+        for part in whole[1:]:
+            total = total + part[at : at + half, :].astype(jnp.float32)
+        for part in group:
+            total = total + part[...].astype(jnp.float32)
+        out[at : at + half, :] = total.astype(out.dtype)
+
+
+def summed(whole, first, second):
+    rows = [*whole, *first, *second]
+    return pl.pallas_call(
+        functools.partial(sum_kernel, (len(first), len(second))),
+        out_shape=jax.ShapeDtypeStruct(whole[0].shape, whole[0].dtype),
+        in_specs=[VMEM] * len(rows),
+        out_specs=VMEM,
+        compiler_params=LIMIT,
+        name="total",
+    )(*rows)
 
 
 def body(
@@ -273,8 +366,6 @@
     across = spatial // shards
     experts = router_weight.shape[1]
     capacity = 4 * spatial // experts
-    at = lax.axis_index("tm")
-    place = jnp.stack([at // 2, at % 2, lax.axis_index("group") // 2]).astype(jnp.int32)
 
     def swapped(rows, axis, step):
         if step == 0:
@@ -284,7 +375,8 @@
 
     routed = expert_ids.reshape(spatial, 2).T
     pair = jnp.concatenate([routed, swapped(routed, "tm", 1)], 0)
-    ids = [swapped(pair, "group", step) for step in range(groups)]
+    blocked = [step for step in range(groups) if step != 1]
+    ids = {step: swapped(pair, "group", step) for step in blocked}
 
     received = lax.all_to_all(
         tokens.reshape(1, shards, across, channels),
@@ -293,7 +385,9 @@
         concat_axis=0,
         tiled=True,
     ).reshape(shards, across, channels)
-    stream_two = time_mixing(received, conv_weight, qkv_weight, attn_out_weight)
+    stream_two, inner, outer = time_mixing(
+        received, conv_weight, qkv_weight, attn_out_weight, expert_in, expert_out
+    )
     stream = lax.all_to_all(
         stream_two.reshape(shards, 1, across, channels),
         "tm",
@@ -303,19 +397,20 @@
     ).reshape(spatial, channels)
 
     router = router_weight.T
-    normed = layer_normed(stream)
-    blocks = [normed]
-    for step in range(1, groups):
+    normed = row_normed(stream)
+    blocks = {0: normed}
+    for step in blocked[1:]:
         if step % 2:
-            blocks.append(swapped(blocks[step - 1], "group", 1))
+            blocks[step] = swapped(blocks[step - 1], "group", 1)
         else:
-            blocks.append(swapped(normed, "group", step))
-    total = stream.astype(jnp.float32)
-    for step in range(groups):
+            blocks[step] = swapped(normed, "group", step)
+    whole, first, second, waiting = [stream], [], [], None
+    half = spatial // 2
+    bf16 = jnp.bfloat16
+    for step in blocked:
         own = blocks[step]
         other = swapped(own, "tm", 1)
         boxes, combs = dispatched(
-            place,
             own,
             other,
             ids[step][:2],
@@ -326,15 +421,27 @@
             capacity,
         )
         pieces = [swapped(boxes[k], "tm", 2 * k) for k in range(chips)]
-        results = expert_rows(pieces, expert_in, expert_out)
+        results = expert_rows(pieces, inner, outer, step == 0)
+        if step == 0:
+            near = [swapped(pieces[k], "group", 1) for k in range(chips)]
+            others = expert_rows(near, inner, outer, True)
+            others = swapped(others[0], "group", 1)
+            results = pair_summed(results[0], others, chips)
         returned = [swapped(results[k], "tm", 2 * k) for k in range(chips)]
         here, there = combined(returned, combs)
-        mixed = here + swapped(there, "tm", 1).astype(jnp.float32)
-        if step:
-            mixed = swapped(mixed.astype(jnp.bfloat16), "group", step)
-            mixed = mixed.astype(jnp.float32)
-        total = total + mixed
-    return total.astype(jnp.bfloat16).reshape(1, spatial, channels)
+        across_core = swapped(there, "tm", 1)
+        if step == 0:
+            whole += [here, across_core]
+            continue
+        mixed = here + across_core.astype(jnp.float32)
+        first.append(swapped(mixed[:half].astype(bf16), "group", step))
+        if step % 2 == 0:
+            waiting = mixed[half:]
+        else:
+            near = swapped(mixed[half:].astype(bf16), "group", 1)
+            joint = (waiting + near.astype(jnp.float32)).astype(bf16)
+            second.append(swapped(joint, "group", step - 1))
+    return summed(whole, first, second).reshape(1, spatial, channels)
 
 
 def solution(mesh):

time: 231 us -> 209 us (0.905)
  Pallas kernels: 45.8 us -> 35.5 us
  starting transfers between devices: 54.6 us -> 47.2 us
  local copies, waits for them, and re-layouts: 5.27 us -> 0.08 us
    pallas_call x4, Pallas kernels: 31.8 us -> 20.4 us  [expert_rows(): pl.pallas_call(functools.partial(expert_kernel, chips), out_shape=[jax.Sh...]
    ppermute x42 -> x38, starting transfers between devices: 54.6 us -> 47.2 us  [swapped(): return lax.ppermute(rows, axis, [(i, i ^ step) for i in range(size)])]
    unnamed x10 -> x4, local copies, waits for them, and re-layouts: 5.1 us -> 0.01 us
    pallas_call x1 -> x4, Pallas kernels: 6.51 us -> 11.1 us  [the longest x1 9.47 us: time_mixing(): pl.pallas_call(mixing_kernel, out_shape=[jax.ShapeDtypeStruct(received.sh...]
    pallas_call x4 -> x3, Pallas kernels: 5.67 us -> 2.59 us  [dispatched(): pl.pallas_call(functools.partial(dispatch_kernel, chips, classes, capacit...]
    ppermute x42 -> x38, waiting for transfers between devices: 95.9 us -> 97.8 us  [swapped(): return lax.ppermute(rows, axis, [(i, i ^ step) for i in range(size)])]
  transfers between devices with their start and end apart: 42 -> 38, of which waited for: 13 -> 19; matrix products, arithmetic and copies ran while one was open for 0% -> 0% of each run, Pallas kernels for 17% -> 12%
where the time goes in v3:
time: 209 us; the launch traced here: 206 us
  waiting for transfers between devices  97.8 us (47%)
  starting transfers between devices  47.2 us (23%)
  Pallas kernels  35.5 us (17%)
  blocking collectives  25 us (12%)
    ppermute x38, waiting for transfers between devices, swapped(): return lax.ppermute(rows, axis, [(i, i ^ step) for i in range(size)])  97.8 us
    ppermute x38, starting transfers between devices, swapped(): return lax.ppermute(rows, axis, [(i, i ^ step) for i in range(size)])  47.2 us
    pallas_call x4, Pallas kernels, expert_rows(): pl.pallas_call(functools.partial(expert_kernel, chips), out_shape=[jax.Sh...  20.4 us
    all_to_all x1, blocking collectives, body(): lax.all_to_all(tokens.reshape(1, shards, across, channels), 'tm', split_a...  12.9 us
    all_to_all x1, blocking collectives, body(): lax.all_to_all(stream_two.reshape(shards, 1, across, channels), 'tm', spl...  12.1 us
    pallas_call x1, Pallas kernels, time_mixing(): pl.pallas_call(mixing_kernel, out_shape=[jax.ShapeDtypeStruct(received.sh...  9.47 us
  transfers between devices with their start and end apart: 38, of which 19 were waited for; matrix products, arithmetic and copies ran while one was open for 0% of the time, Pallas kernels for 12%

profile of v3, /device:TPU:9, one launch (start us, length us, event | category | flops | bytes accessed | tf_op | source)
XLA Modules:
  0.0 206.0 jit_solution(1293059359725529468)
XLA Ops:
  0.0 12.9 %all_to_all.8 = bf16[1,8,32,1024]{3,2,0,1:T(8,128)(2,1)S(1)} all-to-all(bf16[1,8,32,1024]{3,2,0,1:T(8,128)(2,1)} %bitcast.21), channel_id=1, replica_groups=mesh['tm'=8,'group'=4] {'tm'}, dimensions={1} | all-to-all | bytes 1048576 | tf_op jit(solution)/shard_map/all_to_all | solution.py:381
  12.9 9.5 %mixing.1 = (bf16[8,32,1024]{2,1,0:T(8,128)(2,1)S(1)}, bf16[1024,2048]{1,0:T(8,128)(2,1)S(1)}, bf16[2048,1024]{1,0:T(8,128)(2,1)S(1)}) custom-call(bf16[8,32,1024]{2,1,0:T(8,128)(2,1)S(1)} %bitcast.13, f32[3,1024]{1,0:T(4,128)} %taps_far.1, bf16[1024,3072]{1,0:T(8,128)(2,1)} %qkv_far.1, bf16[1024,1024]{1,0:T(8,128)(2,1)} %outer_far.1, ...), custom_call_target="tpu_custom_call" | custom-call | tf_op jit(solution)/shard_map/mixing/pallas_call | solution.py:132
  22.4 12.1 %all_to_all.9 = bf16[8,1,32,1024]{3,2,1,0:T(8,128)(2,1)S(1)} all-to-all(bf16[8,1,32,1024]{3,2,1,0:T(8,128)(2,1)S(1)} %bitcast.14), channel_id=1, replica_groups=mesh['tm'=8,'group'=4] {'tm'}, dimensions={0} | all-to-all | bytes 1048576 | tf_op jit(solution)/shard_map/all_to_all | solution.py:391
  34.8 2.4 %collective-permute-start.14 = (bf16[256,1024]{1,0:T(8,128)(2,1)S(1)}, bf16[256,1024]{1,0:T(8,128)(2,1)S(1)}, u32[]{:S(2)}, u32[]{:S(2)}) collective-permute-start(bf16[256,1024]{1,0:T(8,128)(2,1)S(1)} %norm.1.own), channel_id=1, source_target_pairs={{0,2},{1,3},{2,0},{3,1},{4,6},{5,7},{6,4},{7,5},{8,10},{9,11},{10,... | collective-permute-start | bytes 1572872 | tf_op jit(solution)/shard_map/ppermute | solution.py:374
  37.2 22.8 %collective-permute-done.14.own = bf16[256,1024]{1,0:T(8,128)(2,1)S(1)} collective-permute-done((bf16[256,1024]{1,0:T(8,128)(2,1)S(1)}, bf16[256,1024]{1,0:T(8,128)(2,1)S(1)}, u32[]{:S(2)}, u32[]{:S(2)}) %collective-permute-start.14) | collective-permute-done | bytes 524320 | tf_op jit(solution)/shard_map/ppermute | solution.py:374
  60.0 1.8 collective-permute-start
  61.8 11.1 %collective-permute-done.25.own = bf16[256,1024]{1,0:T(8,128)(2,1)S(1)} collective-permute-done((bf16[256,1024]{1,0:T(8,128)(2,1)S(1)}, bf16[256,1024]{1,0:T(8,128)(2,1)S(1)}, u32[]{:S(2)}, u32[]{:S(2)}) %collective-permute-start.25) | collective-permute-done | bytes 524320 | tf_op jit(solution)/shard_map/ppermute | solution.py:374
  73.0 1.3 collective-permute-start.26
  74.3 1.5 collective-permute-done.1.other_ids
  77.9 1.6 collective-permute-start.4
  79.5 1.9 collective-permute-start.27
  81.4 1.3 collective-permute-done.27
  82.7 4.1 %collective-permute-start.16 = (s32[4,256]{1,0:T(4,128)S(1)}, s32[4,256]{1,0:T(4,128)S(1)}, u32[]{:S(2)}, u32[]{:S(2)}) collective-permute-start(s32[4,256]{1,0:T(4,128)S(1)} %pad_add_fusion), channel_id=1, source_target_pairs={{0,2},{1,3},{2,0},{3,1},{4,6},{5,7},{6,4},{7,5},{8,10},{9,11},{10,... | collective-permute-start | bytes 12296 | tf_op jit(solution)/shard_map/ppermute | solution.py:374
  86.8 1.3 collective-permute-done.16
  91.1 4.1 %collective-permute-start.15 = (bf16[256,1024]{1,0:T(8,128)(2,1)S(1)}, bf16[256,1024]{1,0:T(8,128)(2,1)S(1)}, u32[]{:S(2)}, u32[]{:S(2)}) collective-permute-start(bf16[256,1024]{1,0:T(8,128)(2,1)S(1)} %collective-permute-done.14.own), channel_id=1, source_target_pairs={{0,4},{4,0},{8,12},{12,8},{16,20},{20,16},{24,28},{28,24},{1,5},{5... | collective-permute-start | bytes 1572872 | tf_op jit(solution)/shard_map/ppermute | solution.py:374
  97.0 1.7 collective-permute-done.6.refs_1_
  98.9 5.3 %collective-permute-done.7.refs_2_ = bf16[128,1024]{1,0:T(8,128)(2,1)S(1)} collective-permute-done((bf16[128,1024]{1,0:T(8,128)(2,1)S(1)}, bf16[128,1024]{1,0:T(8,128)(2,1)S(1)}, u32[]{:S(2)}, u32[]{:S(2)}) %collective-permute-start.7) | collective-permute-done | bytes 262176 | tf_op jit(solution)/shard_map/ppermute | solution.py:374
  105.1 4.8 %collective-permute-done.8.refs_3_ = bf16[128,1024]{1,0:T(8,128)(2,1)S(1)} collective-permute-done((bf16[128,1024]{1,0:T(8,128)(2,1)S(1)}, bf16[128,1024]{1,0:T(8,128)(2,1)S(1)}, u32[]{:S(2)}, u32[]{:S(2)}) %collective-permute-start.8) | collective-permute-done | bytes 262176 | tf_op jit(solution)/shard_map/ppermute | solution.py:374
  109.9 5.0 %experts.5 = bf16[512,1024]{1,0:T(8,128)(2,1)S(1)} custom-call(bf16[128,1024]{1,0:T(8,128)(2,1)S(1)} %collective-permute-done.5.refs_0_, bf16[128,1024]{1,0:T(8,128)(2,1)S(1)} %collective-permute-done.6.refs_1_, bf16[128,1024]{1,0:T(8,128)(2,1)S(1)} %collective-permute-done.7.refs_2_, bf16[128,1024]{1,0:T(8,128)(2,1)S(1)} %collective-permute-done.8.refs_3_, ...), custom_call_target="tpu_custom_call" | custom-call | flops 4294967296 | bytes 8388608 | tf_op jit(solution)/shard_map/experts/pallas_call | solution.py:243
  117.3 1.6 collective-permute-start.19
  118.9 5.3 %experts.7 = (bf16[128,1024]{1,0:T(8,128)(2,1)S(1)}, bf16[128,1024]{1,0:T(8,128)(2,1)S(1)}, bf16[128,1024]{1,0:T(8,128)(2,1)S(1)}, bf16[128,1024]{1,0:T(8,128)(2,1)S(1)}) custom-call(bf16[128,1024]{1,0:T(8,128)(2,1)S(1)} %get-tuple-element.71.refs_0_, bf16[128,1024]{1,0:T(8,128)(2,1)S(1)} %collective-permute-done.28.refs_1_, ...), custom_call_target="tpu_custom_call" | custom-call | flops 4294967296 | bytes 8388608 | tf_op jit(solution)/shard_map/experts/pallas_call | solution.py:243
  126.9 5.0 %experts.6 = (bf16[128,1024]{1,0:T(8,128)(2,1)S(1)}, bf16[128,1024]{1,0:T(8,128)(2,1)S(1)}, bf16[128,1024]{1,0:T(8,128)(2,1)S(1)}, bf16[128,1024]{1,0:T(8,128)(2,1)S(1)}) custom-call(bf16[128,1024]{1,0:T(8,128)(2,1)S(1)} %get-tuple-element.59.refs_0_, bf16[128,1024]{1,0:T(8,128)(2,1)S(1)} %collective-permute-done.17.refs_1_, ...), custom_call_target="tpu_custom_call" | custom-call | flops 4294967296 | bytes 8388608 | tf_op jit(solution)/shard_map/experts/pallas_call | solution.py:243
  133.5 3.2 %collective-permute-done.32.refs_2_ = bf16[128,1024]{1,0:T(8,128)(2,1)S(1)} collective-permute-done((bf16[128,1024]{1,0:T(8,128)(2,1)S(1)}, bf16[128,1024]{1,0:T(8,128)(2,1)S(1)}, u32[]{:S(2)}, u32[]{:S(2)}) %collective-permute-start.32) | collective-permute-done | bytes 262176 | tf_op jit(solution)/shard_map/ppermute | solution.py:374
  138.3 7.4 %collective-permute-start.34 = (bf16[256,1024]{1,0:T(8,128)(2,1)S(1)}, bf16[256,1024]{1,0:T(8,128)(2,1)S(1)}, u32[]{:S(2)}, u32[]{:S(2)}) collective-permute-start(bf16[256,1024]{1,0:T(8,128)(2,1)S(1)} %get-tuple-element.82), channel_id=1, source_target_pairs={{0,4},{4,0},{8,12},{12,8},{16,20},{20,16},{24,28},{28,24},{1,5},{5... | collective-permute-start | bytes 1572872 | tf_op jit(solution)/shard_map/ppermute | solution.py:374
  145.8 5.0 %experts.4.one = bf16[512,1024]{1,0:T(8,128)(2,1)S(1)} custom-call(bf16[128,1024]{1,0:T(8,128)(2,1)S(1)} %get-tuple-element.45.refs_0_, bf16[128,1024]{1,0:T(8,128)(2,1)S(1)} %collective-permute-done.2.refs_1_, bf16[128,1024]{1,0:T(8,128)(2,1)S(1)} %collective-permute-done.3.refs_2_, bf16[128,1024]{1,0:T(8,128)(2,1)S(1)} %collective-permute-done.4.refs_3_, ...), custom_call_target="tpu_custom_call" | custom-call | flops 4294967296 | bytes 8388608 | tf_op jit(solution)/shard_map/experts/pallas_call | solution.py:243
  155.2 3.8 %collective-permute-done.10.refs_1_ = bf16[128,1024]{1,0:T(8,128)(2,1)S(1)} collective-permute-done((bf16[128,1024]{1,0:T(8,128)(2,1)S(1)}, bf16[128,1024]{1,0:T(8,128)(2,1)S(1)}, u32[]{:S(2)}, u32[]{:S(2)}) %collective-permute-start.10) | collective-permute-done | bytes 262176 | tf_op jit(solution)/shard_map/ppermute | solution.py:374
  159.5 6.2 %collective-permute-done.12.refs_3_ = bf16[128,1024]{1,0:T(8,128)(2,1)S(1)} collective-permute-done((bf16[128,1024]{1,0:T(8,128)(2,1)S(1)}, bf16[128,1024]{1,0:T(8,128)(2,1)S(1)}, u32[]{:S(2)}, u32[]{:S(2)}) %collective-permute-start.12) | collective-permute-done | bytes 262176 | tf_op jit(solution)/shard_map/ppermute | solution.py:374
  168.7 2.8 %collective-permute-start.24 = (bf16[128,1024]{1,0:T(8,128)(2,1)S(1)}, bf16[128,1024]{1,0:T(8,128)(2,1)S(1)}, u32[]{:S(2)}, u32[]{:S(2)}) collective-permute-start(bf16[128,1024]{1,0:T(8,128)(2,1)S(1)} %slice.47), channel_id=1, source_target_pairs={{0,2},{1,3},{2,0},{3,1},{4,6},{5,7},{6,4},{7,5},{8,10},{9,11},{10,... | collective-permute-start | bytes 786440 | tf_op jit(solution)/shard_map/ppermute | solution.py:374
  171.5 8.3 %collective-permute-done.36 = bf16[128,1024]{1,0:T(8,128)(2,1)S(1)} collective-permute-done((bf16[128,1024]{1,0:T(8,128)(2,1)S(1)}, bf16[128,1024]{1,0:T(8,128)(2,1)S(1)}, u32[]{:S(2)}, u32[]{:S(2)}) %collective-permute-start.36) | collective-permute-done | bytes 262176 | tf_op jit(solution)/shard_map/ppermute | solution.py:374
  180.7 13.0 %collective-permute-done.24.refs_3_ = bf16[128,1024]{1,0:T(8,128)(2,1)S(1)} collective-permute-done((bf16[128,1024]{1,0:T(8,128)(2,1)S(1)}, bf16[128,1024]{1,0:T(8,128)(2,1)S(1)}, u32[]{:S(2)}, u32[]{:S(2)}) %collective-permute-start.24) | collective-permute-done | bytes 262176 | tf_op jit(solution)/shard_map/ppermute | solution.py:374
  193.7 5.6 %collective-permute-done.35.refs_4_ = bf16[128,1024]{1,0:T(8,128)(2,1)S(1)} collective-permute-done((bf16[128,1024]{1,0:T(8,128)(2,1)S(1)}, bf16[128,1024]{1,0:T(8,128)(2,1)S(1)}, u32[]{:S(2)}, u32[]{:S(2)}) %collective-permute-start.35) | collective-permute-done | bytes 262176 | tf_op jit(solution)/shard_map/ppermute | solution.py:374
  199.3 5.6 %collective-permute-done.37.refs_5_ = bf16[128,1024]{1,0:T(8,128)(2,1)S(1)} collective-permute-done((bf16[128,1024]{1,0:T(8,128)(2,1)S(1)}, bf16[128,1024]{1,0:T(8,128)(2,1)S(1)}, u32[]{:S(2)}, u32[]{:S(2)}) %collective-permute-start.37) | collective-permute-done | bytes 262176 | tf_op jit(solution)/shard_map/ppermute | solution.py:374
  (72 shorter events, 26.4 us)
Async XLA Ops:
  34.8 25.1 %collective-permute-start.14 = (bf16[256,1024]{1,0:T(8,128)(2,1)S(1)}, bf16[256,1024]{1,0:T(8,128)(2,1)S(1)}, u32[]{:S(2)}, u32[]{:S(2)}) collective-permute-start(bf16[256,1024]{1,0:T(8,128)(2,1)S(1)} %norm.1.own), channel_id=1, source_target_pairs={{0,2},{1,3},{2,0},{3,1},{4,6},{5,7},{6,4},{7,5},{8,10},{9,11},{10,... | collective-permute-start | bytes 1572872 | tf_op jit(solution)/shard_map/ppermute | solution.py:374
  60.0 13.0 %collective-permute-start.25 = (bf16[256,1024]{1,0:T(8,128)(2,1)S(1)}, bf16[256,1024]{1,0:T(8,128)(2,1)S(1)}, u32[]{:S(2)}, u32[]{:S(2)}) collective-permute-start(bf16[256,1024]{1,0:T(8,128)(2,1)S(1)} %collective-permute-done.14.own), channel_id=1, source_target_pairs={{0,1},{1,0},{2,3},{3,2},{4,5},{5,4},{6,7},{7,6},{8,9},{9,8},{10,11... | collective-permute-start | bytes 1572872 | tf_op jit(solution)/shard_map/ppermute | solution.py:374
  60.0 15.8 %collective-permute-start = (bf16[256,1024]{1,0:T(8,128)(2,1)S(1)}, bf16[256,1024]{1,0:T(8,128)(2,1)S(1)}, u32[]{:S(2)}, u32[]{:S(2)}) collective-permute-start(bf16[256,1024]{1,0:T(8,128)(2,1)S(1)} %norm.1.own), channel_id=1, source_target_pairs={{0,4},{4,0},{8,12},{12,8},{16,20},{20,16},{24,28},{28,24},{1,5},{5... | collective-permute-start | bytes 1572872 | tf_op jit(solution)/shard_map/ppermute | solution.py:374
  73.0 18.1 %collective-permute-start.26 = (bf16[256,1024]{1,0:T(8,128)(2,1)S(1)}, bf16[256,1024]{1,0:T(8,128)(2,1)S(1)}, u32[]{:S(2)}, u32[]{:S(2)}) collective-permute-start(bf16[256,1024]{1,0:T(8,128)(2,1)S(1)} %collective-permute-done.25.own), channel_id=1, source_target_pairs={{0,4},{4,0},{8,12},{12,8},{16,20},{20,16},{24,28},{28,24},{1,5},{5... | collective-permute-start | bytes 1572872 | tf_op jit(solution)/shard_map/ppermute | solution.py:374
  76.7 11.7 %collective-permute-start.2 = (bf16[128,1024]{1,0:T(8,128)(2,1)S(1)}, bf16[128,1024]{1,0:T(8,128)(2,1)S(1)}, u32[]{:S(2)}, u32[]{:S(2)}) collective-permute-start(bf16[128,1024]{1,0:T(8,128)(2,1)S(1)} %get-tuple-element.46), channel_id=1, source_target_pairs={{0,8},{4,12},{8,0},{12,4},{16,24},{20,28},{24,16},{28,20},{1,9},{5... | collective-permute-start | bytes 786440 | tf_op jit(solution)/shard_map/ppermute | solution.py:374
  77.7 11.9 %collective-permute-start.3 = (bf16[128,1024]{1,0:T(8,128)(2,1)S(1)}, bf16[128,1024]{1,0:T(8,128)(2,1)S(1)}, u32[]{:S(2)}, u32[]{:S(2)}) collective-permute-start(bf16[128,1024]{1,0:T(8,128)(2,1)S(1)} %get-tuple-element.47), channel_id=1, source_target_pairs={{0,16},{4,20},{8,24},{12,28},{16,0},{20,4},{24,8},{28,12},{1,17},{... | collective-permute-start | bytes 786440 | tf_op jit(solution)/shard_map/ppermute | solution.py:374
  77.9 12.0 %collective-permute-start.4 = (bf16[128,1024]{1,0:T(8,128)(2,1)S(1)}, bf16[128,1024]{1,0:T(8,128)(2,1)S(1)}, u32[]{:S(2)}, u32[]{:S(2)}) collective-permute-start(bf16[128,1024]{1,0:T(8,128)(2,1)S(1)} %get-tuple-element.48), channel_id=1, source_target_pairs={{0,24},{4,28},{8,16},{12,20},{16,8},{20,12},{24,0},{28,4},{1,25},{... | collective-permute-start | bytes 786440 | tf_op jit(solution)/shard_map/ppermute | solution.py:374
  88.4 10.3 %collective-permute-start.6 = (bf16[128,1024]{1,0:T(8,128)(2,1)S(1)}, bf16[128,1024]{1,0:T(8,128)(2,1)S(1)}, u32[]{:S(2)}, u32[]{:S(2)}) collective-permute-start(bf16[128,1024]{1,0:T(8,128)(2,1)S(1)} %collective-permute-done.2.refs_1_), channel_id=1, source_target_pairs={{0,1},{1,0},{2,3},{3,2},{4,5},{5,4},{6,7},{7,6},{8,9},{9,8},{10,11... | collective-permute-start | bytes 786440 | tf_op jit(solution)/shard_map/ppermute | solution.py:374
  89.6 14.7 %collective-permute-start.7 = (bf16[128,1024]{1,0:T(8,128)(2,1)S(1)}, bf16[128,1024]{1,0:T(8,128)(2,1)S(1)}, u32[]{:S(2)}, u32[]{:S(2)}) collective-permute-start(bf16[128,1024]{1,0:T(8,128)(2,1)S(1)} %collective-permute-done.3.refs_2_), channel_id=1, source_target_pairs={{0,1},{1,0},{2,3},{3,2},{4,5},{5,4},{6,7},{7,6},{8,9},{9,8},{10,11... | collective-permute-start | bytes 786440 | tf_op jit(solution)/shard_map/ppermute | solution.py:374
  89.9 19.9 %collective-permute-start.8 = (bf16[128,1024]{1,0:T(8,128)(2,1)S(1)}, bf16[128,1024]{1,0:T(8,128)(2,1)S(1)}, u32[]{:S(2)}, u32[]{:S(2)}) collective-permute-start(bf16[128,1024]{1,0:T(8,128)(2,1)S(1)} %collective-permute-done.4.refs_3_), channel_id=1, source_target_pairs={{0,1},{1,0},{2,3},{3,2},{4,5},{5,4},{6,7},{7,6},{8,9},{9,8},{10,11... | collective-permute-start | bytes 786440 | tf_op jit(solution)/shard_map/ppermute | solution.py:374
  91.1 24.2 %collective-permute-start.15 = (bf16[256,1024]{1,0:T(8,128)(2,1)S(1)}, bf16[256,1024]{1,0:T(8,128)(2,1)S(1)}, u32[]{:S(2)}, u32[]{:S(2)}) collective-permute-start(bf16[256,1024]{1,0:T(8,128)(2,1)S(1)} %collective-permute-done.14.own), channel_id=1, source_target_pairs={{0,4},{4,0},{8,12},{12,8},{16,20},{20,16},{24,28},{28,24},{1,5},{5... | collective-permute-start | bytes 1572872 | tf_op jit(solution)/shard_map/ppermute | solution.py:374
  96.0 21.1 %collective-permute-start.28 = (bf16[128,1024]{1,0:T(8,128)(2,1)S(1)}, bf16[128,1024]{1,0:T(8,128)(2,1)S(1)}, u32[]{:S(2)}, u32[]{:S(2)}) collective-permute-start(bf16[128,1024]{1,0:T(8,128)(2,1)S(1)} %get-tuple-element.72), channel_id=1, source_target_pairs={{0,8},{4,12},{8,0},{12,4},{16,24},{20,28},{24,16},{28,20},{1,9},{5... | collective-permute-start | bytes 786440 | tf_op jit(solution)/shard_map/ppermute | solution.py:374
  98.7 18.7 %collective-permute-start.29 = (bf16[128,1024]{1,0:T(8,128)(2,1)S(1)}, bf16[128,1024]{1,0:T(8,128)(2,1)S(1)}, u32[]{:S(2)}, u32[]{:S(2)}) collective-permute-start(bf16[128,1024]{1,0:T(8,128)(2,1)S(1)} %get-tuple-element.73), channel_id=1, source_target_pairs={{0,16},{4,20},{8,24},{12,28},{16,0},{20,4},{24,8},{28,12},{1,17},{... | collective-permute-start | bytes 786440 | tf_op jit(solution)/shard_map/ppermute | solution.py:374
  104.3 14.6 %collective-permute-start.30 = (bf16[128,1024]{1,0:T(8,128)(2,1)S(1)}, bf16[128,1024]{1,0:T(8,128)(2,1)S(1)}, u32[]{:S(2)}, u32[]{:S(2)}) collective-permute-start(bf16[128,1024]{1,0:T(8,128)(2,1)S(1)} %get-tuple-element.74), channel_id=1, source_target_pairs={{0,24},{4,28},{8,16},{12,20},{16,8},{20,12},{24,0},{28,4},{1,25},{... | collective-permute-start | bytes 786440 | tf_op jit(solution)/shard_map/ppermute | solution.py:374
  114.9 35.9 %collective-permute-start.9 = (bf16[512,1024]{1,0:T(8,128)(2,1)S(1)}, bf16[512,1024]{1,0:T(8,128)(2,1)S(1)}, u32[]{:S(2)}, u32[]{:S(2)}) collective-permute-start(bf16[512,1024]{1,0:T(8,128)(2,1)S(1)} %experts.5), channel_id=1, source_target_pairs={{0,1},{1,0},{2,3},{3,2},{4,5},{5,4},{6,7},{7,6},{8,9},{9,8},{10,11... | collective-permute-start | bytes 3145736 | tf_op jit(solution)/shard_map/ppermute | solution.py:374
  116.2 9.0 %collective-permute-start.17 = (bf16[128,1024]{1,0:T(8,128)(2,1)S(1)}, bf16[128,1024]{1,0:T(8,128)(2,1)S(1)}, u32[]{:S(2)}, u32[]{:S(2)}) collective-permute-start(bf16[128,1024]{1,0:T(8,128)(2,1)S(1)} %get-tuple-element.60), channel_id=1, source_target_pairs={{0,8},{4,12},{8,0},{12,4},{16,24},{20,28},{24,16},{28,20},{1,9},{5... | collective-permute-start | bytes 786440 | tf_op jit(solution)/shard_map/ppermute | solution.py:374
  117.1 8.6 %collective-permute-start.18 = (bf16[128,1024]{1,0:T(8,128)(2,1)S(1)}, bf16[128,1024]{1,0:T(8,128)(2,1)S(1)}, u32[]{:S(2)}, u32[]{:S(2)}) collective-permute-start(bf16[128,1024]{1,0:T(8,128)(2,1)S(1)} %get-tuple-element.61), channel_id=1, source_target_pairs={{0,16},{4,20},{8,24},{12,28},{16,0},{20,4},{24,8},{28,12},{1,17},{... | collective-permute-start | bytes 786440 | tf_op jit(solution)/shard_map/ppermute | solution.py:374
  117.3 9.6 %collective-permute-start.19 = (bf16[128,1024]{1,0:T(8,128)(2,1)S(1)}, bf16[128,1024]{1,0:T(8,128)(2,1)S(1)}, u32[]{:S(2)}, u32[]{:S(2)}) collective-permute-start(bf16[128,1024]{1,0:T(8,128)(2,1)S(1)} %get-tuple-element.62), channel_id=1, source_target_pairs={{0,24},{4,28},{8,16},{12,20},{16,8},{20,12},{24,0},{28,4},{1,25},{... | collective-permute-start | bytes 786440 | tf_op jit(solution)/shard_map/ppermute | solution.py:374
  124.2 8.7 %collective-permute-start.31 = (bf16[128,1024]{1,0:T(8,128)(2,1)S(1)}, bf16[128,1024]{1,0:T(8,128)(2,1)S(1)}, u32[]{:S(2)}, u32[]{:S(2)}) collective-permute-start(bf16[128,1024]{1,0:T(8,128)(2,1)S(1)} %get-tuple-element.76), channel_id=1, source_target_pairs={{0,8},{4,12},{8,0},{12,4},{16,24},{20,28},{24,16},{28,20},{1,9},{5... | collective-permute-start | bytes 786440 | tf_op jit(solution)/shard_map/ppermute | solution.py:374
  125.1 11.6 %collective-permute-start.32 = (bf16[128,1024]{1,0:T(8,128)(2,1)S(1)}, bf16[128,1024]{1,0:T(8,128)(2,1)S(1)}, u32[]{:S(2)}, u32[]{:S(2)}) collective-permute-start(bf16[128,1024]{1,0:T(8,128)(2,1)S(1)} %get-tuple-element.77), channel_id=1, source_target_pairs={{0,16},{4,20},{8,24},{12,28},{16,0},{20,4},{24,8},{28,12},{1,17},{... | collective-permute-start | bytes 786440 | tf_op jit(solution)/shard_map/ppermute | solution.py:374
  125.7 12.2 %collective-permute-start.33 = (bf16[128,1024]{1,0:T(8,128)(2,1)S(1)}, bf16[128,1024]{1,0:T(8,128)(2,1)S(1)}, u32[]{:S(2)}, u32[]{:S(2)}) collective-permute-start(bf16[128,1024]{1,0:T(8,128)(2,1)S(1)} %get-tuple-element.78), channel_id=1, source_target_pairs={{0,24},{4,28},{8,16},{12,20},{16,8},{20,12},{24,0},{28,4},{1,25},{... | collective-permute-start | bytes 786440 | tf_op jit(solution)/shard_map/ppermute | solution.py:374
  131.9 20.0 %collective-permute-start.20 = (bf16[128,1024]{1,0:T(8,128)(2,1)S(1)}, bf16[128,1024]{1,0:T(8,128)(2,1)S(1)}, u32[]{:S(2)}, u32[]{:S(2)}) collective-permute-start(bf16[128,1024]{1,0:T(8,128)(2,1)S(1)} %get-tuple-element.64), channel_id=1, source_target_pairs={{0,8},{4,12},{8,0},{12,4},{16,24},{20,28},{24,16},{28,20},{1,9},{5... | collective-permute-start | bytes 786440 | tf_op jit(solution)/shard_map/ppermute | solution.py:374
  132.9 20.2 %collective-permute-start.21 = (bf16[128,1024]{1,0:T(8,128)(2,1)S(1)}, bf16[128,1024]{1,0:T(8,128)(2,1)S(1)}, u32[]{:S(2)}, u32[]{:S(2)}) collective-permute-start(bf16[128,1024]{1,0:T(8,128)(2,1)S(1)} %get-tuple-element.65), channel_id=1, source_target_pairs={{0,16},{4,20},{8,24},{12,28},{16,0},{20,4},{24,8},{28,12},{1,17},{... | collective-permute-start | bytes 786440 | tf_op jit(solution)/shard_map/ppermute | solution.py:374
  136.7 17.1 %collective-permute-start.22 = (bf16[128,1024]{1,0:T(8,128)(2,1)S(1)}, bf16[128,1024]{1,0:T(8,128)(2,1)S(1)}, u32[]{:S(2)}, u32[]{:S(2)}) collective-permute-start(bf16[128,1024]{1,0:T(8,128)(2,1)S(1)} %get-tuple-element.66), channel_id=1, source_target_pairs={{0,24},{4,28},{8,16},{12,20},{16,8},{20,12},{24,0},{28,4},{1,25},{... | collective-permute-start | bytes 786440 | tf_op jit(solution)/shard_map/ppermute | solution.py:374
  138.3 28.7 %collective-permute-start.34 = (bf16[256,1024]{1,0:T(8,128)(2,1)S(1)}, bf16[256,1024]{1,0:T(8,128)(2,1)S(1)}, u32[]{:S(2)}, u32[]{:S(2)}) collective-permute-start(bf16[256,1024]{1,0:T(8,128)(2,1)S(1)} %get-tuple-element.82), channel_id=1, source_target_pairs={{0,4},{4,0},{8,12},{12,8},{16,20},{20,16},{24,28},{28,24},{1,5},{5... | collective-permute-start | bytes 1572872 | tf_op jit(solution)/shard_map/ppermute | solution.py:374
  153.1 12.5 %collective-permute-start.12 = (bf16[128,1024]{1,0:T(8,128)(2,1)S(1)}, bf16[128,1024]{1,0:T(8,128)(2,1)S(1)}, u32[]{:S(2)}, u32[]{:S(2)}) collective-permute-start(bf16[128,1024]{1,0:T(8,128)(2,1)S(1)} %get-tuple-element.54), channel_id=1, source_target_pairs={{0,24},{4,28},{8,16},{12,20},{16,8},{20,12},{24,0},{28,4},{1,25},{... | collective-permute-start | bytes 786440 | tf_op jit(solution)/shard_map/ppermute | solution.py:374
  154.3 14.2 %collective-permute-start.23 = (bf16[256,1024]{1,0:T(8,128)(2,1)S(1)}, bf16[256,1024]{1,0:T(8,128)(2,1)S(1)}, u32[]{:S(2)}, u32[]{:S(2)}) collective-permute-start(bf16[256,1024]{1,0:T(8,128)(2,1)S(1)} %get-tuple-element.70), channel_id=1, source_target_pairs={{0,4},{4,0},{8,12},{12,8},{16,20},{20,16},{24,28},{28,24},{1,5},{5... | collective-permute-start | bytes 1572872 | tf_op jit(solution)/shard_map/ppermute | solution.py:374
  166.1 27.6 %collective-permute-start.13 = (bf16[256,1024]{1,0:T(8,128)(2,1)S(1)}, bf16[256,1024]{1,0:T(8,128)(2,1)S(1)}, u32[]{:S(2)}, u32[]{:S(2)}) collective-permute-start(bf16[256,1024]{1,0:T(8,128)(2,1)S(1)} %get-tuple-element.58), channel_id=1, source_target_pairs={{0,4},{4,0},{8,12},{12,8},{16,20},{20,16},{24,28},{28,24},{1,5},{5... | collective-permute-start | bytes 1572872 | tf_op jit(solution)/shard_map/ppermute | solution.py:374
  167.2 12.5 %collective-permute-start.36 = (bf16[128,1024]{1,0:T(8,128)(2,1)S(1)}, bf16[128,1024]{1,0:T(8,128)(2,1)S(1)}, u32[]{:S(2)}, u32[]{:S(2)}) collective-permute-start(bf16[128,1024]{1,0:T(8,128)(2,1)S(1)} %get-tuple-element.83), channel_id=1, source_target_pairs={{0,1},{1,0},{2,3},{3,2},{4,5},{5,4},{6,7},{7,6},{8,9},{9,8},{10,11... | collective-permute-start | bytes 786440 | tf_op jit(solution)/shard_map/ppermute | solution.py:374
  168.7 25.0 %collective-permute-start.24 = (bf16[128,1024]{1,0:T(8,128)(2,1)S(1)}, bf16[128,1024]{1,0:T(8,128)(2,1)S(1)}, u32[]{:S(2)}, u32[]{:S(2)}) collective-permute-start(bf16[128,1024]{1,0:T(8,128)(2,1)S(1)} %slice.47), channel_id=1, source_target_pairs={{0,2},{1,3},{2,0},{3,1},{4,6},{5,7},{6,4},{7,5},{8,10},{9,11},{10,... | collective-permute-start | bytes 786440 | tf_op jit(solution)/shard_map/ppermute | solution.py:374
  171.5 27.9 %collective-permute-start.35 = (bf16[128,1024]{1,0:T(8,128)(2,1)S(1)}, bf16[128,1024]{1,0:T(8,128)(2,1)S(1)}, u32[]{:S(2)}, u32[]{:S(2)}) collective-permute-start(bf16[128,1024]{1,0:T(8,128)(2,1)S(1)} %get-tuple-element.84), channel_id=1, source_target_pairs={{0,3},{1,2},{2,1},{3,0},{4,7},{5,6},{6,5},{7,4},{8,11},{9,10},{10,... | collective-permute-start | bytes 786440 | tf_op jit(solution)/shard_map/ppermute | solution.py:374
  179.8 25.1 %collective-permute-start.37 = (bf16[128,1024]{1,0:T(8,128)(2,1)S(1)}, bf16[128,1024]{1,0:T(8,128)(2,1)S(1)}, u32[]{:S(2)}, u32[]{:S(2)}) collective-permute-start(bf16[128,1024]{1,0:T(8,128)(2,1)S(1)} %fusion), channel_id=1, source_target_pairs={{0,2},{1,3},{2,0},{3,1},{4,6},{5,7},{6,4},{7,5},{8,10},{9,11},{10,... | collective-permute-start | bytes 786440 | tf_op jit(solution)/shard_map/ppermute | solution.py:374
  (8 other events, 158.0 us)

commit v4 on v3

--- a/solution.py
+++ b/solution.py
@@ -29,9 +29,10 @@
 
 
 def mixing_kernel(
-    tokens, taps_far, qkv_far, outer_far, inner_far, last_far, stream, inner, last, *scratch
+    tokens, taps, outer, qkv_far, *refs
 ):
-    kept, normed, queries, keys, values, mixed, taps, qkv, outer, arrived = scratch
+    pieces = refs[:-8]
+    kept, normed, queries, keys, values, mixed, qkv, arrived = refs[-8:]
     size = tokens.shape[-1]
     copies = [
         pltpu.make_async_copy(
@@ -41,14 +42,7 @@
         )
         for part in range(3)
     ]
-    copies.append(pltpu.make_async_copy(outer_far, outer, arrived.at[3]))
-    copies.append(pltpu.make_async_copy(inner_far.at[0], inner, arrived.at[4]))
-    copies.append(pltpu.make_async_copy(last_far.at[0], last, arrived.at[5]))
-    copies.append(pltpu.make_async_copy(taps_far, taps, arrived.at[6]))
-    copies[6].start()
-    for copy in copies[:4]:
-        copy.start()
-    copies[6].wait()
+    copies[0].start()
     frames, across, channels = tokens.shape
     blocks = across // PLACES
     rows = frames * PLACES
@@ -72,6 +66,8 @@
             kept[at : at + PLACES, :] = stream_one[place : place + PLACES, :]
             normed[at : at + PLACES, :] = unit[place : place + PLACES, :]
 
+    copies[1].start()
+    copies[2].start()
     width = 256
     head_a = lax.broadcasted_iota(jnp.int32, (width, width), 0) // HD
     head_b = lax.broadcasted_iota(jnp.int32, (width, width), 1) // HD
@@ -87,8 +83,6 @@
             mean = dot(high, same_head) + dot(low, same_head)
             target[:, at : at + width] = (part / jnp.sqrt(mean + 1e-06)).astype(bf16)
     copies[2].wait()
-    copies[4].start()
-    copies[5].start()
     for at in range(0, channels, width):
         base = 2 * channels + at
         values[:, at : at + width] = dot(normed[...], qkv[:, base : base + width]).astype(bf16)
@@ -114,53 +108,69 @@
             summed = dot(weights, jnp.concatenate([both, ones], 1))
             mixed[here, at : at + pair] = (summed[:, :pair] / summed[:, pair:]).astype(bf16)
 
-    copies[3].wait()
     attended = dot(mixed[...], outer[...]).astype(bf16).astype(jnp.float32)
-    total = (kept[...].astype(jnp.float32) + attended).astype(bf16)
-    for frame in range(frames):
-        for place, at in spans(frame):
-            stream[frame, place : place + PLACES, :] = total[at : at + PLACES, :]
-    copies[4].wait()
-    copies[5].wait()
-
-
-def time_mixing(received, conv_weight, qkv_weight, attn_out_weight, expert_in, expert_out):
+    kept[...] = (kept[...].astype(jnp.float32) + attended).astype(bf16)
+    chip = lax.axis_index("tm") // 2
+    for k, piece in enumerate(pieces):
+        for side in range(2):
+            frame = 2 * jnp.bitwise_xor(chip, k) + side
+            for block in range(blocks):
+                at = pl.multiple_of(block * rows + frame * PLACES, PLACES)
+                to = side * across + block * PLACES
+                piece[to : to + PLACES, :] = kept[pl.ds(at, PLACES), :]
+
+
+def fetch_kernel(count, *refs):
+    arrived = refs[-1]
+    copies = [
+        pltpu.make_async_copy(refs[at], refs[count + at], arrived.at[at]) for at in range(count)
+    ]
+    for copy in copies:
+        copy.start()
+    for copy in copies:
+        copy.wait()
+
+
+def fetched(*parts):
+    return pl.pallas_call(
+        functools.partial(fetch_kernel, len(parts)),
+        out_shape=[jax.ShapeDtypeStruct(part.shape, part.dtype) for part in parts],
+        in_specs=[pl.BlockSpec(memory_space=pltpu.HBM)] * len(parts),
+        out_specs=[VMEM] * len(parts),
+        scratch_shapes=[pltpu.SemaphoreType.DMA((len(parts),))],
+        compiler_params=pltpu.CompilerParams(vmem_limit_bytes=2**20),
+        name="fetch",
+    )(*(pltpu.with_memory_space_constraint(part, pltpu.HBM) for part in parts))
+
+
+def time_mixing(received, conv_weight, qkv_weight, attn_out_weight):
     frames, across, channels = received.shape
     bf16 = jnp.bfloat16
     rows = pltpu.VMEM((frames * across, channels), bf16)
     far = pl.BlockSpec(memory_space=pltpu.HBM)
     return pl.pallas_call(
         mixing_kernel,
-        out_shape=[
-            jax.ShapeDtypeStruct(received.shape, bf16),
-            jax.ShapeDtypeStruct(expert_in.shape[1:], bf16),
-            jax.ShapeDtypeStruct(expert_out.shape[1:], bf16),
-        ],
-        in_specs=[VMEM] + [far] * 5,
-        out_specs=[VMEM] * 3,
+        out_shape=[jax.ShapeDtypeStruct((2 * across, channels), bf16)] * (frames // 2),
+        in_specs=[VMEM] * 3 + [far],
+        out_specs=[VMEM] * (frames // 2),
         scratch_shapes=[rows] * 6
-        + [
-            pltpu.VMEM(conv_weight.shape, jnp.float32),
-            pltpu.VMEM(qkv_weight.shape, bf16),
-            pltpu.VMEM(attn_out_weight.shape, bf16),
-            pltpu.SemaphoreType.DMA((7,)),
-        ],
-        compiler_params=pltpu.CompilerParams(vmem_limit_bytes=40 * 2**20),
+        + [pltpu.VMEM(qkv_weight.shape, bf16), pltpu.SemaphoreType.DMA((3,))],
+        compiler_params=pltpu.CompilerParams(vmem_limit_bytes=28 * 2**20),
         name="mixing",
     )(
         received,
-        *(
-            pltpu.with_memory_space_constraint(part, pltpu.HBM)
-            for part in (conv_weight, qkv_weight, attn_out_weight, expert_in, expert_out)
-        ),
+        conv_weight,
+        attn_out_weight,
+        pltpu.with_memory_space_constraint(qkv_weight, pltpu.HBM),
     )
 
 
 def dispatch_kernel(
-    chips, classes, capacity, own, other, own_ids, other_ids, router, *outs
+    chips, classes, capacity, parts, own_ids, other_ids, router, *refs
 ):
+    own, other, outs = refs[:parts], refs[parts : 2 * parts], refs[2 * parts :]
     boxes, combs = outs[:chips], outs[chips:]
-    tokens = own.shape[0]
+    tokens = own_ids.shape[1]
     experts = router.shape[0]
     slots = chips * capacity
     at = lax.axis_index("tm")
@@ -173,9 +183,10 @@
     after = lax.broadcasted_iota(jnp.int32, (tokens, tokens), 1)
     earlier = (before < after).astype(jnp.float32).astype(jnp.bfloat16)
     kinds = lax.broadcasted_iota(jnp.int32, (experts, tokens), 0)
-    for side, (rows, ids) in enumerate(((own, own_ids), (other, other_ids))):
+    for side, (pieces, ids) in enumerate(((own, own_ids), (other, other_ids))):
+        rows = jnp.concatenate([piece[...] for piece in pieces], 0)
         first, second = ids[0:1, :], ids[1:2, :]
-        logits = dot(router[...], rows[...], ((1,), (1,)))
+        logits = dot(router[...], rows, ((1,), (1,)))
         gate_a = jax.nn.sigmoid(
             jnp.sum(jnp.where(kinds == first, logits, 0.0), 0, keepdims=True)
         )
@@ -189,7 +200,7 @@
         taken = jnp.where(rank == order.astype(jnp.float32), member, 0.0)
         share = jnp.where(hit_a, gate_a / whole, gate_b / whole)
         combs[side][...] = (taken * share).astype(jnp.bfloat16)
-        moved = dot(taken.astype(jnp.bfloat16), rows[...]).astype(jnp.bfloat16)
+        moved = dot(taken.astype(jnp.bfloat16), rows).astype(jnp.bfloat16)
         for k in range(chips):
             boxes[k][side * capacity : (side + 1) * capacity, :] = moved[
                 k * capacity : (k + 1) * capacity, :
@@ -197,18 +208,18 @@
 
 
 def dispatched(own, other, own_ids, other_ids, router, chips, classes, capacity):
-    tokens, channels = own.shape
+    tokens, channels = own_ids.shape[1], own[0].shape[1]
     bf16 = jnp.bfloat16
     shapes = [jax.ShapeDtypeStruct((2 * capacity, channels), bf16)] * chips
     shapes += [jax.ShapeDtypeStruct((chips * capacity, tokens), bf16)] * 2
     outs = pl.pallas_call(
-        functools.partial(dispatch_kernel, chips, classes, capacity),
+        functools.partial(dispatch_kernel, chips, classes, capacity, len(own)),
         out_shape=shapes,
-        in_specs=[VMEM] * 5,
+        in_specs=[VMEM] * (3 + 2 * len(own)),
         out_specs=[VMEM] * (chips + 2),
         compiler_params=LIMIT,
         name="dispatch",
-    )(own, other, own_ids, other_ids, router)
+    )(own_ids, other_ids, router, *own, *other)
     return outs[:chips], outs[chips:]
 
 
@@ -259,22 +270,21 @@
     )(*pieces, inner, outer)
 
 
-def pair_kernel(one, two, *outs):
+def pair_kernel(first, one, two, *outs):
     size = outs[0].shape[0]
     for k, out in enumerate(outs):
-        at = slice(k * size, (k + 1) * size)
-        out[...] = (one[at, :].astype(jnp.float32) + two[at, :].astype(jnp.float32)).astype(
-            out.dtype
-        )
-
-
-def pair_summed(one, two, chips):
-    rows, channels = one.shape
-    return pl.pallas_call(
-        pair_kernel,
-        out_shape=[jax.ShapeDtypeStruct((rows // chips, channels), one.dtype)] * chips,
+        both = one[(first + k) * size : (first + k + 1) * size, :].astype(jnp.float32)
+        both = both + two[k * size : (k + 1) * size, :].astype(jnp.float32)
+        out[...] = both.astype(out.dtype)
+
+
+def pair_summed(one, two, first, count):
+    rows, channels = two.shape
+    return pl.pallas_call(
+        functools.partial(pair_kernel, first),
+        out_shape=[jax.ShapeDtypeStruct((rows // count, channels), one.dtype)] * count,
         in_specs=[VMEM] * 2,
-        out_specs=[VMEM] * chips,
+        out_specs=[VMEM] * count,
         compiler_params=LIMIT,
         name="pair",
     )(one, two)
@@ -308,19 +318,33 @@
     )(*pieces, *combs)
 
 
-def norm_kernel(rows, out):
-    out[...] = layer_normed(rows[...])
-
-
-def row_normed(rows):
-    return pl.pallas_call(
-        norm_kernel,
-        out_shape=jax.ShapeDtypeStruct(rows.shape, rows.dtype),
-        in_specs=[VMEM],
-        out_specs=VMEM,
+def norm_kernel(chips, *refs):
+    sides, (stream, own, other) = (refs[:chips], refs[chips : 2 * chips]), refs[2 * chips :]
+    at = lax.axis_index("tm")
+    chip, core = at // 2, at % 2
+    across = refs[0].shape[0] // 2
+    for k in range(chips):
+        for far, pieces in enumerate(sides):
+            block = 2 * jnp.bitwise_xor(chip, k) + (1 - core if far else core)
+            to = pl.ds(pl.multiple_of(block * across, across), across)
+            rows = pieces[k][pl.ds(pl.multiple_of(core * across, across), across), :]
+            stream[to, :] = rows
+            own[to, :] = layer_normed(rows)
+            rows = pieces[k][pl.ds(pl.multiple_of((1 - core) * across, across), across), :]
+            other[to, :] = layer_normed(rows)
+
+
+def rows_normed(mine, theirs):
+    chips = len(mine)
+    size, channels = mine[0].shape
+    return pl.pallas_call(
+        functools.partial(norm_kernel, chips),
+        out_shape=[jax.ShapeDtypeStruct((chips * size, channels), mine[0].dtype)] * 3,
+        in_specs=[VMEM] * (2 * chips),
+        out_specs=[VMEM] * 3,
         compiler_params=LIMIT,
         name="norm",
-    )(rows)
+    )(*mine, *theirs)
 
 
 def sum_kernel(halves, *refs):
@@ -385,31 +409,25 @@
         concat_axis=0,
         tiled=True,
     ).reshape(shards, across, channels)
-    stream_two, inner, outer = time_mixing(
-        received, conv_weight, qkv_weight, attn_out_weight, expert_in, expert_out
-    )
-    stream = lax.all_to_all(
-        stream_two.reshape(shards, 1, across, channels),
-        "tm",
-        split_axis=0,
-        concat_axis=1,
-        tiled=True,
-    ).reshape(spatial, channels)
+    conv_weight, attn_out_weight = fetched(conv_weight, attn_out_weight)
+    pieces = time_mixing(received, conv_weight, qkv_weight, attn_out_weight)
+    inner, outer = fetched(expert_in[0], expert_out[0])
+    mine = [swapped(pieces[k], "tm", 2 * k) for k in range(chips)]
+    theirs = [swapped(mine[k], "tm", 1) for k in range(chips)]
+    stream, normed, beside = rows_normed(mine, theirs)
 
     router = router_weight.T
-    normed = row_normed(stream)
-    blocks = {0: normed}
+    blocks = {0: (normed,)}
     for step in blocked[1:]:
-        if step % 2:
-            blocks[step] = swapped(blocks[step - 1], "group", 1)
-        else:
-            blocks[step] = swapped(normed, "group", step)
+        sources = blocks[step - 1] if step % 2 else blocks[0]
+        blocks[step] = tuple(swapped(rows, "group", 1 if step % 2 else step) for rows in sources)
     whole, first, second, waiting = [stream], [], [], None
     half = spatial // 2
     bf16 = jnp.bfloat16
     for step in blocked:
         own = blocks[step]
-        other = swapped(own, "tm", 1)
+        other = tuple(swapped(rows, "tm", 1) for rows in own)
+        other = other if step else (beside,)
         boxes, combs = dispatched(
             own,
             other,
@@ -424,9 +442,11 @@
         results = expert_rows(pieces, inner, outer, step == 0)
         if step == 0:
             near = [swapped(pieces[k], "group", 1) for k in range(chips)]
-            others = expert_rows(near, inner, outer, True)
-            others = swapped(others[0], "group", 1)
-            results = pair_summed(results[0], others, chips)
+            joined, results = results[0], []
+            for at in (0, chips // 2):
+                others = expert_rows(near[at : at + chips // 2], inner, outer, True)
+                others = swapped(others[0], "group", 1)
+                results += pair_summed(joined, others, at, chips // 2)
         returned = [swapped(results[k], "tm", 2 * k) for k in range(chips)]
         here, there = combined(returned, combs)
         across_core = swapped(there, "tm", 1)

time: 209 us -> 215 us (1.029)
  blocking collectives: 25 us -> 0 us
  starting transfers between devices: 47.2 us -> 70.4 us
  Pallas kernels: 35.5 us -> 40.8 us
    all_to_all x2 -> x0, blocking collectives: 25 us -> none  [the longest x1 12.9 us: body(): lax.all_to_all(tokens.reshape(1, shards, across, channels), 'tm', split_a...]
    ppermute x38 -> x45, starting transfers between devices: 47.2 us -> 66 us  [swapped(): return lax.ppermute(rows, axis, [(i, i ^ step) for i in range(size)])]
    all_to_all x0 -> x1, waiting for transfers between devices: none -> 5.16 us  [body(): lax.all_to_all(tokens.reshape(1, shards, across, channels), 'tm', split_a...]
    all_to_all x0 -> x1, starting transfers between devices: none -> 4.39 us  [body(): lax.all_to_all(tokens.reshape(1, shards, across, channels), 'tm', split_a...]
    ppermute x38 -> x45, waiting for transfers between devices: 97.8 us -> 93.4 us  [swapped(): return lax.ppermute(rows, axis, [(i, i ^ step) for i in range(size)])]
    pallas_call x3 -> x6, Pallas kernels: 10.1 us -> 14.3 us  [the longest x1 8.26 us: time_mixing(): pl.pallas_call(mixing_kernel, out_shape=[jax.ShapeDtypeStruct((2 * across...]
    pallas_call x4 -> x5, Pallas kernels: 20.4 us -> 21.4 us  [expert_rows(): pl.pallas_call(functools.partial(expert_kernel, chips), out_shape=[jax.Sh...]
  transfers between devices with their start and end apart: 38 -> 46, of which waited for: 19 -> 20; matrix products, arithmetic and copies ran while one was open for 0% -> 0% of each run, Pallas kernels for 12% -> 15%
where the time goes in v4:
time: 215 us; the launch traced here: 211 us
  waiting for transfers between devices  98.6 us (46%)
  starting transfers between devices  70.4 us (33%)
  Pallas kernels  40.8 us (19%)
    ppermute x45, waiting for transfers between devices, swapped(): return lax.ppermute(rows, axis, [(i, i ^ step) for i in range(size)])  93.4 us
    ppermute x45, starting transfers between devices, swapped(): return lax.ppermute(rows, axis, [(i, i ^ step) for i in range(size)])  66 us
    pallas_call x5, Pallas kernels, expert_rows(): pl.pallas_call(functools.partial(expert_kernel, chips), out_shape=[jax.Sh...  21.4 us
    pallas_call x1, Pallas kernels, time_mixing(): pl.pallas_call(mixing_kernel, out_shape=[jax.ShapeDtypeStruct((2 * across...  8.26 us
    all_to_all x1, waiting for transfers between devices, body(): lax.all_to_all(tokens.reshape(1, shards, across, channels), 'tm', split_a...  5.16 us
    pallas_call x2, Pallas kernels, fetched(): pl.pallas_call(functools.partial(fetch_kernel, len(parts)), out_shape=[ja...  5.11 us
    all_to_all x1, starting transfers between devices, body(): lax.all_to_all(tokens.reshape(1, shards, across, channels), 'tm', split_a...  4.39 us
  transfers between devices with their start and end apart: 46, of which 20 were waited for; matrix products, arithmetic and copies ran while one was open for 0% of the time, Pallas kernels for 15%

profile of v4, /device:TPU:9, one launch (start us, length us, event | category | flops | bytes accessed | tf_op | source)
XLA Modules:
  0.0 210.6 jit_solution(2147609748687873252)
XLA Ops:
  0.0 4.4 %all-to-all-start = ((bf16[1,8,32,1024]{3,2,0,1:T(8,128)(2,1)}), bf16[1,8,32,1024]{3,2,0,1:T(8,128)(2,1)S(1)}, u32[]{:S(2)}, u32[]{:S(2)}) async-start(bf16[1,8,32,1024]{3,2,0,1:T(8,128)(2,1)} %bitcast.18), calls=%async_computation | async-start | bytes 1048576 | tf_op jit(solution)/shard_map/all_to_all | solution.py:405
  6.0 5.2 %all-to-all-done = bf16[1,8,32,1024]{3,2,0,1:T(8,128)(2,1)S(1)} async-done(((bf16[1,8,32,1024]{3,2,0,1:T(8,128)(2,1)}), bf16[1,8,32,1024]{3,2,0,1:T(8,128)(2,1)S(1)}, u32[]{:S(2)}, u32[]{:S(2)}) %all-to-all-start) | async-done | bytes 524320 | tf_op jit(solution)/shard_map/all_to_all | solution.py:405
  11.2 8.3 %mixing.1 = (bf16[64,1024]{1,0:T(8,128)(2,1)S(1)}, bf16[64,1024]{1,0:T(8,128)(2,1)S(1)}, bf16[64,1024]{1,0:T(8,128)(2,1)S(1)}, bf16[64,1024]{1,0:T(8,128)(2,1)S(1)}) custom-call(bf16[8,32,1024]{2,1,0:T(8,128)(2,1)S(1)} %bitcast.9, f32[3,1024]{1,0:T(4,128)S(1)} %get-tuple-element.52.taps, bf16[1024,1024]{1,0:T(8,128)(2,1)S(1)} %get-tuple-element.53.outer, ...), custom_call_target="tpu_custom_call" | custom-call | tf_op jit(solution)/shard_map/mixing/pallas_call | solution.py:151
  19.5 2.8 %collective-permute-start = (bf16[64,1024]{1,0:T(8,128)(2,1)S(1)}, bf16[64,1024]{1,0:T(8,128)(2,1)S(1)}, u32[]{:S(2)}, u32[]{:S(2)}) collective-permute-start(bf16[64,1024]{1,0:T(8,128)(2,1)S(1)} %get-tuple-element.55), channel_id=1, source_target_pairs={{0,8},{4,12},{8,0},{12,4},{16,24},{20,28},{24,16},{28,20},{1,9},{5... | collective-permute-start | bytes 393224 | tf_op jit(solution)/shard_map/ppermute | solution.py:398
  23.6 2.4 %collective-permute-start.3 = (bf16[64,1024]{1,0:T(8,128)(2,1)S(1)}, bf16[64,1024]{1,0:T(8,128)(2,1)S(1)}, u32[]{:S(2)}, u32[]{:S(2)}) collective-permute-start(bf16[64,1024]{1,0:T(8,128)(2,1)S(1)} %get-tuple-element.54.refs_0_), channel_id=1, source_target_pairs={{0,4},{4,0},{8,12},{12,8},{16,20},{20,16},{24,28},{28,24},{1,5},{5... | collective-permute-start | bytes 393224 | tf_op jit(solution)/shard_map/ppermute | solution.py:398
  25.9 2.3 %collective-permute-start.4 = (bf16[64,1024]{1,0:T(8,128)(2,1)S(1)}, bf16[64,1024]{1,0:T(8,128)(2,1)S(1)}, u32[]{:S(2)}, u32[]{:S(2)}) collective-permute-start(bf16[64,1024]{1,0:T(8,128)(2,1)S(1)} %collective-permute-done.refs_1_), channel_id=1, source_target_pairs={{0,4},{4,0},{8,12},{12,8},{16,20},{20,16},{24,28},{28,24},{1,5},{5... | collective-permute-start | bytes 393224 | tf_op jit(solution)/shard_map/ppermute | solution.py:398
  28.3 2.7 %collective-permute-start.5 = (bf16[64,1024]{1,0:T(8,128)(2,1)S(1)}, bf16[64,1024]{1,0:T(8,128)(2,1)S(1)}, u32[]{:S(2)}, u32[]{:S(2)}) collective-permute-start(bf16[64,1024]{1,0:T(8,128)(2,1)S(1)} %collective-permute-done.1.refs_2_), channel_id=1, source_target_pairs={{0,4},{4,0},{8,12},{12,8},{16,20},{20,16},{24,28},{28,24},{1,5},{5... | collective-permute-start | bytes 393224 | tf_op jit(solution)/shard_map/ppermute | solution.py:398
  33.1 2.4 %collective-permute-start.22 = (bf16[256,1024]{1,0:T(8,128)(2,1)S(1)}, bf16[256,1024]{1,0:T(8,128)(2,1)S(1)}, u32[]{:S(2)}, u32[]{:S(2)}) collective-permute-start(bf16[256,1024]{1,0:T(8,128)(2,1)S(1)} %get-tuple-element.59.refs_0_), channel_id=1, source_target_pairs={{0,2},{1,3},{2,0},{3,1},{4,6},{5,7},{6,4},{7,5},{8,10},{9,11},{10,... | collective-permute-start | bytes 1572872 | tf_op jit(solution)/shard_map/ppermute | solution.py:398
  35.4 22.8 %collective-permute-done.22.refs_0_ = bf16[256,1024]{1,0:T(8,128)(2,1)S(1)} collective-permute-done((bf16[256,1024]{1,0:T(8,128)(2,1)S(1)}, bf16[256,1024]{1,0:T(8,128)(2,1)S(1)}, u32[]{:S(2)}, u32[]{:S(2)}) %collective-permute-start.22) | collective-permute-done | bytes 524320 | tf_op jit(solution)/shard_map/ppermute | solution.py:398
  58.7 12.5 %collective-permute-done.33.refs_0_ = bf16[256,1024]{1,0:T(8,128)(2,1)S(1)} collective-permute-done((bf16[256,1024]{1,0:T(8,128)(2,1)S(1)}, bf16[256,1024]{1,0:T(8,128)(2,1)S(1)}, u32[]{:S(2)}, u32[]{:S(2)}) %collective-permute-start.33) | collective-permute-done | bytes 524320 | tf_op jit(solution)/shard_map/ppermute | solution.py:398
  77.7 1.9 collective-permute-start.32
  80.9 4.1 %collective-permute-start.21 = (s32[4,256]{1,0:T(4,128)S(1)}, s32[4,256]{1,0:T(4,128)S(1)}, u32[]{:S(2)}, u32[]{:S(2)}) collective-permute-start(s32[4,256]{1,0:T(4,128)S(1)} %pad_add_fusion), channel_id=1, source_target_pairs={{0,2},{1,3},{2,0},{3,1},{4,6},{5,7},{6,4},{7,5},{8,10},{9,11},{10,... | collective-permute-start | bytes 12296 | tf_op jit(solution)/shard_map/ppermute | solution.py:398
  85.1 3.5 %fetch.3 = (bf16[1024,2048]{1,0:T(8,128)(2,1)S(1)}, bf16[2048,1024]{1,0:T(8,128)(2,1)S(1)}) custom-call(bf16[1024,2048]{1,0:T(8,128)(2,1)} %bitcast.16, bf16[2048,1024]{1,0:T(8,128)(2,1)} %bitcast.17), custom_call_target="tpu_custom_call" | custom-call | tf_op jit(solution)/shard_map/fetch/pallas_call | solution.py:135
  91.6 3.8 %collective-permute-start.23 = (bf16[256,1024]{1,0:T(8,128)(2,1)S(1)}, bf16[256,1024]{1,0:T(8,128)(2,1)S(1)}, u32[]{:S(2)}, u32[]{:S(2)}) collective-permute-start(bf16[256,1024]{1,0:T(8,128)(2,1)S(1)} %collective-permute-done.22.refs_0_), channel_id=1, source_target_pairs={{0,4},{4,0},{8,12},{12,8},{16,20},{20,16},{24,28},{28,24},{1,5},{5... | collective-permute-start | bytes 1572872 | tf_op jit(solution)/shard_map/ppermute | solution.py:398
  96.9 2.6 %collective-permute-done.15.refs_0_ = bf16[128,1024]{1,0:T(8,128)(2,1)S(1)} collective-permute-done((bf16[128,1024]{1,0:T(8,128)(2,1)S(1)}, bf16[128,1024]{1,0:T(8,128)(2,1)S(1)}, u32[]{:S(2)}, u32[]{:S(2)}) %collective-permute-start.15) | collective-permute-done | bytes 262176 | tf_op jit(solution)/shard_map/ppermute | solution.py:398
  99.6 5.5 %collective-permute-done.16.refs_1_ = bf16[128,1024]{1,0:T(8,128)(2,1)S(1)} collective-permute-done((bf16[128,1024]{1,0:T(8,128)(2,1)S(1)}, bf16[128,1024]{1,0:T(8,128)(2,1)S(1)}, u32[]{:S(2)}, u32[]{:S(2)}) %collective-permute-start.16) | collective-permute-done | bytes 262176 | tf_op jit(solution)/shard_map/ppermute | solution.py:398
  105.7 2.9 %experts.7 = bf16[256,1024]{1,0:T(8,128)(2,1)S(1)} custom-call(bf16[128,1024]{1,0:T(8,128)(2,1)S(1)} %collective-permute-done.15.refs_0_, bf16[128,1024]{1,0:T(8,128)(2,1)S(1)} %collective-permute-done.16.refs_1_, bf16[1024,2048]{1,0:T(8,128)(2,1)S(1)} %get-tuple-element.65.refs_4_.refs_2_, bf16[2048,1024]{1,0:T(8,128)(2,1)S(1)} %get-tuple-element.66.refs_5_.refs_3_), custom_call_target="tpu_custom_call" | custom-call | flops 2147483648 | bytes 8388608 | tf_op jit(solution)/shard_map/experts/pallas_call | solution.py:254
  108.6 2.1 %collective-permute-done.12.refs_1_ = bf16[128,1024]{1,0:T(8,128)(2,1)S(1)} collective-permute-done((bf16[128,1024]{1,0:T(8,128)(2,1)S(1)}, bf16[128,1024]{1,0:T(8,128)(2,1)S(1)}, u32[]{:S(2)}, u32[]{:S(2)}) %collective-permute-start.12) | collective-permute-done | bytes 262176 | tf_op jit(solution)/shard_map/ppermute | solution.py:398
  111.0 3.1 %experts.6 = bf16[256,1024]{1,0:T(8,128)(2,1)S(1)} custom-call(bf16[128,1024]{1,0:T(8,128)(2,1)S(1)} %collective-permute-done.11.refs_0_, bf16[128,1024]{1,0:T(8,128)(2,1)S(1)} %collective-permute-done.12.refs_1_, bf16[1024,2048]{1,0:T(8,128)(2,1)S(1)} %get-tuple-element.65.refs_4_.refs_2_, bf16[2048,1024]{1,0:T(8,128)(2,1)S(1)} %get-tuple-element.66.refs_5_.refs_3_), custom_call_target="tpu_custom_call" | custom-call | flops 2147483648 | bytes 8388608 | tf_op jit(solution)/shard_map/experts/pallas_call | solution.py:254
  119.0 5.0 %experts.9 = (bf16[128,1024]{1,0:T(8,128)(2,1)S(1)}, bf16[128,1024]{1,0:T(8,128)(2,1)S(1)}, bf16[128,1024]{1,0:T(8,128)(2,1)S(1)}, bf16[128,1024]{1,0:T(8,128)(2,1)S(1)}) custom-call(bf16[128,1024]{1,0:T(8,128)(2,1)S(1)} %get-tuple-element.87.refs_0_, bf16[128,1024]{1,0:T(8,128)(2,1)S(1)} %collective-permute-done.35.refs_1_, ...), custom_call_target="tpu_custom_call" | custom-call | flops 4294967296 | bytes 8388608 | tf_op jit(solution)/shard_map/experts/pallas_call | solution.py:254
  125.2 2.1 collective-permute-start.40
  127.3 5.0 %experts.8 = (bf16[128,1024]{1,0:T(8,128)(2,1)S(1)}, bf16[128,1024]{1,0:T(8,128)(2,1)S(1)}, bf16[128,1024]{1,0:T(8,128)(2,1)S(1)}, bf16[128,1024]{1,0:T(8,128)(2,1)S(1)}) custom-call(bf16[128,1024]{1,0:T(8,128)(2,1)S(1)} %get-tuple-element.75.refs_0_, bf16[128,1024]{1,0:T(8,128)(2,1)S(1)} %collective-permute-done.24.refs_1_, ...), custom_call_target="tpu_custom_call" | custom-call | flops 4294967296 | bytes 8388608 | tf_op jit(solution)/shard_map/experts/pallas_call | solution.py:254
  134.8 2.3 %collective-permute-start.28 = (bf16[128,1024]{1,0:T(8,128)(2,1)S(1)}, bf16[128,1024]{1,0:T(8,128)(2,1)S(1)}, u32[]{:S(2)}, u32[]{:S(2)}) collective-permute-start(bf16[128,1024]{1,0:T(8,128)(2,1)S(1)} %get-tuple-element.81), channel_id=1, source_target_pairs={{0,16},{4,20},{8,24},{12,28},{16,0},{20,4},{24,8},{28,12},{1,17},{... | collective-permute-start | bytes 786440 | tf_op jit(solution)/shard_map/ppermute | solution.py:398
  139.8 9.8 %collective-permute-start.41 = (bf16[256,1024]{1,0:T(8,128)(2,1)S(1)}, bf16[256,1024]{1,0:T(8,128)(2,1)S(1)}, u32[]{:S(2)}, u32[]{:S(2)}) collective-permute-start(bf16[256,1024]{1,0:T(8,128)(2,1)S(1)} %get-tuple-element.98), channel_id=1, source_target_pairs={{0,4},{4,0},{8,12},{12,8},{16,20},{20,16},{24,28},{28,24},{1,5},{5... | collective-permute-start | bytes 1572872 | tf_op jit(solution)/shard_map/ppermute | solution.py:398
  149.6 5.3 %experts.5.one = bf16[512,1024]{1,0:T(8,128)(2,1)S(1)} custom-call(bf16[128,1024]{1,0:T(8,128)(2,1)S(1)} %get-tuple-element.61.refs_0_, bf16[128,1024]{1,0:T(8,128)(2,1)S(1)} %collective-permute-done.8.refs_1_, bf16[128,1024]{1,0:T(8,128)(2,1)S(1)} %collective-permute-done.9.refs_2_, bf16[128,1024]{1,0:T(8,128)(2,1)S(1)} %collective-permute-done.10.refs_3_, ...), custom_call_target="tpu_custom_call" | custom-call | flops 4294967296 | bytes 8388608 | tf_op jit(solution)/shard_map/experts/pallas_call | solution.py:254
  159.4 9.1 %collective-permute-done.18.refs_2_ = bf16[128,1024]{1,0:T(8,128)(2,1)S(1)} collective-permute-done((bf16[128,1024]{1,0:T(8,128)(2,1)S(1)}, bf16[128,1024]{1,0:T(8,128)(2,1)S(1)}, u32[]{:S(2)}, u32[]{:S(2)}) %collective-permute-start.18) | collective-permute-done | bytes 262176 | tf_op jit(solution)/shard_map/ppermute | solution.py:398
  172.1 3.6 %collective-permute-start.31 = (bf16[128,1024]{1,0:T(8,128)(2,1)S(1)}, bf16[128,1024]{1,0:T(8,128)(2,1)S(1)}, u32[]{:S(2)}, u32[]{:S(2)}) collective-permute-start(bf16[128,1024]{1,0:T(8,128)(2,1)S(1)} %slice.47), channel_id=1, source_target_pairs={{0,2},{1,3},{2,0},{3,1},{4,6},{5,7},{6,4},{7,5},{8,10},{9,11},{10,... | collective-permute-start | bytes 786440 | tf_op jit(solution)/shard_map/ppermute | solution.py:398
  176.0 6.9 %collective-permute-done.43 = bf16[128,1024]{1,0:T(8,128)(2,1)S(1)} collective-permute-done((bf16[128,1024]{1,0:T(8,128)(2,1)S(1)}, bf16[128,1024]{1,0:T(8,128)(2,1)S(1)}, u32[]{:S(2)}, u32[]{:S(2)}) %collective-permute-start.43) | collective-permute-done | bytes 262176 | tf_op jit(solution)/shard_map/ppermute | solution.py:398
  183.0 3.4 %collective-permute-start.44 = (bf16[128,1024]{1,0:T(8,128)(2,1)S(1)}, bf16[128,1024]{1,0:T(8,128)(2,1)S(1)}, u32[]{:S(2)}, u32[]{:S(2)}) collective-permute-start(bf16[128,1024]{1,0:T(8,128)(2,1)S(1)} %fusion), channel_id=1, source_target_pairs={{0,2},{1,3},{2,0},{3,1},{4,6},{5,7},{6,4},{7,5},{8,10},{9,11},{10,... | collective-permute-start | bytes 786440 | tf_op jit(solution)/shard_map/ppermute | solution.py:398
  186.4 11.8 %collective-permute-done.31.refs_3_ = bf16[128,1024]{1,0:T(8,128)(2,1)S(1)} collective-permute-done((bf16[128,1024]{1,0:T(8,128)(2,1)S(1)}, bf16[128,1024]{1,0:T(8,128)(2,1)S(1)}, u32[]{:S(2)}, u32[]{:S(2)}) %collective-permute-start.31) | collective-permute-done | bytes 262176 | tf_op jit(solution)/shard_map/ppermute | solution.py:398
  198.2 6.6 %collective-permute-done.42.refs_4_ = bf16[128,1024]{1,0:T(8,128)(2,1)S(1)} collective-permute-done((bf16[128,1024]{1,0:T(8,128)(2,1)S(1)}, bf16[128,1024]{1,0:T(8,128)(2,1)S(1)}, u32[]{:S(2)}, u32[]{:S(2)}) %collective-permute-start.42) | collective-permute-done | bytes 262176 | tf_op jit(solution)/shard_map/ppermute | solution.py:398
  204.9 4.6 %collective-permute-done.44.refs_5_ = bf16[128,1024]{1,0:T(8,128)(2,1)S(1)} collective-permute-done((bf16[128,1024]{1,0:T(8,128)(2,1)S(1)}, bf16[128,1024]{1,0:T(8,128)(2,1)S(1)}, u32[]{:S(2)}, u32[]{:S(2)}) %collective-permute-start.44) | collective-permute-done | bytes 262176 | tf_op jit(solution)/shard_map/ppermute | solution.py:398
  (90 shorter events, 39.3 us)
Async XLA Ops:
  0.0 11.2 %all-to-all-start = ((bf16[1,8,32,1024]{3,2,0,1:T(8,128)(2,1)}), bf16[1,8,32,1024]{3,2,0,1:T(8,128)(2,1)S(1)}, u32[]{:S(2)}, u32[]{:S(2)}) async-start(bf16[1,8,32,1024]{3,2,0,1:T(8,128)(2,1)} %bitcast.18), calls=%async_computation | async-start | bytes 1048576 | tf_op jit(solution)/shard_map/all_to_all | solution.py:405
  22.4 8.6 %collective-permute-start.2 = (bf16[64,1024]{1,0:T(8,128)(2,1)S(1)}, bf16[64,1024]{1,0:T(8,128)(2,1)S(1)}, u32[]{:S(2)}, u32[]{:S(2)}) collective-permute-start(bf16[64,1024]{1,0:T(8,128)(2,1)S(1)} %get-tuple-element.57), channel_id=1, source_target_pairs={{0,24},{4,28},{8,16},{12,20},{16,8},{20,12},{24,0},{28,4},{1,25},{... | collective-permute-start | bytes 393224 | tf_op jit(solution)/shard_map/ppermute | solution.py:398
  33.1 25.2 %collective-permute-start.22 = (bf16[256,1024]{1,0:T(8,128)(2,1)S(1)}, bf16[256,1024]{1,0:T(8,128)(2,1)S(1)}, u32[]{:S(2)}, u32[]{:S(2)}) collective-permute-start(bf16[256,1024]{1,0:T(8,128)(2,1)S(1)} %get-tuple-element.59.refs_0_), channel_id=1, source_target_pairs={{0,2},{1,3},{2,0},{3,1},{4,6},{5,7},{6,4},{7,5},{8,10},{9,11},{10,... | collective-permute-start | bytes 1572872 | tf_op jit(solution)/shard_map/ppermute | solution.py:398
  58.2 13.0 %collective-permute-start.33 = (bf16[256,1024]{1,0:T(8,128)(2,1)S(1)}, bf16[256,1024]{1,0:T(8,128)(2,1)S(1)}, u32[]{:S(2)}, u32[]{:S(2)}) collective-permute-start(bf16[256,1024]{1,0:T(8,128)(2,1)S(1)} %collective-permute-done.22.refs_0_), channel_id=1, source_target_pairs={{0,1},{1,0},{2,3},{3,2},{4,5},{5,4},{6,7},{7,6},{8,9},{9,8},{10,11... | collective-permute-start | bytes 1572872 | tf_op jit(solution)/shard_map/ppermute | solution.py:398
  71.2 20.4 %collective-permute-start.34 = (bf16[256,1024]{1,0:T(8,128)(2,1)S(1)}, bf16[256,1024]{1,0:T(8,128)(2,1)S(1)}, u32[]{:S(2)}, u32[]{:S(2)}) collective-permute-start(bf16[256,1024]{1,0:T(8,128)(2,1)S(1)} %collective-permute-done.33.refs_0_), channel_id=1, source_target_pairs={{0,4},{4,0},{8,12},{12,8},{16,20},{20,16},{24,28},{28,24},{1,5},{5... | collective-permute-start | bytes 1572872 | tf_op jit(solution)/shard_map/ppermute | solution.py:398
  75.0 13.7 %collective-permute-start.9 = (bf16[128,1024]{1,0:T(8,128)(2,1)S(1)}, bf16[128,1024]{1,0:T(8,128)(2,1)S(1)}, u32[]{:S(2)}, u32[]{:S(2)}) collective-permute-start(bf16[128,1024]{1,0:T(8,128)(2,1)S(1)} %get-tuple-element.63), channel_id=1, source_target_pairs={{0,16},{4,20},{8,24},{12,28},{16,0},{20,4},{24,8},{28,12},{1,17},{... | collective-permute-start | bytes 786440 | tf_op jit(solution)/shard_map/ppermute | solution.py:398
  75.1 15.0 %collective-permute-start.10 = (bf16[128,1024]{1,0:T(8,128)(2,1)S(1)}, bf16[128,1024]{1,0:T(8,128)(2,1)S(1)}, u32[]{:S(2)}, u32[]{:S(2)}) collective-permute-start(bf16[128,1024]{1,0:T(8,128)(2,1)S(1)} %get-tuple-element.64), channel_id=1, source_target_pairs={{0,24},{4,28},{8,16},{12,20},{16,8},{20,12},{24,0},{28,4},{1,25},{... | collective-permute-start | bytes 786440 | tf_op jit(solution)/shard_map/ppermute | solution.py:398
  76.8 13.4 %collective-permute-start.8 = (bf16[128,1024]{1,0:T(8,128)(2,1)S(1)}, bf16[128,1024]{1,0:T(8,128)(2,1)S(1)}, u32[]{:S(2)}, u32[]{:S(2)}) collective-permute-start(bf16[128,1024]{1,0:T(8,128)(2,1)S(1)} %get-tuple-element.62), channel_id=1, source_target_pairs={{0,8},{4,12},{8,0},{12,4},{16,24},{20,28},{24,16},{28,20},{1,9},{5... | collective-permute-start | bytes 786440 | tf_op jit(solution)/shard_map/ppermute | solution.py:398
  88.7 10.8 %collective-permute-start.15 = (bf16[128,1024]{1,0:T(8,128)(2,1)S(1)}, bf16[128,1024]{1,0:T(8,128)(2,1)S(1)}, u32[]{:S(2)}, u32[]{:S(2)}) collective-permute-start(bf16[128,1024]{1,0:T(8,128)(2,1)S(1)} %collective-permute-done.9.refs_2_), channel_id=1, source_target_pairs={{0,1},{1,0},{2,3},{3,2},{4,5},{5,4},{6,7},{7,6},{8,9},{9,8},{10,11... | collective-permute-start | bytes 786440 | tf_op jit(solution)/shard_map/ppermute | solution.py:398
  90.1 15.0 %collective-permute-start.16 = (bf16[128,1024]{1,0:T(8,128)(2,1)S(1)}, bf16[128,1024]{1,0:T(8,128)(2,1)S(1)}, u32[]{:S(2)}, u32[]{:S(2)}) collective-permute-start(bf16[128,1024]{1,0:T(8,128)(2,1)S(1)} %collective-permute-done.10.refs_3_), channel_id=1, source_target_pairs={{0,1},{1,0},{2,3},{3,2},{4,5},{5,4},{6,7},{7,6},{8,9},{9,8},{10,11... | collective-permute-start | bytes 786440 | tf_op jit(solution)/shard_map/ppermute | solution.py:398
  90.2 20.5 %collective-permute-start.12 = (bf16[128,1024]{1,0:T(8,128)(2,1)S(1)}, bf16[128,1024]{1,0:T(8,128)(2,1)S(1)}, u32[]{:S(2)}, u32[]{:S(2)}) collective-permute-start(bf16[128,1024]{1,0:T(8,128)(2,1)S(1)} %collective-permute-done.8.refs_1_), channel_id=1, source_target_pairs={{0,1},{1,0},{2,3},{3,2},{4,5},{5,4},{6,7},{7,6},{8,9},{9,8},{10,11... | collective-permute-start | bytes 786440 | tf_op jit(solution)/shard_map/ppermute | solution.py:398
  91.6 22.5 %collective-permute-start.23 = (bf16[256,1024]{1,0:T(8,128)(2,1)S(1)}, bf16[256,1024]{1,0:T(8,128)(2,1)S(1)}, u32[]{:S(2)}, u32[]{:S(2)}) collective-permute-start(bf16[256,1024]{1,0:T(8,128)(2,1)S(1)} %collective-permute-done.22.refs_0_), channel_id=1, source_target_pairs={{0,4},{4,0},{8,12},{12,8},{16,20},{20,16},{24,28},{28,24},{1,5},{5... | collective-permute-start | bytes 1572872 | tf_op jit(solution)/shard_map/ppermute | solution.py:398
  96.3 20.0 %collective-permute-start.35 = (bf16[128,1024]{1,0:T(8,128)(2,1)S(1)}, bf16[128,1024]{1,0:T(8,128)(2,1)S(1)}, u32[]{:S(2)}, u32[]{:S(2)}) collective-permute-start(bf16[128,1024]{1,0:T(8,128)(2,1)S(1)} %get-tuple-element.88), channel_id=1, source_target_pairs={{0,8},{4,12},{8,0},{12,4},{16,24},{20,28},{24,16},{28,20},{1,9},{5... | collective-permute-start | bytes 786440 | tf_op jit(solution)/shard_map/ppermute | solution.py:398
  99.5 17.4 %collective-permute-start.36 = (bf16[128,1024]{1,0:T(8,128)(2,1)S(1)}, bf16[128,1024]{1,0:T(8,128)(2,1)S(1)}, u32[]{:S(2)}, u32[]{:S(2)}) collective-permute-start(bf16[128,1024]{1,0:T(8,128)(2,1)S(1)} %get-tuple-element.89), channel_id=1, source_target_pairs={{0,16},{4,20},{8,24},{12,28},{16,0},{20,4},{24,8},{28,12},{1,17},{... | collective-permute-start | bytes 786440 | tf_op jit(solution)/shard_map/ppermute | solution.py:398
  105.1 12.1 %collective-permute-start.37 = (bf16[128,1024]{1,0:T(8,128)(2,1)S(1)}, bf16[128,1024]{1,0:T(8,128)(2,1)S(1)}, u32[]{:S(2)}, u32[]{:S(2)}) collective-permute-start(bf16[128,1024]{1,0:T(8,128)(2,1)S(1)} %get-tuple-element.90), channel_id=1, source_target_pairs={{0,24},{4,28},{8,16},{12,20},{16,8},{20,12},{24,0},{28,4},{1,25},{... | collective-permute-start | bytes 786440 | tf_op jit(solution)/shard_map/ppermute | solution.py:398
  110.7 29.0 %collective-permute-start.17 = (bf16[256,1024]{1,0:T(8,128)(2,1)S(1)}, bf16[256,1024]{1,0:T(8,128)(2,1)S(1)}, u32[]{:S(2)}, u32[]{:S(2)}) collective-permute-start(bf16[256,1024]{1,0:T(8,128)(2,1)S(1)} %experts.7), channel_id=1, source_target_pairs={{0,1},{1,0},{2,3},{3,2},{4,5},{5,4},{6,7},{7,6},{8,9},{9,8},{10,11... | collective-permute-start | bytes 1572872 | tf_op jit(solution)/shard_map/ppermute | solution.py:398
  114.1 40.8 %collective-permute-start.13 = (bf16[256,1024]{1,0:T(8,128)(2,1)S(1)}, bf16[256,1024]{1,0:T(8,128)(2,1)S(1)}, u32[]{:S(2)}, u32[]{:S(2)}) collective-permute-start(bf16[256,1024]{1,0:T(8,128)(2,1)S(1)} %experts.6), channel_id=1, source_target_pairs={{0,1},{1,0},{2,3},{3,2},{4,5},{5,4},{6,7},{7,6},{8,9},{9,8},{10,11... | collective-permute-start | bytes 1572872 | tf_op jit(solution)/shard_map/ppermute | solution.py:398
  125.2 9.6 %collective-permute-start.39 = (bf16[128,1024]{1,0:T(8,128)(2,1)S(1)}, bf16[128,1024]{1,0:T(8,128)(2,1)S(1)}, u32[]{:S(2)}, u32[]{:S(2)}) collective-permute-start(bf16[128,1024]{1,0:T(8,128)(2,1)S(1)} %get-tuple-element.93), channel_id=1, source_target_pairs={{0,16},{4,20},{8,24},{12,28},{16,0},{20,4},{24,8},{28,12},{1,17},{... | collective-permute-start | bytes 786440 | tf_op jit(solution)/shard_map/ppermute | solution.py:398
  125.2 12.4 %collective-permute-start.40 = (bf16[128,1024]{1,0:T(8,128)(2,1)S(1)}, bf16[128,1024]{1,0:T(8,128)(2,1)S(1)}, u32[]{:S(2)}, u32[]{:S(2)}) collective-permute-start(bf16[128,1024]{1,0:T(8,128)(2,1)S(1)} %get-tuple-element.94), channel_id=1, source_target_pairs={{0,24},{4,28},{8,16},{12,20},{16,8},{20,12},{24,0},{28,4},{1,25},{... | collective-permute-start | bytes 786440 | tf_op jit(solution)/shard_map/ppermute | solution.py:398
  132.4 23.5 %collective-permute-start.27 = (bf16[128,1024]{1,0:T(8,128)(2,1)S(1)}, bf16[128,1024]{1,0:T(8,128)(2,1)S(1)}, u32[]{:S(2)}, u32[]{:S(2)}) collective-permute-start(bf16[128,1024]{1,0:T(8,128)(2,1)S(1)} %get-tuple-element.80), channel_id=1, source_target_pairs={{0,8},{4,12},{8,0},{12,4},{16,24},{20,28},{24,16},{28,20},{1,9},{5... | collective-permute-start | bytes 786440 | tf_op jit(solution)/shard_map/ppermute | solution.py:398
  134.8 23.1 %collective-permute-start.28 = (bf16[128,1024]{1,0:T(8,128)(2,1)S(1)}, bf16[128,1024]{1,0:T(8,128)(2,1)S(1)}, u32[]{:S(2)}, u32[]{:S(2)}) collective-permute-start(bf16[128,1024]{1,0:T(8,128)(2,1)S(1)} %get-tuple-element.81), channel_id=1, source_target_pairs={{0,16},{4,20},{8,24},{12,28},{16,0},{20,4},{24,8},{28,12},{1,17},{... | collective-permute-start | bytes 786440 | tf_op jit(solution)/shard_map/ppermute | solution.py:398
  137.6 20.6 %collective-permute-start.29 = (bf16[128,1024]{1,0:T(8,128)(2,1)S(1)}, bf16[128,1024]{1,0:T(8,128)(2,1)S(1)}, u32[]{:S(2)}, u32[]{:S(2)}) collective-permute-start(bf16[128,1024]{1,0:T(8,128)(2,1)S(1)} %get-tuple-element.82), channel_id=1, source_target_pairs={{0,24},{4,28},{8,16},{12,20},{16,8},{20,12},{24,0},{28,4},{1,25},{... | collective-permute-start | bytes 786440 | tf_op jit(solution)/shard_map/ppermute | solution.py:398
  139.8 31.9 %collective-permute-start.41 = (bf16[256,1024]{1,0:T(8,128)(2,1)S(1)}, bf16[256,1024]{1,0:T(8,128)(2,1)S(1)}, u32[]{:S(2)}, u32[]{:S(2)}) collective-permute-start(bf16[256,1024]{1,0:T(8,128)(2,1)S(1)} %get-tuple-element.98), channel_id=1, source_target_pairs={{0,4},{4,0},{8,12},{12,8},{16,20},{20,16},{24,28},{28,24},{1,5},{5... | collective-permute-start | bytes 1572872 | tf_op jit(solution)/shard_map/ppermute | solution.py:398
  155.0 13.5 %collective-permute-start.18 = (bf16[128,1024]{1,0:T(8,128)(2,1)S(1)}, bf16[128,1024]{1,0:T(8,128)(2,1)S(1)}, u32[]{:S(2)}, u32[]{:S(2)}) collective-permute-start(bf16[128,1024]{1,0:T(8,128)(2,1)S(1)} %get-tuple-element.69), channel_id=1, source_target_pairs={{0,16},{4,20},{8,24},{12,28},{16,0},{20,4},{24,8},{28,12},{1,17},{... | collective-permute-start | bytes 786440 | tf_op jit(solution)/shard_map/ppermute | solution.py:398
  156.0 12.5 %collective-permute-start.19 = (bf16[128,1024]{1,0:T(8,128)(2,1)S(1)}, bf16[128,1024]{1,0:T(8,128)(2,1)S(1)}, u32[]{:S(2)}, u32[]{:S(2)}) collective-permute-start(bf16[128,1024]{1,0:T(8,128)(2,1)S(1)} %get-tuple-element.70), channel_id=1, source_target_pairs={{0,24},{4,28},{8,16},{12,20},{16,8},{20,12},{24,0},{28,4},{1,25},{... | collective-permute-start | bytes 786440 | tf_op jit(solution)/shard_map/ppermute | solution.py:398
  157.9 12.3 %collective-permute-start.14 = (bf16[128,1024]{1,0:T(8,128)(2,1)S(1)}, bf16[128,1024]{1,0:T(8,128)(2,1)S(1)}, u32[]{:S(2)}, u32[]{:S(2)}) collective-permute-start(bf16[128,1024]{1,0:T(8,128)(2,1)S(1)} %get-tuple-element.68), channel_id=1, source_target_pairs={{0,8},{4,12},{8,0},{12,4},{16,24},{20,28},{24,16},{28,20},{1,9},{5... | collective-permute-start | bytes 786440 | tf_op jit(solution)/shard_map/ppermute | solution.py:398
  158.7 13.2 %collective-permute-start.30 = (bf16[256,1024]{1,0:T(8,128)(2,1)S(1)}, bf16[256,1024]{1,0:T(8,128)(2,1)S(1)}, u32[]{:S(2)}, u32[]{:S(2)}) collective-permute-start(bf16[256,1024]{1,0:T(8,128)(2,1)S(1)} %get-tuple-element.86), channel_id=1, source_target_pairs={{0,4},{4,0},{8,12},{12,8},{16,20},{20,16},{24,28},{28,24},{1,5},{5... | collective-permute-start | bytes 1572872 | tf_op jit(solution)/shard_map/ppermute | solution.py:398
  170.7 15.7 %collective-permute-start.20 = (bf16[256,1024]{1,0:T(8,128)(2,1)S(1)}, bf16[256,1024]{1,0:T(8,128)(2,1)S(1)}, u32[]{:S(2)}, u32[]{:S(2)}) collective-permute-start(bf16[256,1024]{1,0:T(8,128)(2,1)S(1)} %get-tuple-element.74), channel_id=1, source_target_pairs={{0,4},{4,0},{8,12},{12,8},{16,20},{20,16},{24,28},{28,24},{1,5},{5... | collective-permute-start | bytes 1572872 | tf_op jit(solution)/shard_map/ppermute | solution.py:398
  171.8 11.1 %collective-permute-start.43 = (bf16[128,1024]{1,0:T(8,128)(2,1)S(1)}, bf16[128,1024]{1,0:T(8,128)(2,1)S(1)}, u32[]{:S(2)}, u32[]{:S(2)}) collective-permute-start(bf16[128,1024]{1,0:T(8,128)(2,1)S(1)} %get-tuple-element.99), channel_id=1, source_target_pairs={{0,1},{1,0},{2,3},{3,2},{4,5},{5,4},{6,7},{7,6},{8,9},{9,8},{10,11... | collective-permute-start | bytes 786440 | tf_op jit(solution)/shard_map/ppermute | solution.py:398
  172.1 26.1 %collective-permute-start.31 = (bf16[128,1024]{1,0:T(8,128)(2,1)S(1)}, bf16[128,1024]{1,0:T(8,128)(2,1)S(1)}, u32[]{:S(2)}, u32[]{:S(2)}) collective-permute-start(bf16[128,1024]{1,0:T(8,128)(2,1)S(1)} %slice.47), channel_id=1, source_target_pairs={{0,2},{1,3},{2,0},{3,1},{4,6},{5,7},{6,4},{7,5},{8,10},{9,11},{10,... | collective-permute-start | bytes 786440 | tf_op jit(solution)/shard_map/ppermute | solution.py:398
  175.7 29.2 %collective-permute-start.42 = (bf16[128,1024]{1,0:T(8,128)(2,1)S(1)}, bf16[128,1024]{1,0:T(8,128)(2,1)S(1)}, u32[]{:S(2)}, u32[]{:S(2)}) collective-permute-start(bf16[128,1024]{1,0:T(8,128)(2,1)S(1)} %get-tuple-element.100), channel_id=1, source_target_pairs={{0,3},{1,2},{2,1},{3,0},{4,7},{5,6},{6,5},{7,4},{8,11},{9,10},{10,... | collective-permute-start | bytes 786440 | tf_op jit(solution)/shard_map/ppermute | solution.py:398
  183.0 26.5 %collective-permute-start.44 = (bf16[128,1024]{1,0:T(8,128)(2,1)S(1)}, bf16[128,1024]{1,0:T(8,128)(2,1)S(1)}, u32[]{:S(2)}, u32[]{:S(2)}) collective-permute-start(bf16[128,1024]{1,0:T(8,128)(2,1)S(1)} %fusion), channel_id=1, source_target_pairs={{0,2},{1,3},{2,0},{3,1},{4,6},{5,7},{6,4},{7,5},{8,10},{9,11},{10,... | collective-permute-start | bytes 786440 | tf_op jit(solution)/shard_map/ppermute | solution.py:398
  (16 other events, 207.0 us)

commit v5 on v4

--- a/solution.py
+++ b/solution.py
@@ -349,15 +349,17 @@
 
 def sum_kernel(halves, *refs):
     whole, (first, second), out = refs[:-1], halves, refs[-1]
-    half = out.shape[0] // 2
     parts, whole = whole[-(first + second) :], whole[: -(first + second)]
-    for at, group in ((0, parts[:first]), (half, parts[first:])):
-        total = whole[0][at : at + half, :].astype(jnp.float32)
+    at = 0
+    for group in (parts[:first], parts[first:]):
+        here = slice(at, at + group[0].shape[0])
+        total = whole[0][here, :].astype(jnp.float32)
         for part in whole[1:]:
-            total = total + part[at : at + half, :].astype(jnp.float32)
+            total = total + part[here, :].astype(jnp.float32)
         for part in group:
             total = total + part[...].astype(jnp.float32)
-        out[at : at + half, :] = total.astype(out.dtype)
+        out[here, :] = total.astype(out.dtype)
+        at = here.stop
 
 
 def summed(whole, first, second):
@@ -422,7 +424,7 @@
         sources = blocks[step - 1] if step % 2 else blocks[0]
         blocks[step] = tuple(swapped(rows, "group", 1 if step % 2 else step) for rows in sources)
     whole, first, second, waiting = [stream], [], [], None
-    half = spatial // 2
+    cut = spatial * 5 // 8
     bf16 = jnp.bfloat16
     for step in blocked:
         own = blocks[step]
@@ -454,11 +456,11 @@
             whole += [here, across_core]
             continue
         mixed = here + across_core.astype(jnp.float32)
-        first.append(swapped(mixed[:half].astype(bf16), "group", step))
+        first.append(swapped(mixed[:cut].astype(bf16), "group", step))
         if step % 2 == 0:
-            waiting = mixed[half:]
+            waiting = mixed[cut:]
         else:
-            near = swapped(mixed[half:].astype(bf16), "group", 1)
+            near = swapped(mixed[cut:].astype(bf16), "group", 1)
             joint = (waiting + near.astype(jnp.float32)).astype(bf16)
             second.append(swapped(joint, "group", step - 1))
     return summed(whole, first, second).reshape(1, spatial, channels)

time: 215 us -> 217 us (level)
  transfers between devices with their start and end apart: 46 -> 46, of which waited for: 20 -> 20; matrix products, arithmetic and copies ran while one was open for 0% -> 0% of each run, Pallas kernels for 15% -> 14%
where the time goes in v5:
time: 217 us; the launch traced here: 213 us
  waiting for transfers between devices  99.6 us (46%)
  starting transfers between devices  72.2 us (33%)
  Pallas kernels  40.8 us (19%)
    ppermute x45, waiting for transfers between devices, swapped(): return lax.ppermute(rows, axis, [(i, i ^ step) for i in range(size)])  94.5 us
    ppermute x45, starting transfers between devices, swapped(): return lax.ppermute(rows, axis, [(i, i ^ step) for i in range(size)])  67.8 us
    pallas_call x5, Pallas kernels, expert_rows(): pl.pallas_call(functools.partial(expert_kernel, chips), out_shape=[jax.Sh...  21.4 us
    pallas_call x1, Pallas kernels, time_mixing(): pl.pallas_call(mixing_kernel, out_shape=[jax.ShapeDtypeStruct((2 * across...  8.26 us
    all_to_all x1, waiting for transfers between devices, body(): lax.all_to_all(tokens.reshape(1, shards, across, channels), 'tm', split_a...  5.16 us
    pallas_call x2, Pallas kernels, fetched(): pl.pallas_call(functools.partial(fetch_kernel, len(parts)), out_shape=[ja...  5.11 us
    all_to_all x1, starting transfers between devices, body(): lax.all_to_all(tokens.reshape(1, shards, across, channels), 'tm', split_a...  4.39 us
  transfers between devices with their start and end apart: 46, of which 20 were waited for; matrix products, arithmetic and copies ran while one was open for 0% of the time, Pallas kernels for 14%

profile of v5, /device:TPU:9, one launch (start us, length us, event | category | flops | bytes accessed | tf_op | source)
XLA Modules:
  0.0 213.4 jit_solution(4124039623710002347)
XLA Ops:
  0.0 4.4 %all-to-all-start = ((bf16[1,8,32,1024]{3,2,0,1:T(8,128)(2,1)}), bf16[1,8,32,1024]{3,2,0,1:T(8,128)(2,1)S(1)}, u32[]{:S(2)}, u32[]{:S(2)}) async-start(bf16[1,8,32,1024]{3,2,0,1:T(8,128)(2,1)} %bitcast.18), calls=%async_computation | async-start | bytes 1048576 | tf_op jit(solution)/shard_map/all_to_all | solution.py:407
  6.0 5.2 %all-to-all-done = bf16[1,8,32,1024]{3,2,0,1:T(8,128)(2,1)S(1)} async-done(((bf16[1,8,32,1024]{3,2,0,1:T(8,128)(2,1)}), bf16[1,8,32,1024]{3,2,0,1:T(8,128)(2,1)S(1)}, u32[]{:S(2)}, u32[]{:S(2)}) %all-to-all-start) | async-done | bytes 524320 | tf_op jit(solution)/shard_map/all_to_all | solution.py:407
  11.2 8.3 %mixing.1 = (bf16[64,1024]{1,0:T(8,128)(2,1)S(1)}, bf16[64,1024]{1,0:T(8,128)(2,1)S(1)}, bf16[64,1024]{1,0:T(8,128)(2,1)S(1)}, bf16[64,1024]{1,0:T(8,128)(2,1)S(1)}) custom-call(bf16[8,32,1024]{2,1,0:T(8,128)(2,1)S(1)} %bitcast.9, f32[3,1024]{1,0:T(4,128)S(1)} %get-tuple-element.52.taps, bf16[1024,1024]{1,0:T(8,128)(2,1)S(1)} %get-tuple-element.53.outer, ...), custom_call_target="tpu_custom_call" | custom-call | tf_op jit(solution)/shard_map/mixing/pallas_call | solution.py:151
  19.5 2.8 %collective-permute-start = (bf16[64,1024]{1,0:T(8,128)(2,1)S(1)}, bf16[64,1024]{1,0:T(8,128)(2,1)S(1)}, u32[]{:S(2)}, u32[]{:S(2)}) collective-permute-start(bf16[64,1024]{1,0:T(8,128)(2,1)S(1)} %get-tuple-element.55), channel_id=1, source_target_pairs={{0,8},{4,12},{8,0},{12,4},{16,24},{20,28},{24,16},{28,20},{1,9},{5... | collective-permute-start | bytes 393224 | tf_op jit(solution)/shard_map/ppermute | solution.py:400
  23.6 2.4 %collective-permute-start.3 = (bf16[64,1024]{1,0:T(8,128)(2,1)S(1)}, bf16[64,1024]{1,0:T(8,128)(2,1)S(1)}, u32[]{:S(2)}, u32[]{:S(2)}) collective-permute-start(bf16[64,1024]{1,0:T(8,128)(2,1)S(1)} %get-tuple-element.54.refs_0_), channel_id=1, source_target_pairs={{0,4},{4,0},{8,12},{12,8},{16,20},{20,16},{24,28},{28,24},{1,5},{5... | collective-permute-start | bytes 393224 | tf_op jit(solution)/shard_map/ppermute | solution.py:400
  25.9 2.3 %collective-permute-start.4 = (bf16[64,1024]{1,0:T(8,128)(2,1)S(1)}, bf16[64,1024]{1,0:T(8,128)(2,1)S(1)}, u32[]{:S(2)}, u32[]{:S(2)}) collective-permute-start(bf16[64,1024]{1,0:T(8,128)(2,1)S(1)} %collective-permute-done.refs_1_), channel_id=1, source_target_pairs={{0,4},{4,0},{8,12},{12,8},{16,20},{20,16},{24,28},{28,24},{1,5},{5... | collective-permute-start | bytes 393224 | tf_op jit(solution)/shard_map/ppermute | solution.py:400
  28.3 2.7 %collective-permute-start.5 = (bf16[64,1024]{1,0:T(8,128)(2,1)S(1)}, bf16[64,1024]{1,0:T(8,128)(2,1)S(1)}, u32[]{:S(2)}, u32[]{:S(2)}) collective-permute-start(bf16[64,1024]{1,0:T(8,128)(2,1)S(1)} %collective-permute-done.1.refs_2_), channel_id=1, source_target_pairs={{0,4},{4,0},{8,12},{12,8},{16,20},{20,16},{24,28},{28,24},{1,5},{5... | collective-permute-start | bytes 393224 | tf_op jit(solution)/shard_map/ppermute | solution.py:400
  33.1 2.4 %collective-permute-start.22 = (bf16[256,1024]{1,0:T(8,128)(2,1)S(1)}, bf16[256,1024]{1,0:T(8,128)(2,1)S(1)}, u32[]{:S(2)}, u32[]{:S(2)}) collective-permute-start(bf16[256,1024]{1,0:T(8,128)(2,1)S(1)} %get-tuple-element.59.refs_0_), channel_id=1, source_target_pairs={{0,2},{1,3},{2,0},{3,1},{4,6},{5,7},{6,4},{7,5},{8,10},{9,11},{10,... | collective-permute-start | bytes 1572872 | tf_op jit(solution)/shard_map/ppermute | solution.py:400
  35.4 22.8 %collective-permute-done.22.refs_0_ = bf16[256,1024]{1,0:T(8,128)(2,1)S(1)} collective-permute-done((bf16[256,1024]{1,0:T(8,128)(2,1)S(1)}, bf16[256,1024]{1,0:T(8,128)(2,1)S(1)}, u32[]{:S(2)}, u32[]{:S(2)}) %collective-permute-start.22) | collective-permute-done | bytes 524320 | tf_op jit(solution)/shard_map/ppermute | solution.py:400
  58.7 12.5 %collective-permute-done.33.refs_0_ = bf16[256,1024]{1,0:T(8,128)(2,1)S(1)} collective-permute-done((bf16[256,1024]{1,0:T(8,128)(2,1)S(1)}, bf16[256,1024]{1,0:T(8,128)(2,1)S(1)}, u32[]{:S(2)}, u32[]{:S(2)}) %collective-permute-start.33) | collective-permute-done | bytes 524320 | tf_op jit(solution)/shard_map/ppermute | solution.py:400
  77.7 1.9 collective-permute-start.32
  80.9 4.1 %collective-permute-start.21 = (s32[4,256]{1,0:T(4,128)S(1)}, s32[4,256]{1,0:T(4,128)S(1)}, u32[]{:S(2)}, u32[]{:S(2)}) collective-permute-start(s32[4,256]{1,0:T(4,128)S(1)} %pad_add_fusion), channel_id=1, source_target_pairs={{0,2},{1,3},{2,0},{3,1},{4,6},{5,7},{6,4},{7,5},{8,10},{9,11},{10,... | collective-permute-start | bytes 12296 | tf_op jit(solution)/shard_map/ppermute | solution.py:400
  85.1 3.5 %fetch.3 = (bf16[1024,2048]{1,0:T(8,128)(2,1)S(1)}, bf16[2048,1024]{1,0:T(8,128)(2,1)S(1)}) custom-call(bf16[1024,2048]{1,0:T(8,128)(2,1)} %bitcast.16, bf16[2048,1024]{1,0:T(8,128)(2,1)} %bitcast.17), custom_call_target="tpu_custom_call" | custom-call | tf_op jit(solution)/shard_map/fetch/pallas_call | solution.py:135
  91.6 3.8 %collective-permute-start.23 = (bf16[256,1024]{1,0:T(8,128)(2,1)S(1)}, bf16[256,1024]{1,0:T(8,128)(2,1)S(1)}, u32[]{:S(2)}, u32[]{:S(2)}) collective-permute-start(bf16[256,1024]{1,0:T(8,128)(2,1)S(1)} %collective-permute-done.22.refs_0_), channel_id=1, source_target_pairs={{0,4},{4,0},{8,12},{12,8},{16,20},{20,16},{24,28},{28,24},{1,5},{5... | collective-permute-start | bytes 1572872 | tf_op jit(solution)/shard_map/ppermute | solution.py:400
  96.9 2.6 %collective-permute-done.15.refs_0_ = bf16[128,1024]{1,0:T(8,128)(2,1)S(1)} collective-permute-done((bf16[128,1024]{1,0:T(8,128)(2,1)S(1)}, bf16[128,1024]{1,0:T(8,128)(2,1)S(1)}, u32[]{:S(2)}, u32[]{:S(2)}) %collective-permute-start.15) | collective-permute-done | bytes 262176 | tf_op jit(solution)/shard_map/ppermute | solution.py:400
  99.6 5.5 %collective-permute-done.16.refs_1_ = bf16[128,1024]{1,0:T(8,128)(2,1)S(1)} collective-permute-done((bf16[128,1024]{1,0:T(8,128)(2,1)S(1)}, bf16[128,1024]{1,0:T(8,128)(2,1)S(1)}, u32[]{:S(2)}, u32[]{:S(2)}) %collective-permute-start.16) | collective-permute-done | bytes 262176 | tf_op jit(solution)/shard_map/ppermute | solution.py:400
  105.7 2.9 %experts.7 = bf16[256,1024]{1,0:T(8,128)(2,1)S(1)} custom-call(bf16[128,1024]{1,0:T(8,128)(2,1)S(1)} %collective-permute-done.15.refs_0_, bf16[128,1024]{1,0:T(8,128)(2,1)S(1)} %collective-permute-done.16.refs_1_, bf16[1024,2048]{1,0:T(8,128)(2,1)S(1)} %get-tuple-element.65.refs_4_.refs_2_, bf16[2048,1024]{1,0:T(8,128)(2,1)S(1)} %get-tuple-element.66.refs_5_.refs_3_), custom_call_target="tpu_custom_call" | custom-call | flops 2147483648 | bytes 8388608 | tf_op jit(solution)/shard_map/experts/pallas_call | solution.py:254
  108.6 2.1 collective-permute-done.12.refs_1_
  111.0 3.1 %experts.6 = bf16[256,1024]{1,0:T(8,128)(2,1)S(1)} custom-call(bf16[128,1024]{1,0:T(8,128)(2,1)S(1)} %collective-permute-done.11.refs_0_, bf16[128,1024]{1,0:T(8,128)(2,1)S(1)} %collective-permute-done.12.refs_1_, bf16[1024,2048]{1,0:T(8,128)(2,1)S(1)} %get-tuple-element.65.refs_4_.refs_2_, bf16[2048,1024]{1,0:T(8,128)(2,1)S(1)} %get-tuple-element.66.refs_5_.refs_3_), custom_call_target="tpu_custom_call" | custom-call | flops 2147483648 | bytes 8388608 | tf_op jit(solution)/shard_map/experts/pallas_call | solution.py:254
  119.0 5.0 %experts.9 = (bf16[128,1024]{1,0:T(8,128)(2,1)S(1)}, bf16[128,1024]{1,0:T(8,128)(2,1)S(1)}, bf16[128,1024]{1,0:T(8,128)(2,1)S(1)}, bf16[128,1024]{1,0:T(8,128)(2,1)S(1)}) custom-call(bf16[128,1024]{1,0:T(8,128)(2,1)S(1)} %get-tuple-element.87.refs_0_, bf16[128,1024]{1,0:T(8,128)(2,1)S(1)} %collective-permute-done.35.refs_1_, ...), custom_call_target="tpu_custom_call" | custom-call | flops 4294967296 | bytes 8388608 | tf_op jit(solution)/shard_map/experts/pallas_call | solution.py:254
  125.2 2.1 collective-permute-start.40
  127.3 5.0 %experts.8 = (bf16[128,1024]{1,0:T(8,128)(2,1)S(1)}, bf16[128,1024]{1,0:T(8,128)(2,1)S(1)}, bf16[128,1024]{1,0:T(8,128)(2,1)S(1)}, bf16[128,1024]{1,0:T(8,128)(2,1)S(1)}) custom-call(bf16[128,1024]{1,0:T(8,128)(2,1)S(1)} %get-tuple-element.75.refs_0_, bf16[128,1024]{1,0:T(8,128)(2,1)S(1)} %collective-permute-done.24.refs_1_, ...), custom_call_target="tpu_custom_call" | custom-call | flops 4294967296 | bytes 8388608 | tf_op jit(solution)/shard_map/experts/pallas_call | solution.py:254
  134.8 2.3 %collective-permute-start.28 = (bf16[128,1024]{1,0:T(8,128)(2,1)S(1)}, bf16[128,1024]{1,0:T(8,128)(2,1)S(1)}, u32[]{:S(2)}, u32[]{:S(2)}) collective-permute-start(bf16[128,1024]{1,0:T(8,128)(2,1)S(1)} %get-tuple-element.81), channel_id=1, source_target_pairs={{0,16},{4,20},{8,24},{12,28},{16,0},{20,4},{24,8},{28,12},{1,17},{... | collective-permute-start | bytes 786440 | tf_op jit(solution)/shard_map/ppermute | solution.py:400
  139.8 9.8 %collective-permute-start.41 = (bf16[256,1024]{1,0:T(8,128)(2,1)S(1)}, bf16[256,1024]{1,0:T(8,128)(2,1)S(1)}, u32[]{:S(2)}, u32[]{:S(2)}) collective-permute-start(bf16[256,1024]{1,0:T(8,128)(2,1)S(1)} %get-tuple-element.98), channel_id=1, source_target_pairs={{0,4},{4,0},{8,12},{12,8},{16,20},{20,16},{24,28},{28,24},{1,5},{5... | collective-permute-start | bytes 1572872 | tf_op jit(solution)/shard_map/ppermute | solution.py:400
  149.6 5.3 %experts.5.one = bf16[512,1024]{1,0:T(8,128)(2,1)S(1)} custom-call(bf16[128,1024]{1,0:T(8,128)(2,1)S(1)} %get-tuple-element.61.refs_0_, bf16[128,1024]{1,0:T(8,128)(2,1)S(1)} %collective-permute-done.8.refs_1_, bf16[128,1024]{1,0:T(8,128)(2,1)S(1)} %collective-permute-done.9.refs_2_, bf16[128,1024]{1,0:T(8,128)(2,1)S(1)} %collective-permute-done.10.refs_3_, ...), custom_call_target="tpu_custom_call" | custom-call | flops 4294967296 | bytes 8388608 | tf_op jit(solution)/shard_map/experts/pallas_call | solution.py:254
  159.4 9.1 %collective-permute-done.18.refs_2_ = bf16[128,1024]{1,0:T(8,128)(2,1)S(1)} collective-permute-done((bf16[128,1024]{1,0:T(8,128)(2,1)S(1)}, bf16[128,1024]{1,0:T(8,128)(2,1)S(1)}, u32[]{:S(2)}, u32[]{:S(2)}) %collective-permute-start.18) | collective-permute-done | bytes 262176 | tf_op jit(solution)/shard_map/ppermute | solution.py:400
  172.1 3.6 %collective-permute-start.31 = (bf16[160,1024]{1,0:T(8,128)(2,1)S(1)}, bf16[160,1024]{1,0:T(8,128)(2,1)S(1)}, u32[]{:S(2)}, u32[]{:S(2)}) collective-permute-start(bf16[160,1024]{1,0:T(8,128)(2,1)S(1)} %slice.47), channel_id=1, source_target_pairs={{0,2},{1,3},{2,0},{3,1},{4,6},{5,7},{6,4},{7,5},{8,10},{9,11},{10,... | collective-permute-start | bytes 983048 | tf_op jit(solution)/shard_map/ppermute | solution.py:400
  176.1 2.2 %collective-permute-done.43 = bf16[96,1024]{1,0:T(8,128)(2,1)S(1)} collective-permute-done((bf16[96,1024]{1,0:T(8,128)(2,1)S(1)}, bf16[96,1024]{1,0:T(8,128)(2,1)S(1)}, u32[]{:S(2)}, u32[]{:S(2)}) %collective-permute-start.43) | collective-permute-done | bytes 196640 | tf_op jit(solution)/shard_map/ppermute | solution.py:400
  178.3 5.2 %collective-permute-start.44 = (bf16[96,1024]{1,0:T(8,128)(2,1)S(1)}, bf16[96,1024]{1,0:T(8,128)(2,1)S(1)}, u32[]{:S(2)}, u32[]{:S(2)}) collective-permute-start(bf16[96,1024]{1,0:T(8,128)(2,1)S(1)} %fusion), channel_id=1, source_target_pairs={{0,2},{1,3},{2,0},{3,1},{4,6},{5,7},{6,4},{7,5},{8,10},{9,11},{10,... | collective-permute-start | bytes 589832 | tf_op jit(solution)/shard_map/ppermute | solution.py:400
  183.5 17.5 %collective-permute-done.31.refs_3_ = bf16[160,1024]{1,0:T(8,128)(2,1)S(1)} collective-permute-done((bf16[160,1024]{1,0:T(8,128)(2,1)S(1)}, bf16[160,1024]{1,0:T(8,128)(2,1)S(1)}, u32[]{:S(2)}, u32[]{:S(2)}) %collective-permute-start.31) | collective-permute-done | bytes 327712 | tf_op jit(solution)/shard_map/ppermute | solution.py:400
  201.0 8.0 %collective-permute-done.42.refs_4_ = bf16[160,1024]{1,0:T(8,128)(2,1)S(1)} collective-permute-done((bf16[160,1024]{1,0:T(8,128)(2,1)S(1)}, bf16[160,1024]{1,0:T(8,128)(2,1)S(1)}, u32[]{:S(2)}, u32[]{:S(2)}) %collective-permute-start.42) | collective-permute-done | bytes 327712 | tf_op jit(solution)/shard_map/ppermute | solution.py:400
  209.1 3.2 %collective-permute-done.44.refs_5_ = bf16[96,1024]{1,0:T(8,128)(2,1)S(1)} collective-permute-done((bf16[96,1024]{1,0:T(8,128)(2,1)S(1)}, bf16[96,1024]{1,0:T(8,128)(2,1)S(1)}, u32[]{:S(2)}, u32[]{:S(2)}) %collective-permute-start.44) | collective-permute-done | bytes 196640 | tf_op jit(solution)/shard_map/ppermute | solution.py:400
  (91 shorter events, 39.3 us)
Async XLA Ops:
  0.0 11.2 %all-to-all-start = ((bf16[1,8,32,1024]{3,2,0,1:T(8,128)(2,1)}), bf16[1,8,32,1024]{3,2,0,1:T(8,128)(2,1)S(1)}, u32[]{:S(2)}, u32[]{:S(2)}) async-start(bf16[1,8,32,1024]{3,2,0,1:T(8,128)(2,1)} %bitcast.18), calls=%async_computation | async-start | bytes 1048576 | tf_op jit(solution)/shard_map/all_to_all | solution.py:407
  22.4 8.6 %collective-permute-start.2 = (bf16[64,1024]{1,0:T(8,128)(2,1)S(1)}, bf16[64,1024]{1,0:T(8,128)(2,1)S(1)}, u32[]{:S(2)}, u32[]{:S(2)}) collective-permute-start(bf16[64,1024]{1,0:T(8,128)(2,1)S(1)} %get-tuple-element.57), channel_id=1, source_target_pairs={{0,24},{4,28},{8,16},{12,20},{16,8},{20,12},{24,0},{28,4},{1,25},{... | collective-permute-start | bytes 393224 | tf_op jit(solution)/shard_map/ppermute | solution.py:400
  33.1 25.2 %collective-permute-start.22 = (bf16[256,1024]{1,0:T(8,128)(2,1)S(1)}, bf16[256,1024]{1,0:T(8,128)(2,1)S(1)}, u32[]{:S(2)}, u32[]{:S(2)}) collective-permute-start(bf16[256,1024]{1,0:T(8,128)(2,1)S(1)} %get-tuple-element.59.refs_0_), channel_id=1, source_target_pairs={{0,2},{1,3},{2,0},{3,1},{4,6},{5,7},{6,4},{7,5},{8,10},{9,11},{10,... | collective-permute-start | bytes 1572872 | tf_op jit(solution)/shard_map/ppermute | solution.py:400
  58.2 13.0 %collective-permute-start.33 = (bf16[256,1024]{1,0:T(8,128)(2,1)S(1)}, bf16[256,1024]{1,0:T(8,128)(2,1)S(1)}, u32[]{:S(2)}, u32[]{:S(2)}) collective-permute-start(bf16[256,1024]{1,0:T(8,128)(2,1)S(1)} %collective-permute-done.22.refs_0_), channel_id=1, source_target_pairs={{0,1},{1,0},{2,3},{3,2},{4,5},{5,4},{6,7},{7,6},{8,9},{9,8},{10,11... | collective-permute-start | bytes 1572872 | tf_op jit(solution)/shard_map/ppermute | solution.py:400
  71.2 20.4 %collective-permute-start.34 = (bf16[256,1024]{1,0:T(8,128)(2,1)S(1)}, bf16[256,1024]{1,0:T(8,128)(2,1)S(1)}, u32[]{:S(2)}, u32[]{:S(2)}) collective-permute-start(bf16[256,1024]{1,0:T(8,128)(2,1)S(1)} %collective-permute-done.33.refs_0_), channel_id=1, source_target_pairs={{0,4},{4,0},{8,12},{12,8},{16,20},{20,16},{24,28},{28,24},{1,5},{5... | collective-permute-start | bytes 1572872 | tf_op jit(solution)/shard_map/ppermute | solution.py:400
  75.0 13.7 %collective-permute-start.9 = (bf16[128,1024]{1,0:T(8,128)(2,1)S(1)}, bf16[128,1024]{1,0:T(8,128)(2,1)S(1)}, u32[]{:S(2)}, u32[]{:S(2)}) collective-permute-start(bf16[128,1024]{1,0:T(8,128)(2,1)S(1)} %get-tuple-element.63), channel_id=1, source_target_pairs={{0,16},{4,20},{8,24},{12,28},{16,0},{20,4},{24,8},{28,12},{1,17},{... | collective-permute-start | bytes 786440 | tf_op jit(solution)/shard_map/ppermute | solution.py:400
  75.1 15.0 %collective-permute-start.10 = (bf16[128,1024]{1,0:T(8,128)(2,1)S(1)}, bf16[128,1024]{1,0:T(8,128)(2,1)S(1)}, u32[]{:S(2)}, u32[]{:S(2)}) collective-permute-start(bf16[128,1024]{1,0:T(8,128)(2,1)S(1)} %get-tuple-element.64), channel_id=1, source_target_pairs={{0,24},{4,28},{8,16},{12,20},{16,8},{20,12},{24,0},{28,4},{1,25},{... | collective-permute-start | bytes 786440 | tf_op jit(solution)/shard_map/ppermute | solution.py:400
  76.8 13.4 %collective-permute-start.8 = (bf16[128,1024]{1,0:T(8,128)(2,1)S(1)}, bf16[128,1024]{1,0:T(8,128)(2,1)S(1)}, u32[]{:S(2)}, u32[]{:S(2)}) collective-permute-start(bf16[128,1024]{1,0:T(8,128)(2,1)S(1)} %get-tuple-element.62), channel_id=1, source_target_pairs={{0,8},{4,12},{8,0},{12,4},{16,24},{20,28},{24,16},{28,20},{1,9},{5... | collective-permute-start | bytes 786440 | tf_op jit(solution)/shard_map/ppermute | solution.py:400
  88.7 10.8 %collective-permute-start.15 = (bf16[128,1024]{1,0:T(8,128)(2,1)S(1)}, bf16[128,1024]{1,0:T(8,128)(2,1)S(1)}, u32[]{:S(2)}, u32[]{:S(2)}) collective-permute-start(bf16[128,1024]{1,0:T(8,128)(2,1)S(1)} %collective-permute-done.9.refs_2_), channel_id=1, source_target_pairs={{0,1},{1,0},{2,3},{3,2},{4,5},{5,4},{6,7},{7,6},{8,9},{9,8},{10,11... | collective-permute-start | bytes 786440 | tf_op jit(solution)/shard_map/ppermute | solution.py:400
  90.1 15.0 %collective-permute-start.16 = (bf16[128,1024]{1,0:T(8,128)(2,1)S(1)}, bf16[128,1024]{1,0:T(8,128)(2,1)S(1)}, u32[]{:S(2)}, u32[]{:S(2)}) collective-permute-start(bf16[128,1024]{1,0:T(8,128)(2,1)S(1)} %collective-permute-done.10.refs_3_), channel_id=1, source_target_pairs={{0,1},{1,0},{2,3},{3,2},{4,5},{5,4},{6,7},{7,6},{8,9},{9,8},{10,11... | collective-permute-start | bytes 786440 | tf_op jit(solution)/shard_map/ppermute | solution.py:400
  90.2 20.5 %collective-permute-start.12 = (bf16[128,1024]{1,0:T(8,128)(2,1)S(1)}, bf16[128,1024]{1,0:T(8,128)(2,1)S(1)}, u32[]{:S(2)}, u32[]{:S(2)}) collective-permute-start(bf16[128,1024]{1,0:T(8,128)(2,1)S(1)} %collective-permute-done.8.refs_1_), channel_id=1, source_target_pairs={{0,1},{1,0},{2,3},{3,2},{4,5},{5,4},{6,7},{7,6},{8,9},{9,8},{10,11... | collective-permute-start | bytes 786440 | tf_op jit(solution)/shard_map/ppermute | solution.py:400
  91.6 22.5 %collective-permute-start.23 = (bf16[256,1024]{1,0:T(8,128)(2,1)S(1)}, bf16[256,1024]{1,0:T(8,128)(2,1)S(1)}, u32[]{:S(2)}, u32[]{:S(2)}) collective-permute-start(bf16[256,1024]{1,0:T(8,128)(2,1)S(1)} %collective-permute-done.22.refs_0_), channel_id=1, source_target_pairs={{0,4},{4,0},{8,12},{12,8},{16,20},{20,16},{24,28},{28,24},{1,5},{5... | collective-permute-start | bytes 1572872 | tf_op jit(solution)/shard_map/ppermute | solution.py:400
  96.3 20.0 %collective-permute-start.35 = (bf16[128,1024]{1,0:T(8,128)(2,1)S(1)}, bf16[128,1024]{1,0:T(8,128)(2,1)S(1)}, u32[]{:S(2)}, u32[]{:S(2)}) collective-permute-start(bf16[128,1024]{1,0:T(8,128)(2,1)S(1)} %get-tuple-element.88), channel_id=1, source_target_pairs={{0,8},{4,12},{8,0},{12,4},{16,24},{20,28},{24,16},{28,20},{1,9},{5... | collective-permute-start | bytes 786440 | tf_op jit(solution)/shard_map/ppermute | solution.py:400
  99.5 17.4 %collective-permute-start.36 = (bf16[128,1024]{1,0:T(8,128)(2,1)S(1)}, bf16[128,1024]{1,0:T(8,128)(2,1)S(1)}, u32[]{:S(2)}, u32[]{:S(2)}) collective-permute-start(bf16[128,1024]{1,0:T(8,128)(2,1)S(1)} %get-tuple-element.89), channel_id=1, source_target_pairs={{0,16},{4,20},{8,24},{12,28},{16,0},{20,4},{24,8},{28,12},{1,17},{... | collective-permute-start | bytes 786440 | tf_op jit(solution)/shard_map/ppermute | solution.py:400
  105.1 12.1 %collective-permute-start.37 = (bf16[128,1024]{1,0:T(8,128)(2,1)S(1)}, bf16[128,1024]{1,0:T(8,128)(2,1)S(1)}, u32[]{:S(2)}, u32[]{:S(2)}) collective-permute-start(bf16[128,1024]{1,0:T(8,128)(2,1)S(1)} %get-tuple-element.90), channel_id=1, source_target_pairs={{0,24},{4,28},{8,16},{12,20},{16,8},{20,12},{24,0},{28,4},{1,25},{... | collective-permute-start | bytes 786440 | tf_op jit(solution)/shard_map/ppermute | solution.py:400
  110.7 29.0 %collective-permute-start.17 = (bf16[256,1024]{1,0:T(8,128)(2,1)S(1)}, bf16[256,1024]{1,0:T(8,128)(2,1)S(1)}, u32[]{:S(2)}, u32[]{:S(2)}) collective-permute-start(bf16[256,1024]{1,0:T(8,128)(2,1)S(1)} %experts.7), channel_id=1, source_target_pairs={{0,1},{1,0},{2,3},{3,2},{4,5},{5,4},{6,7},{7,6},{8,9},{9,8},{10,11... | collective-permute-start | bytes 1572872 | tf_op jit(solution)/shard_map/ppermute | solution.py:400
  114.1 40.8 %collective-permute-start.13 = (bf16[256,1024]{1,0:T(8,128)(2,1)S(1)}, bf16[256,1024]{1,0:T(8,128)(2,1)S(1)}, u32[]{:S(2)}, u32[]{:S(2)}) collective-permute-start(bf16[256,1024]{1,0:T(8,128)(2,1)S(1)} %experts.6), channel_id=1, source_target_pairs={{0,1},{1,0},{2,3},{3,2},{4,5},{5,4},{6,7},{7,6},{8,9},{9,8},{10,11... | collective-permute-start | bytes 1572872 | tf_op jit(solution)/shard_map/ppermute | solution.py:400
  124.1 8.4 %collective-permute-start.38 = (bf16[128,1024]{1,0:T(8,128)(2,1)S(1)}, bf16[128,1024]{1,0:T(8,128)(2,1)S(1)}, u32[]{:S(2)}, u32[]{:S(2)}) collective-permute-start(bf16[128,1024]{1,0:T(8,128)(2,1)S(1)} %get-tuple-element.92), channel_id=1, source_target_pairs={{0,8},{4,12},{8,0},{12,4},{16,24},{20,28},{24,16},{28,20},{1,9},{5... | collective-permute-start | bytes 786440 | tf_op jit(solution)/shard_map/ppermute | solution.py:400
  125.2 9.6 %collective-permute-start.39 = (bf16[128,1024]{1,0:T(8,128)(2,1)S(1)}, bf16[128,1024]{1,0:T(8,128)(2,1)S(1)}, u32[]{:S(2)}, u32[]{:S(2)}) collective-permute-start(bf16[128,1024]{1,0:T(8,128)(2,1)S(1)} %get-tuple-element.93), channel_id=1, source_target_pairs={{0,16},{4,20},{8,24},{12,28},{16,0},{20,4},{24,8},{28,12},{1,17},{... | collective-permute-start | bytes 786440 | tf_op jit(solution)/shard_map/ppermute | solution.py:400
  125.2 12.4 %collective-permute-start.40 = (bf16[128,1024]{1,0:T(8,128)(2,1)S(1)}, bf16[128,1024]{1,0:T(8,128)(2,1)S(1)}, u32[]{:S(2)}, u32[]{:S(2)}) collective-permute-start(bf16[128,1024]{1,0:T(8,128)(2,1)S(1)} %get-tuple-element.94), channel_id=1, source_target_pairs={{0,24},{4,28},{8,16},{12,20},{16,8},{20,12},{24,0},{28,4},{1,25},{... | collective-permute-start | bytes 786440 | tf_op jit(solution)/shard_map/ppermute | solution.py:400
  132.4 23.5 %collective-permute-start.27 = (bf16[128,1024]{1,0:T(8,128)(2,1)S(1)}, bf16[128,1024]{1,0:T(8,128)(2,1)S(1)}, u32[]{:S(2)}, u32[]{:S(2)}) collective-permute-start(bf16[128,1024]{1,0:T(8,128)(2,1)S(1)} %get-tuple-element.80), channel_id=1, source_target_pairs={{0,8},{4,12},{8,0},{12,4},{16,24},{20,28},{24,16},{28,20},{1,9},{5... | collective-permute-start | bytes 786440 | tf_op jit(solution)/shard_map/ppermute | solution.py:400
  134.8 23.1 %collective-permute-start.28 = (bf16[128,1024]{1,0:T(8,128)(2,1)S(1)}, bf16[128,1024]{1,0:T(8,128)(2,1)S(1)}, u32[]{:S(2)}, u32[]{:S(2)}) collective-permute-start(bf16[128,1024]{1,0:T(8,128)(2,1)S(1)} %get-tuple-element.81), channel_id=1, source_target_pairs={{0,16},{4,20},{8,24},{12,28},{16,0},{20,4},{24,8},{28,12},{1,17},{... | collective-permute-start | bytes 786440 | tf_op jit(solution)/shard_map/ppermute | solution.py:400
  137.6 20.6 %collective-permute-start.29 = (bf16[128,1024]{1,0:T(8,128)(2,1)S(1)}, bf16[128,1024]{1,0:T(8,128)(2,1)S(1)}, u32[]{:S(2)}, u32[]{:S(2)}) collective-permute-start(bf16[128,1024]{1,0:T(8,128)(2,1)S(1)} %get-tuple-element.82), channel_id=1, source_target_pairs={{0,24},{4,28},{8,16},{12,20},{16,8},{20,12},{24,0},{28,4},{1,25},{... | collective-permute-start | bytes 786440 | tf_op jit(solution)/shard_map/ppermute | solution.py:400
  139.8 31.9 %collective-permute-start.41 = (bf16[256,1024]{1,0:T(8,128)(2,1)S(1)}, bf16[256,1024]{1,0:T(8,128)(2,1)S(1)}, u32[]{:S(2)}, u32[]{:S(2)}) collective-permute-start(bf16[256,1024]{1,0:T(8,128)(2,1)S(1)} %get-tuple-element.98), channel_id=1, source_target_pairs={{0,4},{4,0},{8,12},{12,8},{16,20},{20,16},{24,28},{28,24},{1,5},{5... | collective-permute-start | bytes 1572872 | tf_op jit(solution)/shard_map/ppermute | solution.py:400
  155.0 13.5 %collective-permute-start.18 = (bf16[128,1024]{1,0:T(8,128)(2,1)S(1)}, bf16[128,1024]{1,0:T(8,128)(2,1)S(1)}, u32[]{:S(2)}, u32[]{:S(2)}) collective-permute-start(bf16[128,1024]{1,0:T(8,128)(2,1)S(1)} %get-tuple-element.69), channel_id=1, source_target_pairs={{0,16},{4,20},{8,24},{12,28},{16,0},{20,4},{24,8},{28,12},{1,17},{... | collective-permute-start | bytes 786440 | tf_op jit(solution)/shard_map/ppermute | solution.py:400
  156.0 12.5 %collective-permute-start.19 = (bf16[128,1024]{1,0:T(8,128)(2,1)S(1)}, bf16[128,1024]{1,0:T(8,128)(2,1)S(1)}, u32[]{:S(2)}, u32[]{:S(2)}) collective-permute-start(bf16[128,1024]{1,0:T(8,128)(2,1)S(1)} %get-tuple-element.70), channel_id=1, source_target_pairs={{0,24},{4,28},{8,16},{12,20},{16,8},{20,12},{24,0},{28,4},{1,25},{... | collective-permute-start | bytes 786440 | tf_op jit(solution)/shard_map/ppermute | solution.py:400
  157.9 12.3 %collective-permute-start.14 = (bf16[128,1024]{1,0:T(8,128)(2,1)S(1)}, bf16[128,1024]{1,0:T(8,128)(2,1)S(1)}, u32[]{:S(2)}, u32[]{:S(2)}) collective-permute-start(bf16[128,1024]{1,0:T(8,128)(2,1)S(1)} %get-tuple-element.68), channel_id=1, source_target_pairs={{0,8},{4,12},{8,0},{12,4},{16,24},{20,28},{24,16},{28,20},{1,9},{5... | collective-permute-start | bytes 786440 | tf_op jit(solution)/shard_map/ppermute | solution.py:400
  158.7 13.2 %collective-permute-start.30 = (bf16[256,1024]{1,0:T(8,128)(2,1)S(1)}, bf16[256,1024]{1,0:T(8,128)(2,1)S(1)}, u32[]{:S(2)}, u32[]{:S(2)}) collective-permute-start(bf16[256,1024]{1,0:T(8,128)(2,1)S(1)} %get-tuple-element.86), channel_id=1, source_target_pairs={{0,4},{4,0},{8,12},{12,8},{16,20},{20,16},{24,28},{28,24},{1,5},{5... | collective-permute-start | bytes 1572872 | tf_op jit(solution)/shard_map/ppermute | solution.py:400
  170.7 12.9 %collective-permute-start.20 = (bf16[256,1024]{1,0:T(8,128)(2,1)S(1)}, bf16[256,1024]{1,0:T(8,128)(2,1)S(1)}, u32[]{:S(2)}, u32[]{:S(2)}) collective-permute-start(bf16[256,1024]{1,0:T(8,128)(2,1)S(1)} %get-tuple-element.74), channel_id=1, source_target_pairs={{0,4},{4,0},{8,12},{12,8},{16,20},{20,16},{24,28},{28,24},{1,5},{5... | collective-permute-start | bytes 1572872 | tf_op jit(solution)/shard_map/ppermute | solution.py:400
  172.1 28.9 %collective-permute-start.31 = (bf16[160,1024]{1,0:T(8,128)(2,1)S(1)}, bf16[160,1024]{1,0:T(8,128)(2,1)S(1)}, u32[]{:S(2)}, u32[]{:S(2)}) collective-permute-start(bf16[160,1024]{1,0:T(8,128)(2,1)S(1)} %slice.47), channel_id=1, source_target_pairs={{0,2},{1,3},{2,0},{3,1},{4,6},{5,7},{6,4},{7,5},{8,10},{9,11},{10,... | collective-permute-start | bytes 983048 | tf_op jit(solution)/shard_map/ppermute | solution.py:400
  175.7 33.3 %collective-permute-start.42 = (bf16[160,1024]{1,0:T(8,128)(2,1)S(1)}, bf16[160,1024]{1,0:T(8,128)(2,1)S(1)}, u32[]{:S(2)}, u32[]{:S(2)}) collective-permute-start(bf16[160,1024]{1,0:T(8,128)(2,1)S(1)} %slice.40), channel_id=1, source_target_pairs={{0,3},{1,2},{2,1},{3,0},{4,7},{5,6},{6,5},{7,4},{8,11},{9,10},{10,... | collective-permute-start | bytes 983048 | tf_op jit(solution)/shard_map/ppermute | solution.py:400
  178.3 33.9 %collective-permute-start.44 = (bf16[96,1024]{1,0:T(8,128)(2,1)S(1)}, bf16[96,1024]{1,0:T(8,128)(2,1)S(1)}, u32[]{:S(2)}, u32[]{:S(2)}) collective-permute-start(bf16[96,1024]{1,0:T(8,128)(2,1)S(1)} %fusion), channel_id=1, source_target_pairs={{0,2},{1,3},{2,0},{3,1},{4,6},{5,7},{6,4},{7,5},{8,10},{9,11},{10,... | collective-permute-start | bytes 589832 | tf_op jit(solution)/shard_map/ppermute | solution.py:400
  (16 other events, 205.1 us)
